TPU v7x, 32 devices: a whole 2x2x4 slice. The times are simulated.
32 devices in a mesh: gx: 8 (over y, x, core), gy: 4 (over z).
Axes of the slice: x: 2, y: 2, z: 4, core: 2. Of those that a mesh axis runs over, the one named last changes fastest.
Arguments:
- adjoint_end: float32 [19, 2, 128, 512], P(None, None, 'gx', 'gy'), may hold values from -6 to 6
- forward_pop: bfloat16 [19, 2, 128, 512], P(None, None, 'gx', 'gy'), may hold values from 0 to 1, as said below
- porosity_level: int32 [2, 128, 512], P(None, 'gx', 'gy'), may hold values from 0 to 7
- fluid_mask: int32 [2, 128, 512], P(None, 'gx', 'gy'), may hold values 0 or 1
- design_index: int32 [128, 512], P('gx', 'gy'), may hold values from 0 to 4095, as said below
Outputs:
- adjoint_start: float32 [19, 2, 128, 512], P(None, None, 'gx', 'gy')
- design_grad: float32 [128, 32], P(('gx', 'gy'))
Inputs may be any that keep to these rules, and one draw needn't show every extreme that they name: `forward_pop`: every population is positive and a cell's populations sum to between 0.5 and 1.5. `design_index`: the design cell of column (x, y) is (cx, cy) stored as cy * 32 + cx, with cx within two of x // 4 and cy within two of y // 4.
All inputs are finite; a program needn't handle non-finite values. No bound on the sum of `fluid_mask` on one device may be relied on, other than what follows from the above.
Results may differ from a plain program's by a relative error of at most 0.0018.
Values sent between devices are 32-bit elements; how exact they have to be, the bound alone decides.
No kernel may reach another device: no remote copies, remote signals or barrier semaphores. Data moves between devices by JAX's collectives and lax.ppermute only.
A program may use at most 64 MiB of HBM per device.

v0:
```python
import jax
import jax.numpy as jnp
import numpy as np
from jax import lax
from jax.sharding import PartitionSpec as P

STEPS = 3
LEVELS = 8


relax_rate = 1.25
porous_max = 0.5


def padded_2(cells, sides, width):
    for axis, dim in sides:
        count = lax.axis_size(axis)
        ends = count - 1
        head = lax.slice_in_dim(cells, 0, width, axis=dim)
        tail = lax.slice_in_dim(cells, cells.shape[dim] - width, cells.shape[dim], axis=dim)
        cells = jnp.concatenate(
            [
                lax.ppermute(tail, axis, [(i, (i + 1) % count) for i in range(ends)]),
                cells,
                lax.ppermute(head, axis, [((i + 1) % count, i) for i in range(ends)]),
            ],
            axis=dim,
        )
    return cells


def lattice_table():
    speeds = [[0, 0, 0]]
    for axis_index in range(3):
        for sign_value in (1, -1):
            vector_row = [0, 0, 0]
            vector_row[axis_index] = sign_value
            speeds.append(vector_row)
    for plane_pair in ((0, 1), (0, 2), (1, 2)):
        for first_sign in (1, -1):
            for second_sign in (1, -1):
                vector_row = [0, 0, 0]
                vector_row[plane_pair[0]] = first_sign
                vector_row[plane_pair[1]] = second_sign
                speeds.append(vector_row)
    weights = [1.0 / 3.0] + [1.0 / 18.0] * 6 + [1.0 / 36.0] * 12
    opposite = [speeds.index([-component for component in speed_row]) for speed_row in speeds]
    return (speeds, weights, opposite)


def speed_columns(speeds):
    return [
        jnp.asarray(np.array([speed_row[k] for speed_row in speeds], dtype=np.float32))[
            :, None, None, None
        ]
        for k in range(3)
    ]


def cell_terms(forward_pop, porosity_level, fluid_mask):
    speeds, weights, opposite = lattice_table()
    speed_axis = speed_columns(speeds)
    weight_col = jnp.asarray(np.array(weights, dtype=np.float32))[:, None, None, None]
    popul = forward_pop.astype(jnp.float32)
    density = jnp.sum(popul, axis=0)
    velocity = [jnp.sum(popul * speed_axis[k], axis=0) / density for k in range(3)]
    speed_sq = velocity[0] * velocity[0] + velocity[1] * velocity[1] + velocity[2] * velocity[2]
    projected = (
        speed_axis[0] * velocity[0] + speed_axis[1] * velocity[1] + speed_axis[2] * velocity[2]
    )
    equilib = (
        weight_col
        * density
        * (1.0 + 3.0 * projected + 4.5 * projected * projected - 1.5 * speed_sq)
    )
    relaxed = popul - relax_rate * (popul - equilib)
    response = jnp.stack([popul[opposite[q]] for q in range(19)]) - relaxed
    fluid_frac = fluid_mask.astype(jnp.float32)
    porosity = jnp.where(
        fluid_mask == 1,
        porous_max * porosity_level.astype(jnp.float32) / (LEVELS - 1),
        jnp.float32(1.0),
    )
    return (velocity, porosity, response, fluid_frac)


def pull_list(padded):
    speeds, weights, opposite = lattice_table()
    size_x = padded.shape[2]
    size_y = padded.shape[3]
    pieces = []
    for q in range(19):
        shift_x, shift_y, shift_z = speeds[q]
        sliced = padded[
            q, :, 1 + shift_x : size_x - 1 + shift_x, 1 + shift_y : size_y - 1 + shift_y
        ]
        pieces.append(jnp.roll(sliced, -shift_z, axis=0))
    return pieces


def weighted_total(pieces, coeffs):
    total = None
    for q in range(19):
        if coeffs[q] != 0.0:
            term = pieces[q] * coeffs[q]
            total = term if total is None else total + term
    return total


def collide_list(pulled, velocity, porosity):
    speeds, weights, opposite = lattice_table()
    speed_sq = velocity[0] * velocity[0] + velocity[1] * velocity[1] + velocity[2] * velocity[2]
    a_zero = weighted_total(pulled, weights)
    a_one = [
        weighted_total(pulled, [weights[q] * speeds[q][k] for q in range(19)]) for k in range(3)
    ]
    second = {}
    for k in range(3):
        for l in range(k, 3):
            second[k, l] = weighted_total(
                pulled, [weights[q] * speeds[q][k] * speeds[q][l] for q in range(19)]
            )
            second[l, k] = second[k, l]
    b_vec = []
    for k in range(3):
        b_vec.append(
            velocity[0] * second[k, 0] + velocity[1] * second[k, 1] + velocity[2] * second[k, 2]
        )
    b_sq = velocity[0] * b_vec[0] + velocity[1] * b_vec[1] + velocity[2] * b_vec[2]
    base = a_zero * (1.0 + 1.5 * speed_sq) - 4.5 * b_sq
    vector_part = [3.0 * a_one[k] + 9.0 * b_vec[k] - 3.0 * velocity[k] * a_zero for k in range(3)]
    keep = 1.0 - porosity
    results = []
    for j in range(19):
        kernel = base
        for k in range(3):
            if speeds[j][k] != 0:
                kernel = kernel + float(speeds[j][k]) * vector_part[k]
        results.append(
            keep * ((1.0 - relax_rate) * pulled[j] + relax_rate * kernel)
            + porosity * pulled[opposite[j]]
        )
    return results


def sensitivity_term(pieces, response):
    total = pieces[0] * response[0]
    for q in range(1, 19):
        total = total + pieces[q] * response[q]
    return total


def per_device(adjoint_end, forward_pop, porosity_level, fluid_mask, design_index):
    velocity, porosity, response, fluid_frac = cell_terms(forward_pop, porosity_level, fluid_mask)
    tile_x = adjoint_end.shape[2]
    tile_y = adjoint_end.shape[3]
    adjoint = adjoint_end
    sensitivity = jnp.zeros(porosity.shape, jnp.float32)
    for step_num in range(STEPS):
        padded = padded_2(adjoint, (("gx", 2), ("gy", 3)), 1)
        pulled = pull_list(padded)
        sensitivity = sensitivity + sensitivity_term(pulled, response)
        adjoint = jnp.stack(collide_list(pulled, velocity, porosity))
    column_sum = jnp.sum(sensitivity * fluid_frac, axis=0) * (porous_max / (LEVELS - 1))
    gx_count = lax.axis_size("gx")
    gy_count = lax.axis_size("gy")
    design_cols = tile_x * gx_count // 4
    design_rows = tile_y * gy_count // 4
    partial_grid = jax.ops.segment_sum(
        column_sum.reshape(-1), design_index.reshape(-1), num_segments=design_rows * design_cols
    )
    partial_grid = partial_grid.reshape(design_rows, design_cols)
    owned = lax.psum_scatter(partial_grid, ("gx", "gy"), scatter_dimension=0, tiled=True)
    return (adjoint, owned)


def solution(mesh):
    in_specs = (
        P(None, None, "gx", "gy"),
        P(None, None, "gx", "gy"),
        P(None, "gx", "gy"),
        P(None, "gx", "gy"),
        P("gx", "gy"),
    )
    out_specs = (P(None, None, "gx", "gy"), P(("gx", "gy"), None))
    return jax.shard_map(
        per_device, mesh=mesh, in_specs=in_specs, out_specs=out_specs, check_vma=False
    )
```

profile of v0, /device:TPU:0, one launch (start us, length us, event | category | flops | bytes accessed | tf_op | source)
XLA Modules:
  0.0 135.9 jit_solution(2574298998433560441)
XLA Ops:
  0.6 1.0 fusion.74
  1.7 2.4 %collective-permute-start.1 = (f32[19,2,1,128]{3,2,1,0:T(1,128)S(1)}, f32[19,2,1,128]{3,2,1,0:T(1,128)S(1)}, u32[]{:S(2)}, u32[]{:S(2)}) collective-permute-start(f32[19,2,1,128]{3,2,1,0:T(1,128)S(1)} %get-tuple-element.149), channel_id=1, source_target_pairs={{0,4},{4,8},{8,12},{12,16},{16,20},{20,24},{24,28},{1,5},{5,9},{9,... | collective-permute-start | bytes 58376 | tf_op jit(solution)/shard_map/ppermute | solution.py:23
  4.0 1.3 collective-permute-start
  5.3 0.9 convert_element_type.10
  6.5 0.8 copy-done.1
  7.5 0.6 copy-done.8
  8.1 0.3 fusion.4
  8.4 0.7 copy-done
  9.3 0.2 fusion.71
  9.5 1.3 collective-permute-start.2
  10.8 4.9 %collective-permute-start.3 = (f32[19,2,18,1]{3,2,1,0:T(8,128)S(1)}, f32[19,2,18,1]{3,2,1,0:T(8,128)S(1)}, u32[]{:S(2)}, u32[]{:S(2)}) collective-permute-start(f32[19,2,18,1]{3,2,1,0:T(8,128)S(1)} %get-tuple-element.112), channel_id=1, source_target_pairs={{0,1},{1,2},{2,3},{4,5},{5,6},{6,7},{8,9},{9,10},{10,11},{12,13},{... | collective-permute-start | bytes 8216 | tf_op jit(solution)/shard_map/ppermute | solution.py:23
  15.8 7.5 %collective-permute-done.2 = f32[19,2,18,1]{3,2,1,0:T(8,128)S(1)} collective-permute-done((f32[19,2,18,1]{3,2,1,0:T(8,128)S(1)}, f32[19,2,18,1]{3,2,1,0:T(8,128)S(1)}, u32[]{:S(2)}, u32[]{:S(2)}) %collective-permute-start.2) | collective-permute-done | bytes 2768 | tf_op jit(solution)/shard_map/ppermute | solution.py:25
  23.4 1.6 %collective-permute-done.3 = f32[19,2,18,1]{3,2,1,0:T(8,128)S(1)} collective-permute-done((f32[19,2,18,1]{3,2,1,0:T(8,128)S(1)}, f32[19,2,18,1]{3,2,1,0:T(8,128)S(1)}, u32[]{:S(2)}, u32[]{:S(2)}) %collective-permute-start.3) | collective-permute-done | bytes 2768 | tf_op jit(solution)/shard_map/ppermute | solution.py:23
  25.2 0.7 copy-done.2
  26.6 3.7 %collective-permute-start.5 = (f32[19,2,1,128]{3,2,1,0:T(1,128)S(1)}, f32[19,2,1,128]{3,2,1,0:T(1,128)S(1)}, u32[]{:S(2)}, u32[]{:S(2)}) collective-permute-start(f32[19,2,1,128]{3,2,1,0:T(1,128)S(1)} %get-tuple-element.143), channel_id=1, source_target_pairs={{0,4},{4,8},{8,12},{12,16},{16,20},{20,24},{24,28},{1,5},{5,9},{9,... | collective-permute-start | bytes 58376 | tf_op jit(solution)/shard_map/ppermute | solution.py:23
  30.3 1.3 collective-permute-start.4
  31.6 4.6 %collective-permute-done.4 = f32[19,2,1,128]{3,2,1,0:T(1,128)S(1)} collective-permute-done((f32[19,2,1,128]{3,2,1,0:T(1,128)S(1)}, f32[19,2,1,128]{3,2,1,0:T(1,128)S(1)}, u32[]{:S(2)}, u32[]{:S(2)}) %collective-permute-start.4) | collective-permute-done | bytes 19488 | tf_op jit(solution)/shard_map/ppermute | solution.py:25
  36.5 1.3 collective-permute-start.6
  37.7 5.0 %collective-permute-start.7 = (f32[19,2,18,1]{3,2,1,0:T(8,128)S(1)}, f32[19,2,18,1]{3,2,1,0:T(8,128)S(1)}, u32[]{:S(2)}, u32[]{:S(2)}) collective-permute-start(f32[19,2,18,1]{3,2,1,0:T(8,128)S(1)} %get-tuple-element.106), channel_id=1, source_target_pairs={{0,1},{1,2},{2,3},{4,5},{5,6},{6,7},{8,9},{9,10},{10,11},{12,13},{... | collective-permute-start | bytes 8216 | tf_op jit(solution)/shard_map/ppermute | solution.py:23
  42.8 7.7 %collective-permute-done.6 = f32[19,2,18,1]{3,2,1,0:T(8,128)S(1)} collective-permute-done((f32[19,2,18,1]{3,2,1,0:T(8,128)S(1)}, f32[19,2,18,1]{3,2,1,0:T(8,128)S(1)}, u32[]{:S(2)}, u32[]{:S(2)}) %collective-permute-start.6) | collective-permute-done | bytes 2768 | tf_op jit(solution)/shard_map/ppermute | solution.py:25
  50.6 1.6 %collective-permute-done.7 = f32[19,2,18,1]{3,2,1,0:T(8,128)S(1)} collective-permute-done((f32[19,2,18,1]{3,2,1,0:T(8,128)S(1)}, f32[19,2,18,1]{3,2,1,0:T(8,128)S(1)}, u32[]{:S(2)}, u32[]{:S(2)}) %collective-permute-start.7) | collective-permute-done | bytes 2768 | tf_op jit(solution)/shard_map/ppermute | solution.py:23
  53.0 3.6 %collective-permute-start.9 = (f32[19,2,1,128]{3,2,1,0:T(1,128)S(1)}, f32[19,2,1,128]{3,2,1,0:T(1,128)S(1)}, u32[]{:S(2)}, u32[]{:S(2)}) collective-permute-start(f32[19,2,1,128]{3,2,1,0:T(1,128)S(1)} %get-tuple-element.137), channel_id=1, source_target_pairs={{0,4},{4,8},{8,12},{12,16},{16,20},{20,24},{24,28},{1,5},{5,9},{9,... | collective-permute-start | bytes 58376 | tf_op jit(solution)/shard_map/ppermute | solution.py:23
  56.7 1.3 collective-permute-start.8
  58.0 2.4 %collective-permute-done.8 = f32[19,2,1,128]{3,2,1,0:T(1,128)S(1)} collective-permute-done((f32[19,2,1,128]{3,2,1,0:T(1,128)S(1)}, f32[19,2,1,128]{3,2,1,0:T(1,128)S(1)}, u32[]{:S(2)}, u32[]{:S(2)}) %collective-permute-start.8) | collective-permute-done | bytes 19488 | tf_op jit(solution)/shard_map/ppermute | solution.py:25
  60.4 0.2 fusion.69
  60.6 1.3 collective-permute-start.10
  61.9 5.0 %collective-permute-start.11 = (f32[19,2,18,1]{3,2,1,0:T(8,128)S(1)}, f32[19,2,18,1]{3,2,1,0:T(8,128)S(1)}, u32[]{:S(2)}, u32[]{:S(2)}) collective-permute-start(f32[19,2,18,1]{3,2,1,0:T(8,128)S(1)} %get-tuple-element.104), channel_id=1, source_target_pairs={{0,1},{1,2},{2,3},{4,5},{5,6},{6,7},{8,9},{9,10},{10,11},{12,13},{... | collective-permute-start | bytes 8216 | tf_op jit(solution)/shard_map/ppermute | solution.py:23
  67.0 7.7 %collective-permute-done.10 = f32[19,2,18,1]{3,2,1,0:T(8,128)S(1)} collective-permute-done((f32[19,2,18,1]{3,2,1,0:T(8,128)S(1)}, f32[19,2,18,1]{3,2,1,0:T(8,128)S(1)}, u32[]{:S(2)}, u32[]{:S(2)}) %collective-permute-start.10) | collective-permute-done | bytes 2768 | tf_op jit(solution)/shard_map/ppermute | solution.py:25
  74.7 1.6 %collective-permute-done.11 = f32[19,2,18,1]{3,2,1,0:T(8,128)S(1)} collective-permute-done((f32[19,2,18,1]{3,2,1,0:T(8,128)S(1)}, f32[19,2,18,1]{3,2,1,0:T(8,128)S(1)}, u32[]{:S(2)}, u32[]{:S(2)}) %collective-permute-start.11) | collective-permute-done | bytes 2768 | tf_op jit(solution)/shard_map/ppermute | solution.py:23
  76.7 14.7 %scatter_custom_fusion = f32[4096]{0:T(1024)S(1)} fusion(s32[2048]{0:T(1024)} %bitcast.516, f32[2048]{0:T(1024)S(1)} %multiply_bitcast_fusion, f32[]{:T(128)} %constant.27.clone.1), kind=kCustom, calls=%fused_computation.342 | custom fusion | flops 2048 | bytes 16896 | tf_op jit(solution)/shard_map/scatter-add | solution.py:169
  91.4 43.2 %all-reduce = f32[128,32]{1,0:T(8,128)S(1)} all-reduce(f32[128,32]{1,0:T(8,128)S(1)} %reshape.97), channel_id=2, replica_groups=mesh['gx'=8,'gy'=4] {'gx','gy'}, use_global_device_ids=true, to_apply=%region_6.7.clone | all-reduce | flops 4096 | bytes 32768
  135.2 0.6 constant_dynamic-slice_fusion
  (120 shorter events, 3.5 us)
Async XLA Ops:
  1.7 7.5 %collective-permute-start.1 = (f32[19,2,1,128]{3,2,1,0:T(1,128)S(1)}, f32[19,2,1,128]{3,2,1,0:T(1,128)S(1)}, u32[]{:S(2)}, u32[]{:S(2)}) collective-permute-start(f32[19,2,1,128]{3,2,1,0:T(1,128)S(1)} %get-tuple-element.149), channel_id=1, source_target_pairs={{0,4},{4,8},{8,12},{12,16},{16,20},{20,24},{24,28},{1,5},{5,9},{9,... | collective-permute-start | bytes 58376 | tf_op jit(solution)/shard_map/ppermute | solution.py:23
  4.0 5.2 %collective-permute-start = (f32[19,2,1,128]{3,2,1,0:T(1,128)S(1)}, f32[19,2,1,128]{3,2,1,0:T(1,128)S(1)}, u32[]{:S(2)}, u32[]{:S(2)}) collective-permute-start(f32[19,2,1,128]{3,2,1,0:T(1,128)S(1)} %get-tuple-element.150), channel_id=1, source_target_pairs={{4,0},{8,4},{12,8},{16,12},{20,16},{24,20},{28,24},{5,1},{9,5},{13... | collective-permute-start | bytes 58376 | tf_op jit(solution)/shard_map/ppermute | solution.py:25
  6.4 0.9 copy-start.1
  6.5 0.8 copy-start.4
  6.5 0.8 copy-start.5
  6.5 0.8 copy-start.6
  7.5 0.7 copy-start.8
  8.1 1.0 copy-start
  9.5 13.9 %collective-permute-start.2 = (f32[19,2,18,1]{3,2,1,0:T(8,128)S(1)}, f32[19,2,18,1]{3,2,1,0:T(8,128)S(1)}, u32[]{:S(2)}, u32[]{:S(2)}) collective-permute-start(f32[19,2,18,1]{3,2,1,0:T(8,128)S(1)} %get-tuple-element.111), channel_id=1, source_target_pairs={{1,0},{2,1},{3,2},{5,4},{6,5},{7,6},{9,8},{10,9},{11,10},{13,12},{... | collective-permute-start | bytes 8216 | tf_op jit(solution)/shard_map/ppermute | solution.py:25
  10.8 14.3 %collective-permute-start.3 = (f32[19,2,18,1]{3,2,1,0:T(8,128)S(1)}, f32[19,2,18,1]{3,2,1,0:T(8,128)S(1)}, u32[]{:S(2)}, u32[]{:S(2)}) collective-permute-start(f32[19,2,18,1]{3,2,1,0:T(8,128)S(1)} %get-tuple-element.112), channel_id=1, source_target_pairs={{0,1},{1,2},{2,3},{4,5},{5,6},{6,7},{8,9},{9,10},{10,11},{12,13},{... | collective-permute-start | bytes 8216 | tf_op jit(solution)/shard_map/ppermute | solution.py:23
  25.1 0.7 copy-start.2
  25.2 0.7 copy-start.3
  26.6 5.0 %collective-permute-start.5 = (f32[19,2,1,128]{3,2,1,0:T(1,128)S(1)}, f32[19,2,1,128]{3,2,1,0:T(1,128)S(1)}, u32[]{:S(2)}, u32[]{:S(2)}) collective-permute-start(f32[19,2,1,128]{3,2,1,0:T(1,128)S(1)} %get-tuple-element.143), channel_id=1, source_target_pairs={{0,4},{4,8},{8,12},{12,16},{16,20},{20,24},{24,28},{1,5},{5,9},{9,... | collective-permute-start | bytes 58376 | tf_op jit(solution)/shard_map/ppermute | solution.py:23
  30.3 5.9 %collective-permute-start.4 = (f32[19,2,1,128]{3,2,1,0:T(1,128)S(1)}, f32[19,2,1,128]{3,2,1,0:T(1,128)S(1)}, u32[]{:S(2)}, u32[]{:S(2)}) collective-permute-start(f32[19,2,1,128]{3,2,1,0:T(1,128)S(1)} %get-tuple-element.144), channel_id=1, source_target_pairs={{4,0},{8,4},{12,8},{16,12},{20,16},{24,20},{28,24},{5,1},{9,5},{13... | collective-permute-start | bytes 58376 | tf_op jit(solution)/shard_map/ppermute | solution.py:25
  36.5 14.0 %collective-permute-start.6 = (f32[19,2,18,1]{3,2,1,0:T(8,128)S(1)}, f32[19,2,18,1]{3,2,1,0:T(8,128)S(1)}, u32[]{:S(2)}, u32[]{:S(2)}) collective-permute-start(f32[19,2,18,1]{3,2,1,0:T(8,128)S(1)} %get-tuple-element.105), channel_id=1, source_target_pairs={{1,0},{2,1},{3,2},{5,4},{6,5},{7,6},{9,8},{10,9},{11,10},{13,12},{... | collective-permute-start | bytes 8216 | tf_op jit(solution)/shard_map/ppermute | solution.py:25
  37.7 14.5 %collective-permute-start.7 = (f32[19,2,18,1]{3,2,1,0:T(8,128)S(1)}, f32[19,2,18,1]{3,2,1,0:T(8,128)S(1)}, u32[]{:S(2)}, u32[]{:S(2)}) collective-permute-start(f32[19,2,18,1]{3,2,1,0:T(8,128)S(1)} %get-tuple-element.106), channel_id=1, source_target_pairs={{0,1},{1,2},{2,3},{4,5},{5,6},{6,7},{8,9},{9,10},{10,11},{12,13},{... | collective-permute-start | bytes 8216 | tf_op jit(solution)/shard_map/ppermute | solution.py:23
  53.0 5.0 %collective-permute-start.9 = (f32[19,2,1,128]{3,2,1,0:T(1,128)S(1)}, f32[19,2,1,128]{3,2,1,0:T(1,128)S(1)}, u32[]{:S(2)}, u32[]{:S(2)}) collective-permute-start(f32[19,2,1,128]{3,2,1,0:T(1,128)S(1)} %get-tuple-element.137), channel_id=1, source_target_pairs={{0,4},{4,8},{8,12},{12,16},{16,20},{20,24},{24,28},{1,5},{5,9},{9,... | collective-permute-start | bytes 58376 | tf_op jit(solution)/shard_map/ppermute | solution.py:23
  56.7 3.7 %collective-permute-start.8 = (f32[19,2,1,128]{3,2,1,0:T(1,128)S(1)}, f32[19,2,1,128]{3,2,1,0:T(1,128)S(1)}, u32[]{:S(2)}, u32[]{:S(2)}) collective-permute-start(f32[19,2,1,128]{3,2,1,0:T(1,128)S(1)} %get-tuple-element.138), channel_id=1, source_target_pairs={{4,0},{8,4},{12,8},{16,12},{20,16},{24,20},{28,24},{5,1},{9,5},{13... | collective-permute-start | bytes 58376 | tf_op jit(solution)/shard_map/ppermute | solution.py:25
  60.6 14.0 %collective-permute-start.10 = (f32[19,2,18,1]{3,2,1,0:T(8,128)S(1)}, f32[19,2,18,1]{3,2,1,0:T(8,128)S(1)}, u32[]{:S(2)}, u32[]{:S(2)}) collective-permute-start(f32[19,2,18,1]{3,2,1,0:T(8,128)S(1)} %get-tuple-element.103), channel_id=1, source_target_pairs={{1,0},{2,1},{3,2},{5,4},{6,5},{7,6},{9,8},{10,9},{11,10},{13,12},{... | collective-permute-start | bytes 8216 | tf_op jit(solution)/shard_map/ppermute | solution.py:25
  61.9 14.5 %collective-permute-start.11 = (f32[19,2,18,1]{3,2,1,0:T(8,128)S(1)}, f32[19,2,18,1]{3,2,1,0:T(8,128)S(1)}, u32[]{:S(2)}, u32[]{:S(2)}) collective-permute-start(f32[19,2,18,1]{3,2,1,0:T(8,128)S(1)} %get-tuple-element.104), channel_id=1, source_target_pairs={{0,1},{1,2},{2,3},{4,5},{5,6},{6,7},{8,9},{9,10},{10,11},{12,13},{... | collective-permute-start | bytes 8216 | tf_op jit(solution)/shard_map/ppermute | solution.py:23
  135.2 0.7 copy-start.7
where the time goes:
time: 137 us; the launch traced here: 136 us
  blocking collectives  43.2 us (32%)
  waiting for transfers between devices  34.8 us (25%)
  starting transfers between devices  32.4 us (24%)
  other arithmetic  18.6 us (14%)
  local copies, waits for them, and re-layouts  5.48 us (4%)
  between operations  1.47 us (1%)
    unnamed x1, blocking collectives  43.2 us
    ppermute x6, waiting for transfers between devices, padded_2(): lax.ppermute(head, axis, [((i + 1) % count, i) for i in range(ends)])  29.9 us
    ppermute x6, starting transfers between devices, padded_2(): lax.ppermute(tail, axis, [(i, (i + 1) % count) for i in range(ends)])  24.7 us
    scatter-add x1, other arithmetic, per_device(): jax.ops.segment_sum(column_sum.reshape(-1), design_index.reshape(-1), num...  14.7 us
    ppermute x6, starting transfers between devices, padded_2(): lax.ppermute(head, axis, [((i + 1) % count, i) for i in range(ends)])  7.75 us
    ppermute x6, waiting for transfers between devices, padded_2(): lax.ppermute(tail, axis, [(i, (i + 1) % count) for i in range(ends)])  4.95 us
    unnamed x38, local copies, waits for them, and re-layouts  3.65 us
  transfers between devices with their start and end apart: 12, of which 9 were waited for; matrix products, arithmetic and copies ran while one was open for 1% of the time, Pallas kernels for 0%

commit v1 on v0

v1 whole, which is shorter than its diff:
```python
import jax
import jax.numpy as jnp
import numpy as np
from jax import lax
from jax.sharding import PartitionSpec as P

STEPS = 3
LEVELS = 8
BOTH = ("gx", "gy")

relax_rate = 1.25
porous_max = 0.5


def lattice_table():
    speeds = [[0, 0, 0]]
    for axis_index in range(3):
        for sign_value in (1, -1):
            vector_row = [0, 0, 0]
            vector_row[axis_index] = sign_value
            speeds.append(vector_row)
    for plane_pair in ((0, 1), (0, 2), (1, 2)):
        for first_sign in (1, -1):
            for second_sign in (1, -1):
                vector_row = [0, 0, 0]
                vector_row[plane_pair[0]] = first_sign
                vector_row[plane_pair[1]] = second_sign
                speeds.append(vector_row)
    weights = [1.0 / 3.0] + [1.0 / 18.0] * 6 + [1.0 / 36.0] * 12
    opposite = [speeds.index([-component for component in speed_row]) for speed_row in speeds]
    return (speeds, weights, opposite)


def swap_pairs(count, parity):
    pairs = []
    for i in range(count):
        j = (i ^ 1) if parity == 0 else ((i - 1) ^ 1) + 1
        if 0 <= j < count:
            pairs.append((i, j))
    return pairs


def swap_halo(low_face, high_face, axis):
    count = lax.axis_size(axis)
    even = lax.axis_index(axis) % 2 == 0
    inner = jnp.where(even, high_face, low_face)
    outer = jnp.where(even, low_face, high_face)
    got_outer = lax.ppermute(outer, axis, swap_pairs(count, 1))
    got_inner = lax.ppermute(inner, axis, swap_pairs(count, 0))
    return (jnp.where(even, got_outer, got_inner), jnp.where(even, got_inner, got_outer))


def cell_terms(forward_pop, porosity_level, fluid_mask):
    speeds, weights, opposite = lattice_table()
    popul = [forward_pop[q].astype(jnp.float32) for q in range(19)]
    density = sum(popul[1:], popul[0])
    velocity = []
    for k in range(3):
        total = None
        for q in range(19):
            if speeds[q][k] != 0:
                term = popul[q] * float(speeds[q][k])
                total = term if total is None else total + term
        velocity.append(total / density)
    speed_sq = velocity[0] * velocity[0] + velocity[1] * velocity[1] + velocity[2] * velocity[2]
    response = []
    for q in range(19):
        projected = None
        for k in range(3):
            if speeds[q][k] != 0:
                term = velocity[k] * float(speeds[q][k])
                projected = term if projected is None else projected + term
        if projected is None:
            equilib = weights[q] * density * (1.0 - 1.5 * speed_sq)
        else:
            equilib = (
                weights[q]
                * density
                * (1.0 + 3.0 * projected + 4.5 * projected * projected - 1.5 * speed_sq)
            )
        relaxed = popul[q] - relax_rate * (popul[q] - equilib)
        response.append(popul[opposite[q]] - relaxed)
    fluid_frac = fluid_mask.astype(jnp.float32)
    porosity = jnp.where(
        fluid_mask == 1,
        porous_max * porosity_level.astype(jnp.float32) / (LEVELS - 1),
        jnp.float32(1.0),
    )
    return (velocity, porosity, response, fluid_frac)


def pull_list(padded):
    speeds, weights, opposite = lattice_table()
    size_x = padded[0].shape[1]
    size_y = padded[0].shape[2]
    pieces = []
    for q in range(19):
        shift_x, shift_y, shift_z = speeds[q]
        sliced = padded[q][:, 1 + shift_x : size_x - 1 + shift_x, 1 + shift_y : size_y - 1 + shift_y]
        pieces.append(sliced if shift_z == 0 else jnp.roll(sliced, -shift_z, axis=0))
    return pieces


def weighted_total(pieces, coeffs):
    total = None
    for q in range(19):
        if coeffs[q] != 0.0:
            term = pieces[q] * coeffs[q]
            total = term if total is None else total + term
    return total


def collide_list(pulled, velocity, keep, porosity):
    speeds, weights, opposite = lattice_table()
    speed_sq = velocity[0] * velocity[0] + velocity[1] * velocity[1] + velocity[2] * velocity[2]
    a_zero = weighted_total(pulled, weights)
    a_one = [
        weighted_total(pulled, [weights[q] * speeds[q][k] for q in range(19)]) for k in range(3)
    ]
    second = {}
    for k in range(3):
        for l in range(k, 3):
            second[k, l] = weighted_total(
                pulled, [weights[q] * speeds[q][k] * speeds[q][l] for q in range(19)]
            )
            second[l, k] = second[k, l]
    b_vec = []
    for k in range(3):
        b_vec.append(
            velocity[0] * second[k, 0] + velocity[1] * second[k, 1] + velocity[2] * second[k, 2]
        )
    b_sq = velocity[0] * b_vec[0] + velocity[1] * b_vec[1] + velocity[2] * b_vec[2]
    base = a_zero * (1.0 + 1.5 * speed_sq) - 4.5 * b_sq
    vector_part = [3.0 * a_one[k] + 9.0 * b_vec[k] - 3.0 * velocity[k] * a_zero for k in range(3)]
    results = []
    for j in range(19):
        kernel = base
        for k in range(3):
            if speeds[j][k] != 0:
                kernel = kernel + float(speeds[j][k]) * vector_part[k]
        results.append(
            keep * ((1.0 - relax_rate) * pulled[j] + relax_rate * kernel)
            + porosity * pulled[opposite[j]]
        )
    return results


def per_device(adjoint_end, forward_pop, porosity_level, fluid_mask, design_index):
    velocity, porosity, response, fluid_frac = cell_terms(forward_pop, porosity_level, fluid_mask)
    depth = adjoint_end.shape[1]
    tile_x = adjoint_end.shape[2]
    tile_y = adjoint_end.shape[3]
    fields = jnp.stack(velocity + [1.0 - porosity, porosity])

    def pack_x(first):
        adj_rows = adjoint_end[:, :, first : first + 3].reshape(-1, tile_y)
        near = 0 if first == 0 else tile_x - 2
        return jnp.concatenate([adj_rows, fields[:, :, near : near + 2].reshape(-1, tile_y)], axis=0)

    low, high = swap_halo(pack_x(0), pack_x(tile_x - 3), "gx")
    cut = 19 * depth * 3
    adj = jnp.concatenate(
        [
            low[:cut].reshape(19, depth, 3, tile_y),
            adjoint_end,
            high[:cut].reshape(19, depth, 3, tile_y),
        ],
        axis=2,
    )
    fields = jnp.concatenate(
        [low[cut:].reshape(5, depth, 2, tile_y), fields, high[cut:].reshape(5, depth, 2, tile_y)],
        axis=2,
    )
    wide = tile_x + 6

    def pack_y(first):
        cols = jnp.transpose(adj[:, :, :, first : first + 3], (3, 0, 1, 2)).reshape(-1, wide)
        near = 0 if first == 0 else tile_y - 2
        more = jnp.transpose(fields[:, :, :, near : near + 2], (3, 0, 1, 2)).reshape(-1, wide - 2)
        return jnp.concatenate([cols, jnp.pad(more, ((0, 0), (0, 2)))], axis=0)

    def unpack_y(got):
        cols = jnp.transpose(got[:cut].reshape(3, 19, depth, wide), (1, 2, 3, 0))
        more = jnp.transpose(got[cut:, : wide - 2].reshape(2, 5, depth, wide - 2), (1, 2, 3, 0))
        return (cols, more)

    low, high = swap_halo(pack_y(0), pack_y(tile_y - 3), "gy")
    low_adj, low_fields = unpack_y(low)
    high_adj, high_fields = unpack_y(high)
    adj = jnp.concatenate([low_adj, adj, high_adj], axis=3)
    fields = jnp.concatenate([low_fields, fields, high_fields], axis=3)

    padded = [adj[q] for q in range(19)]
    sensitivity = None
    for step_num in range(STEPS):
        edge = STEPS - 1 - step_num
        pulled = pull_list(padded)
        cut_out = slice(None) if edge == 0 else slice(edge, -edge)
        for q in range(19):
            term = pulled[q][:, cut_out, cut_out] * response[q]
            sensitivity = term if sensitivity is None else sensitivity + term
        trim = step_num
        inside = slice(trim, -trim) if trim else slice(None)
        here = [fields[k][:, inside, inside] for k in range(5)]
        padded = collide_list(pulled, here[:3], here[3], here[4])
    adjoint = jnp.stack(padded)
    column_sum = jnp.sum(sensitivity * fluid_frac, axis=0) * (porous_max / (LEVELS - 1))

    owners = lax.axis_size("gx") * lax.axis_size("gy")
    design_cols = tile_x * lax.axis_size("gx") // 4
    design_rows = tile_y * lax.axis_size("gy") // 4
    chunk = design_rows * design_cols // owners
    owner_hot = (design_index // chunk)[:, None, :] == jnp.arange(owners)[None, :, None]
    owner_val = jnp.where(owner_hot, column_sum[:, None, :], 0.0)
    slot_hot = ((design_index % chunk)[:, None, :] == jnp.arange(chunk)[None, :, None]).astype(
        jnp.float32
    )
    partial_grid = lax.dot_general(
        owner_val, slot_hot, (((0, 2), (0, 2)), ((), ())), precision=lax.Precision.HIGHEST
    )
    received = lax.all_to_all(
        partial_grid.reshape(owners, 1, chunk), BOTH, split_axis=0, concat_axis=0, tiled=True
    )
    owned = jnp.sum(received, axis=0).reshape(design_rows // owners, design_cols)
    return (adjoint, owned)


def solution(mesh):
    in_specs = (
        P(None, None, "gx", "gy"),
        P(None, None, "gx", "gy"),
        P(None, "gx", "gy"),
        P(None, "gx", "gy"),
        P("gx", "gy"),
    )
    out_specs = (P(None, None, "gx", "gy"), P(("gx", "gy"), None))
    return jax.shard_map(
        per_device, mesh=mesh, in_specs=in_specs, out_specs=out_specs, check_vma=False
    )
```

time: 137 us -> 41.7 us (0.30)
  blocking collectives: 43.2 us -> 0 us
  waiting for transfers between devices: 34.8 us -> 9.99 us
  starting transfers between devices: 32.4 us -> 16 us
  other arithmetic: 18.6 us -> 6.48 us
    unnamed x1 -> x0, blocking collectives: 43.2 us -> none
    ppermute x12 -> x4, waiting for transfers between devices: 34.8 us -> 2.91 us  [the longest x2 2.9 us: swap_halo(): got_inner = lax.ppermute(inner, axis, swap_pairs(count, 0))]
    ppermute x12 -> x4, starting transfers between devices: 32.4 us -> 10.2 us  [the longest x2 8.83 us: swap_halo(): got_inner = lax.ppermute(inner, axis, swap_pairs(count, 0))]
    scatter-add x1 -> x0, other arithmetic: 14.7 us -> none  [per_device(): jax.ops.segment_sum(column_sum.reshape(-1), design_index.reshape(-1), num...]
    all_to_all x0 -> x1, waiting for transfers between devices: none -> 7.08 us  [per_device(): lax.all_to_all(partial_grid.reshape(owners, 1, chunk), BOTH, split_axis=0...]
    all_to_all x0 -> x1, starting transfers between devices: none -> 5.89 us  [per_device(): lax.all_to_all(partial_grid.reshape(owners, 1, chunk), BOTH, split_axis=0...]
    unnamed x38 -> x14, local copies, waits for them, and re-layouts: 3.65 us -> 0.25 us
    transpose x0 -> x10, local copies, waits for them, and re-layouts: none -> 2.28 us  [the longest x3 0.89 us: pack_y(): jnp.transpose(adj[:, :, :, first:first + 3], (3, 0, 1, 2)).reshape(-1, wide)]
  transfers between devices with their start and end apart: 12 -> 5, of which waited for: 9 -> 3; matrix products, arithmetic and copies ran while one was open for 1% -> 0% of each run, Pallas kernels for 0% -> 0%
where the time goes in v1:
time: 41.7 us; the launch traced here: 41.5 us
  starting transfers between devices  16 us (38%)
  waiting for transfers between devices  9.99 us (24%)
  local copies, waits for them, and re-layouts  6.58 us (16%)
  other arithmetic  6.48 us (16%)
  matrix products  1.27 us (3%)
  between operations  1.14 us (3%)
    ppermute x2, starting transfers between devices, swap_halo(): got_inner = lax.ppermute(inner, axis, swap_pairs(count, 0))  8.83 us
    all_to_all x1, waiting for transfers between devices, per_device(): lax.all_to_all(partial_grid.reshape(owners, 1, chunk), BOTH, split_axis=0...  7.08 us
    all_to_all x1, starting transfers between devices, per_device(): lax.all_to_all(partial_grid.reshape(owners, 1, chunk), BOTH, split_axis=0...  5.89 us
    ppermute x2, waiting for transfers between devices, swap_halo(): got_inner = lax.ppermute(inner, axis, swap_pairs(count, 0))  2.9 us
    unnamed x22, other arithmetic  2.56 us
    add x15, other arithmetic, collide_list(): keep * ((1.0 - relax_rate) * pulled[j] + relax_rate * kernel)  2.17 us
    slice x25, local copies, waits for them, and re-layouts, pull_list(): jnp.roll(sliced, -shift_z, axis=0)  1.63 us
    ppermute x2, starting transfers between devices, swap_halo(): got_outer = lax.ppermute(outer, axis, swap_pairs(count, 1))  1.33 us
  transfers between devices with their start and end apart: 5, of which 3 were waited for; matrix products, arithmetic and copies ran while one was open for 0% of the time, Pallas kernels for 0%

profile of v1, /device:TPU:0, one launch (start us, length us, event | category | flops | bytes accessed | tf_op | source)
XLA Modules:
  0.0 41.5 jit_solution(17281107282971578299)
XLA Ops:
  0.7 0.9 %constant_dynamic-update-slice_fusion.4 = (f32[5,2,16,128]{3,2,1,0:T(8,128)S(1)}, f32[1,2,16,128]{3,2,1,0:T(8,128)S(1)}) fusion(bf16[19,2,16,128]{3,2,1,0:T(8,128)(2,1)} %param.6), kind=kLoop, calls=%fused_computation.84 | loop fusion | flops 212991 | bytes 188416
  2.0 0.7 %collective-permute-start = (f32[134,128]{1,0:T(8,128)S(1)}, f32[134,128]{1,0:T(8,128)S(1)}, u32[]{:S(2)}, u32[]{:S(2)}) collective-permute-start(f32[134,128]{1,0:T(8,128)S(1)} %get-tuple-element.99), channel_id=1, source_target_pairs={{4,8},{8,4},{12,16},{16,12},{20,24},{24,20},{5,9},{9,5},{13,17},{1... | collective-permute-start | bytes 205832 | tf_op jit(solution)/shard_map/ppermute | solution.py:48
  2.6 4.4 %collective-permute-start.1 = (f32[134,128]{1,0:T(8,128)S(1)}, f32[134,128]{1,0:T(8,128)S(1)}, u32[]{:S(2)}, u32[]{:S(2)}) collective-permute-start(f32[134,128]{1,0:T(8,128)S(1)} %get-tuple-element.100), channel_id=1, source_target_pairs={{0,4},{4,0},{8,12},{12,8},{16,20},{20,16},{24,28},{28,24},{1,5},{5... | collective-permute-start | bytes 205832 | tf_op jit(solution)/shard_map/ppermute | solution.py:49
  7.0 0.9 %collective-permute-done.1 = f32[134,128]{1,0:T(8,128)S(1)} collective-permute-done((f32[134,128]{1,0:T(8,128)S(1)}, f32[134,128]{1,0:T(8,128)S(1)}, u32[]{:S(2)}, u32[]{:S(2)}) %collective-permute-start.1) | collective-permute-done | bytes 68640 | tf_op jit(solution)/shard_map/ppermute | solution.py:49
  8.1 0.2 slice_bitcast_fusion
  8.3 0.3 copy.15
  8.8 0.4 copy.19
  9.4 0.1 copy.16
  9.7 0.1 copy.20
  10.0 0.7 %collective-permute-start.2 = (f32[134,22]{0,1:T(8,128)S(1)}, f32[134,22]{0,1:T(8,128)S(1)}, u32[]{:S(2)}, u32[]{:S(2)}) collective-permute-start(f32[134,22]{0,1:T(8,128)S(1)} %get-tuple-element.172), channel_id=1, source_target_pairs={{1,2},{2,1},{5,6},{6,5},{9,10},{10,9},{13,14},{14,13},{17,18},{18,... | collective-permute-start | bytes 35384 | tf_op jit(solution)/shard_map/ppermute | solution.py:48
  10.7 4.5 %collective-permute-start.3 = (f32[134,22]{0,1:T(8,128)S(1)}, f32[134,22]{0,1:T(8,128)S(1)}, u32[]{:S(2)}, u32[]{:S(2)}) collective-permute-start(f32[134,22]{0,1:T(8,128)S(1)} %get-tuple-element.173), channel_id=1, source_target_pairs={{0,1},{1,0},{2,3},{3,2},{4,5},{5,4},{6,7},{7,6},{8,9},{9,8},{10,11... | collective-permute-start | bytes 35384 | tf_op jit(solution)/shard_map/ppermute | solution.py:49
  15.2 2.0 %collective-permute-done.3 = f32[134,22]{0,1:T(8,128)S(1)} collective-permute-done((f32[134,22]{0,1:T(8,128)S(1)}, f32[134,22]{0,1:T(8,128)S(1)}, u32[]{:S(2)}, u32[]{:S(2)}) %collective-permute-start.3) | collective-permute-done | bytes 11824 | tf_op jit(solution)/shard_map/ppermute | solution.py:49
  17.4 0.1 copy.27
  17.5 0.4 copy.29
  17.9 0.1 copy.28
  18.0 0.4 copy.30
  18.4 0.6 %pad_maximum_fusion = f32[19,2,22,134]{3,2,1,0:T(8,128)S(1)} fusion(f32[19,2,22,3]{3,2,1,0:T(8,128)S(1)} %copy.30, f32[19,2,3,128]{3,2,1,0:T(4,128)S(1)} %reshape.108, f32[19,2,16,128]{3,2,1,0:T(8,128)S(1)} %copy-done, f32[19,2,3,128]{3,2,1,0:T(4,128)S(1)} %reshape.107, f32[19,2,22,3]{3,2,1,0:T(8,128)S(1)} %copy.29), kind=kLoop, calls=%fused_computation.2 | loop fusion | flops 448096 | bytes 896192 | tf_op jit(solution)/shard_map/concatenate | solution.py:190
  19.2 0.2 copy.25
  19.4 0.2 copy.26
  20.0 0.2 pad_maximum_fusion.2
  20.2 0.5 %multiply_add_fusion.25 = (f32[2,20,132]{2,1,0:T(8,128)S(1)}, f32[2,20,132]{2,1,0:T(8,128)S(1)}, f32[2,20,132]{2,1,0:T(8,128)S(1)}, f32[2,20,132]{2,1,0:T(8,128)...) fusion(f32[2,22,134]{2,1,0:T(8,128)S(1)} %get-tuple-element.61, f32[2,22,134]{2,1,0:T(8,128)S(1)} %get-tuple-element.58, ...), kind=kLoop, calls=%fused_computation.163 | loop fusion | flops 855360 | bytes 633600 | tf_op jit(solution)/shard_map/add | solution.py:142
  20.7 0.1 multiply_add_fusion.21
  20.9 0.1 multiply_add_fusion.23
  21.0 0.1 multiply_add_fusion.32
  22.6 0.5 %multiply_add_fusion.7 = (f32[2,18,130]{2,1,0:T(8,128)S(1)}, f32[2,18,130]{2,1,0:T(8,128)S(1)}, f32[2,18,130]{2,1,0:T(8,128)S(1)}, f32[2,18,130]{2,1,0:T(8,128)S...) fusion(f32[1,18,130]{2,1,0:T(8,128)S(1)} %get-tuple-element.141, f32[1,18,130]{2,1,0:T(8,128)S(1)} %get-tuple-element.140, ...), kind=kLoop, calls=%fused_computation.135 | loop fusion | flops 758160 | bytes 561600 | tf_op jit(solution)/shard_map/add | solution.py:142
  23.1 0.2 multiply_add_fusion.3
  24.3 0.6 %multiply_reduce_fusion = (f32[16,128]{1,0:T(8,128)S(1)}, f32[2,16,128]{2,1,0:T(8,128)S(1)}, f32[2,16,128]{2,1,0:T(8,128)S(1)}, f32[2,16,128]{2,1,0:T(8,128)S(1)...) fusion(s32[2,16,128]{2,1,0:T(8,128)S(1)} %copy-done.2, ...), kind=kLoop, calls=%fused_computation.653 | loop fusion | flops 2091008 | bytes 1971264 | tf_op jit(solution)/shard_map/reduce_sum | solution.py:207
  24.8 0.1 constant_dynamic-update-slice_fusion.23
  26.4 1.3 %fusion = f32[32,128,1]{1,0,2:T(8,128)} fusion(s32[16,128]{1,0:T(8,128)S(1)} %get-tuple-element.175, f32[16,128]{1,0:T(8,128)S(1)} %broadcast_multiply_fusion.1, s32[16,128]{1,0:T(8,128)S(1)} %get-tuple-element.174), kind=kOutput, calls=%fused_computation.1 | convolution fusion | flops 101056512 | bytes 40960 | tf_op jit(solution)/shard_map/dot_general | solution.py:218
  27.7 5.9 %all-to-all-start = ((f32[32,1,128]{2,1,0:T(1,128)}), f32[32,1,128]{2,1,0:T(1,128)S(1)}, u32[]{:S(2)}, u32[]{:S(2)}) async-start(f32[32,1,128]{2,1,0:T(1,128)} %bitcast.74), calls=%async_computation | async-start | bytes 32768 | tf_op jit(solution)/shard_map/all_to_all | solution.py:221
  33.7 7.1 %all-to-all-done = f32[32,1,128]{2,1,0:T(1,128)S(1)} async-done(((f32[32,1,128]{2,1,0:T(1,128)}), f32[32,1,128]{2,1,0:T(1,128)S(1)}, u32[]{:S(2)}, u32[]{:S(2)}) %all-to-all-start) | async-done | bytes 16416 | tf_op jit(solution)/shard_map/all_to_all | solution.py:221
  40.8 0.7 %reshape.120 = f32[4,32]{1,0:T(4,128)} reshape(f32[128]{0:T(128)S(1)} %reduce_sum.19) | data formatting | bytes 1024 | tf_op jit(solution)/shard_map/reshape | solution.py:224
  (122 shorter events, 6.0 us)
Async XLA Ops:
  0.6 1.0 %copy-start.1 = (bf16[19,2,16,128]{3,2,1,0:T(8,128)(2,1)S(1)}, bf16[19,2,16,128]{3,2,1,0:T(8,128)(2,1)}, u32[]{:S(2)}) copy-start(bf16[19,2,16,128]{3,2,1,0:T(8,128)(2,1)} %param.6) | copy-start | bytes 466948
  0.6 1.0 %copy-start.2 = (s32[2,16,128]{2,1,0:T(8,128)S(1)}, s32[2,16,128]{2,1,0:T(8,128)}, u32[]{:S(2)}) copy-start(s32[2,16,128]{2,1,0:T(8,128)} %param.8) | copy-start | bytes 49156
  0.7 1.0 %copy-start.3 = (s32[2,16,128]{2,1,0:T(8,128)S(1)}, s32[2,16,128]{2,1,0:T(8,128)}, u32[]{:S(2)}) copy-start(s32[2,16,128]{2,1,0:T(8,128)} %param.7) | copy-start | bytes 49156
  0.7 1.2 %copy-start = (f32[19,2,16,128]{3,2,1,0:T(8,128)S(1)}, f32[19,2,16,128]{3,2,1,0:T(8,128)}, u32[]{:S(2)}) copy-start(f32[19,2,16,128]{3,2,1,0:T(8,128)} %param.5) | copy-start | bytes 933892
  2.0 5.0 %collective-permute-start = (f32[134,128]{1,0:T(8,128)S(1)}, f32[134,128]{1,0:T(8,128)S(1)}, u32[]{:S(2)}, u32[]{:S(2)}) collective-permute-start(f32[134,128]{1,0:T(8,128)S(1)} %get-tuple-element.99), channel_id=1, source_target_pairs={{4,8},{8,4},{12,16},{16,12},{20,24},{24,20},{5,9},{9,5},{13,17},{1... | collective-permute-start | bytes 205832 | tf_op jit(solution)/shard_map/ppermute | solution.py:48
  2.6 5.3 %collective-permute-start.1 = (f32[134,128]{1,0:T(8,128)S(1)}, f32[134,128]{1,0:T(8,128)S(1)}, u32[]{:S(2)}, u32[]{:S(2)}) collective-permute-start(f32[134,128]{1,0:T(8,128)S(1)} %get-tuple-element.100), channel_id=1, source_target_pairs={{0,4},{4,0},{8,12},{12,8},{16,20},{20,16},{24,28},{28,24},{1,5},{5... | collective-permute-start | bytes 205832 | tf_op jit(solution)/shard_map/ppermute | solution.py:49
  9.9 5.2 %copy-start.4 = (s32[16,128]{1,0:T(8,128)S(1)}, s32[16,128]{1,0:T(8,128)}, u32[]{:S(2)}) copy-start(s32[16,128]{1,0:T(8,128)} %param.9) | copy-start | bytes 24580
  10.0 5.2 %collective-permute-start.2 = (f32[134,22]{0,1:T(8,128)S(1)}, f32[134,22]{0,1:T(8,128)S(1)}, u32[]{:S(2)}, u32[]{:S(2)}) collective-permute-start(f32[134,22]{0,1:T(8,128)S(1)} %get-tuple-element.172), channel_id=1, source_target_pairs={{1,2},{2,1},{5,6},{6,5},{9,10},{10,9},{13,14},{14,13},{17,18},{18,... | collective-permute-start | bytes 35384 | tf_op jit(solution)/shard_map/ppermute | solution.py:48
  10.7 6.5 %collective-permute-start.3 = (f32[134,22]{0,1:T(8,128)S(1)}, f32[134,22]{0,1:T(8,128)S(1)}, u32[]{:S(2)}, u32[]{:S(2)}) collective-permute-start(f32[134,22]{0,1:T(8,128)S(1)} %get-tuple-element.173), channel_id=1, source_target_pairs={{0,1},{1,0},{2,3},{3,2},{4,5},{5,4},{6,7},{7,6},{8,9},{9,8},{10,11... | collective-permute-start | bytes 35384 | tf_op jit(solution)/shard_map/ppermute | solution.py:49
  27.7 13.1 %all-to-all-start = ((f32[32,1,128]{2,1,0:T(1,128)}), f32[32,1,128]{2,1,0:T(1,128)S(1)}, u32[]{:S(2)}, u32[]{:S(2)}) async-start(f32[32,1,128]{2,1,0:T(1,128)} %bitcast.74), calls=%async_computation | async-start | bytes 32768 | tf_op jit(solution)/shard_map/all_to_all | solution.py:221
  33.7 7.8 %copy-start.5 = (f32[19,2,16,128]{3,2,1,0:T(8,128)}, f32[19,2,16,128]{3,2,1,0:T(8,128)S(1)}, u32[]{:S(2)}) copy-start(f32[19,2,16,128]{3,2,1,0:T(8,128)S(1)} %constant_dynamic-update-slice_fusion.5) | copy-start | bytes 933892

commit v2 on v0

v2 whole, which is shorter than its diff:
```python
import jax
import jax.numpy as jnp
from jax import lax
from jax.experimental import pallas as pl
from jax.experimental.pallas import tpu as pltpu
from jax.sharding import PartitionSpec as P

STEPS = 3
LEVELS = 8
BOTH = ("gx", "gy")
FIELDS = 5

relax_rate = 1.25
porous_max = 0.5


def lattice_table():
    speeds = [[0, 0, 0]]
    for axis_index in range(3):
        for sign_value in (1, -1):
            vector_row = [0, 0, 0]
            vector_row[axis_index] = sign_value
            speeds.append(vector_row)
    for plane_pair in ((0, 1), (0, 2), (1, 2)):
        for first_sign in (1, -1):
            for second_sign in (1, -1):
                vector_row = [0, 0, 0]
                vector_row[plane_pair[0]] = first_sign
                vector_row[plane_pair[1]] = second_sign
                speeds.append(vector_row)
    return speeds


SPEEDS = lattice_table()
PAIRS = ((1, 2), (3, 4), (5, 6), (7, 10), (8, 9), (11, 14), (12, 13), (15, 18), (16, 17))

WIDTHS = [3 if SPEEDS[q][1] != 0 else 2 for q in range(19)] + [2] * FIELDS
STARTS = [sum(WIDTHS[:n]) for n in range(19 + FIELDS)]
Z_LANES = 64


def swap_pairs(count, parity):
    pairs = []
    for i in range(count):
        j = (i ^ 1) if parity == 0 else ((i - 1) ^ 1) + 1
        if 0 <= j < count:
            pairs.append((i, j))
    return pairs


def is_even(axis):
    return lax.rem(lax.axis_index(axis), 2) == 0


def iota(shape, dim):
    return lax.broadcasted_iota(jnp.int32, shape, dim)


def moments(even, odd, rest):
    e_x, e_y, e_z, e_xy, e_xw, e_xz, e_xv, e_yz, e_yv = even
    o_x, o_y, o_z, o_xy, o_xw, o_xz, o_xv, o_yz, o_yv = odd
    d_xy = e_xy + e_xw
    d_xz = e_xz + e_xv
    d_yz = e_yz + e_yv
    s_xx = 2.0 * e_x + (d_xy + d_xz)
    s_yy = 2.0 * e_y + (d_xy + d_yz)
    s_zz = 2.0 * e_z + (d_xz + d_yz)
    s_xy = e_xy - e_xw
    s_xz = e_xz - e_xv
    s_yz = e_yz - e_yv
    total = 12.0 * rest + 2.0 * ((e_x + e_y) + e_z) + ((d_xy + d_xz) + d_yz)
    v_x = 2.0 * o_x + ((o_xy + o_xw) + (o_xz + o_xv))
    v_y = 2.0 * o_y + ((o_xy - o_xw) + (o_yz + o_yv))
    v_z = 2.0 * o_z + ((o_xz - o_xv) + (o_yz - o_yv))
    return total, (v_x, v_y, v_z), ((s_xx, s_xy, s_xz), (s_xy, s_yy, s_yz), (s_xz, s_yz, s_zz))


def contract(second, velocity):
    return [
        second[k][0] * velocity[0] + second[k][1] * velocity[1] + second[k][2] * velocity[2]
        for k in range(3)
    ]


def dot3(a, b):
    return a[0] * b[0] + a[1] * b[1] + a[2] * b[2]


def split_pairs(pulled):
    even = [pulled[i] + pulled[j] for i, j in PAIRS]
    odd = [pulled[i] - pulled[j] for i, j in PAIRS]
    return even, odd


def collide(pulled, velocity, keep, porosity):
    even, odd = split_pairs(pulled)
    total, first, second = moments(even, odd, pulled[0])
    flux = contract(second, velocity)
    twice = dot3(velocity, flux)
    gain = keep * (relax_rate / 36.0)
    stay = keep * (1.0 - relax_rate)
    base = gain * (total * (1.0 + 1.5 * dot3(velocity, velocity)) - 4.5 * twice)
    turn = [gain * (3.0 * (first[k] - velocity[k] * total) + 9.0 * flux[k]) for k in range(3)]
    both = 0.5 * (stay + porosity)
    diff = 0.5 * (stay - porosity)
    results = [None] * 19
    results[0] = (stay + porosity) * pulled[0] + base
    for n, (i, j) in enumerate(PAIRS):
        along = None
        for k in range(3):
            if SPEEDS[i][k] == 1:
                along = turn[k] if along is None else along + turn[k]
            elif SPEEDS[i][k] == -1:
                along = along - turn[k]
        same = both * even[n] + base
        swing = diff * odd[n] + along
        results[i] = same + swing
        results[j] = same - swing
    return results


MIRRORS = [
    (q, SPEEDS.index([-SPEEDS[q][0], SPEEDS[q][1], SPEEDS[q][2]]))
    for q in range(19)
    if SPEEDS[q][0] == 1
]
FLAT = [q for q in range(19) if SPEEDS[q][0] == 0] + list(range(19, 19 + FIELDS))
X_TILES = len(MIRRORS) + (len(FLAT) + 1) // 2


def turned(tile, shift, axis):
    shift = shift % tile.shape[axis]
    return tile if shift == 0 else pltpu.roll(tile, shift, axis)


def edge_kernel(
    adj_hbm, fwd_hbm, level_hbm, mask_hbm, index_hbm,
    outer, inner, fields, adj, fwd, mask, index, level, sems,
):
    copies = [
        pltpu.make_async_copy(src, dst, sems.at[n])
        for n, (src, dst) in enumerate(
            (
                (fwd_hbm, fwd), (mask_hbm, mask), (level_hbm, level),
                (adj_hbm, adj), (index_hbm, index),
            )
        )
    ]
    for copy in copies:
        copy.start()
    for copy in copies[:3]:
        copy.wait()
    depth, rows = adj.shape[1], adj.shape[2]
    for z in range(depth):
        popul = [fwd[q, z].astype(jnp.float32) for q in range(19)]
        even, odd = split_pairs(popul)
        density = popul[0]
        for n in range(9):
            density = density + even[n]
        o_x, o_y, o_z, o_xy, o_xw, o_xz, o_xv, o_yz, o_yv = odd
        per_mass = 1.0 / density
        fields[0, z] = (o_x + ((o_xy + o_xw) + (o_xz + o_xv))) * per_mass
        fields[1, z] = (o_y + ((o_xy - o_xw) + (o_yz + o_yv))) * per_mass
        fields[2, z] = (o_z + ((o_xz - o_xv) + (o_yz - o_yv))) * per_mass
        porosity = jnp.where(
            mask[z] == 1, level[z].astype(jnp.float32) * (porous_max / (LEVELS - 1)), 1.0
        )
        fields[3, z] = 1.0 - porosity
        fields[4, z] = porosity
    copies[3].wait()
    even_x = is_even("gx")
    row = iota((8, 128), 0)

    def top(n, z):
        return adj[n, z, 0:8, :] if n < 19 else fields[n - 19, z, 0:8, :]

    def bottom(n, z):
        at = slice(rows - 8, rows)
        return adj[n, z, at, :] if n < 19 else fields[n - 19, z, at, :]

    for n, (up, down) in enumerate(MIRRORS):
        low = jnp.where(row < 3, top(up, 0), turned(top(up, 1), 3, 0))
        low = jnp.where(row < 6, low, turned(top(down, 0), 6, 0))
        low = jnp.where(row < 7, low, turned(top(down, 1), 7, 0))
        high = jnp.where(row < 3, turned(bottom(down, 0), 3, 0), turned(bottom(down, 1), 6, 0))
        high = jnp.where(row < 6, high, turned(bottom(up, 0), 7, 0))
        high = jnp.where(row < 7, high, bottom(up, 1))
        inner[n] = jnp.where(even_x, high, low)
        outer[n] = jnp.where(even_x, low, high)
    for n in range(0, len(FLAT), 2):
        low = high = None
        for m, item in enumerate(FLAT[n : n + 2]):
            for z in range(depth):
                at = 4 * m + 2 * z
                up = turned(top(item, z), at, 0)
                down = turned(bottom(item, z), at + 2, 0)
                low = up if low is None else jnp.where(row < at, low, up)
                high = down if high is None else jnp.where(row < at, high, down)
        tile = len(MIRRORS) + n // 2
        inner[tile] = jnp.where(even_x, high, low)
        outer[tile] = jnp.where(even_x, low, high)
    copies[4].wait()


def side_kernel(adj, fields, got_outer, got_inner, inner, outer, adj_rim, field_rim):
    depth = adj.shape[1]
    even_x = is_even("gx")
    row = iota((8, 128), 0)

    def received(tile):
        from_in = got_inner[tile]
        from_out = got_outer[tile]
        return jnp.where(even_x, from_out, from_in), jnp.where(even_x, from_in, from_out)

    for n, (up, down) in enumerate(MIRRORS):
        low, high = received(n)
        for z in range(depth):
            adj_rim[up, z] = jnp.where(row < 4, turned(high, -3 * z, 0), turned(low, 1 - z, 0))
            adj_rim[down, z] = jnp.where(row < 4, turned(high, 2 - z, 0), turned(low, 5 - 3 * z, 0))
    for n in range(0, len(FLAT), 2):
        low, high = received(len(MIRRORS) + n // 2)
        for m, item in enumerate(FLAT[n : n + 2]):
            for z in range(depth):
                at = 4 * m + 2 * z
                rim = jnp.where(row < 4, turned(high, -at, 0), turned(low, 6 - at, 0))
                if item < 19:
                    adj_rim[item, z] = rim
                else:
                    field_rim[item - 19, z] = rim
    full = adj.shape[2] + 8
    lane = iota((full, 128), 1)
    low = high = None
    for z in range(depth):
        for n in range(19 + FIELDS):
            at = z * Z_LANES + STARTS[n]
            if n < 19:
                tile = jnp.concatenate([adj[n, z], adj_rim[n, z]], axis=0)
            else:
                tile = jnp.concatenate([fields[n - 19, z], field_rim[n - 19, z]], axis=0)
            up = turned(tile, at, 1)
            down = turned(tile, at + WIDTHS[n], 1)
            low = up if low is None else jnp.where(lane >= at, up, low)
            high = down if high is None else jnp.where(lane >= at, down, high)
    even_y = is_even("gy")
    inner[...] = jnp.where(even_y, high, low)
    outer[...] = jnp.where(even_y, low, high)


def step_kernel(
    owners, chunk, adj, adj_rim, fields, field_rim, got_inner, got_outer, fwd, mask, index,
    grid, last, adj_m, adj_h, pull_m, pull_h, field_h, summed,
):
    depth, rows = adj.shape[1], adj.shape[2]
    full = rows + 8
    lane = iota((full, 128), 1)
    even_y = is_even("gy")
    from_in = got_inner[...]
    from_out = got_outer[...]
    low = jnp.where(even_y, from_out, from_in)
    high = jnp.where(even_y, from_in, from_out)
    for n in range(19 + FIELDS):
        for z in range(depth):
            at = z * Z_LANES + STARTS[n]
            above = high if at == 0 else pltpu.roll(high, 128 - at, 1)
            turn = (256 - WIDTHS[n] - at) % 128
            below = low if turn == 0 else pltpu.roll(low, turn, 1)
            halo = jnp.where(lane < 64, above, below)
            if n < 19:
                adj_h[n, z] = halo
            else:
                field_h[n - 19, z] = halo

    for step_num in range(STEPS):
        final = step_num == STEPS - 1
        for q in range(19):
            shift_x, shift_y, shift_z = SPEEDS[q]
            for z in range(depth):
                src = (z + shift_z) % depth
                if step_num == 0:
                    main = jnp.concatenate([adj[q, src], adj_rim[q, src]], axis=0)
                else:
                    main = adj_m[q, src]
                side = adj_h[q, src]
                if shift_x:
                    main = pltpu.roll(main, (-shift_x) % full, 0)
                    side = pltpu.roll(side, (-shift_x) % full, 0)
                if shift_y:
                    main = pltpu.roll(main, (-shift_y) % 128, 1)
                    side = pltpu.roll(side, (-shift_y) % 128, 1)
                    cross = lane == (127 if shift_y == 1 else 0)
                    main, side = jnp.where(cross, side, main), jnp.where(cross, main, side)
                own = main[:rows]
                if final:
                    last[q, z] = own
                    summed[q, z] = summed[q, z] + own
                else:
                    pull_m[q, z] = main
                    pull_h[q, z] = side
                    summed[q, z] = own if step_num == 0 else summed[q, z] + own
        if not final:
            for z in range(depth):
                for t in range(full // 8):
                    at = slice(8 * t, 8 * t + 8)
                    pulled = [pull_m[q, z, at, :] for q in range(19)]
                    if 8 * t < rows:
                        here = [fields[k, z, at, :] for k in range(FIELDS)]
                    else:
                        here = [field_rim[k, z] for k in range(FIELDS)]
                    out = collide(pulled, here[:3], here[3], here[4])
                    for q in range(19):
                        adj_m[q, z, at, :] = out[q]
                    pulled = [pull_h[q, z, at, :] for q in range(19)]
                    here = [field_h[k, z, at, :] for k in range(FIELDS)]
                    out = collide(pulled, here[:3], here[3], here[4])
                    for q in range(19):
                        adj_h[q, z, at, :] = out[q]

    column = None
    for z in range(depth):
        popul = [fwd[q, z].astype(jnp.float32) for q in range(19)]
        f_even, f_odd = split_pairs(popul)
        density = popul[0]
        for n in range(9):
            density = density + f_even[n]
        pulled = [summed[q, z] for q in range(19)]
        even, odd = split_pairs(pulled)
        total, first, second = moments(even, odd, pulled[0])
        velocity = [fields[k, z] for k in range(3)]
        flux = contract(second, velocity)
        even_sum = even[0] * f_even[0]
        odd_sum = odd[0] * f_odd[0]
        for n in range(1, 9):
            even_sum = even_sum + even[n] * f_even[n]
            odd_sum = odd_sum + odd[n] * f_odd[n]
        relaxed = (
            total * (1.0 - 1.5 * dot3(velocity, velocity))
            + 3.0 * dot3(velocity, first)
            + 4.5 * dot3(velocity, flux)
        )
        half = 0.5 * relax_rate
        sensitivity = (
            half * even_sum
            + (half - 1.0) * odd_sum
            + relax_rate * (popul[0] * pulled[0])
            - (relax_rate / 36.0) * (density * relaxed)
        )
        term = sensitivity * mask[z].astype(jnp.float32)
        column = term if column is None else column + term
    column = column * (porous_max / (LEVELS - 1))
    top = column.astype(jnp.bfloat16).astype(jnp.float32)
    rest = column - top
    owner = lax.div(index[...], chunk) if chunk & (chunk - 1) else index[...] >> (chunk.bit_length() - 1)
    slot = index[...] - owner * chunk
    owner_row = iota((owners, 128), 0)
    slot_row = iota((chunk, 128), 0)
    acc = None
    for x in range(0, rows, 2):
        lhs = []
        rhs = []
        for r in (x, x + 1):
            hot = owner_row == owner[r : r + 1, :]
            lhs.append(
                jnp.concatenate(
                    [
                        jnp.where(hot, top[r : r + 1, :], 0.0).astype(jnp.bfloat16),
                        jnp.where(hot, rest[r : r + 1, :], 0.0).astype(jnp.bfloat16),
                    ],
                    axis=0,
                )
            )
            rhs.append(jnp.where(slot_row == slot[r : r + 1, :], 1.0, 0.0).astype(jnp.bfloat16))
        part = lax.dot_general(
            jnp.concatenate(lhs, axis=1),
            jnp.concatenate(rhs, axis=1),
            (((1,), (1,)), ((), ())),
            preferred_element_type=jnp.float32,
        )
        acc = part if acc is None else acc + part
    grid[...] = acc[:owners] + acc[owners:]


def final_kernel(last, fields, out):
    depth, rows = last.shape[1], last.shape[2]
    for z in range(depth):
        for t in range(rows // 8):
            at = slice(8 * t, 8 * t + 8)
            here = [fields[k, z, at, :] for k in range(FIELDS)]
            result = collide([last[q, z, at, :] for q in range(19)], here[:3], here[3], here[4])
            for q in range(19):
                out[q, z, at, :] = result[q]


def call(kernel, out_types, args, scratch=(), flops=0, where=pltpu.VMEM):
    moved = sum(a.size * a.dtype.itemsize for a in args)
    return pl.pallas_call(
        kernel,
        out_shape=[pltpu.VMEM(shape, dtype) for shape, dtype in out_types],
        in_specs=[pl.BlockSpec(memory_space=where)] * len(args),
        out_specs=[pl.BlockSpec(memory_space=pltpu.VMEM)] * len(out_types),
        scratch_shapes=list(scratch),
        compiler_params=pltpu.CompilerParams(vmem_limit_bytes=16 << 20),
        cost_estimate=pl.CostEstimate(flops=flops, bytes_accessed=moved, transcendentals=0),
    )(*[pltpu.with_memory_space_constraint(a, where) for a in args])


def per_device(adjoint_end, forward_pop, porosity_level, fluid_mask, design_index):
    depth, tile_x, tile_y = adjoint_end.shape[1:]
    full = tile_x + 8
    gx_count = lax.axis_size("gx")
    gy_count = lax.axis_size("gy")
    owners = gx_count * gy_count
    design_cols = tile_x * gx_count // 4
    design_rows = tile_y * gy_count // 4
    chunk = design_rows * design_cols // owners
    f32 = jnp.float32
    own = ((19, depth, tile_x, tile_y), f32)
    wide = pltpu.VMEM((19, depth, full, tile_y), f32)

    outer, inner, fields, adj, fwd, mask, index = call(
        edge_kernel,
        [
            ((X_TILES, 8, tile_y), f32), ((X_TILES, 8, tile_y), f32),
            ((FIELDS, depth, tile_x, tile_y), f32), own, (forward_pop.shape, forward_pop.dtype),
            (fluid_mask.shape, fluid_mask.dtype), (design_index.shape, design_index.dtype),
        ],
        [adjoint_end, forward_pop, porosity_level, fluid_mask, design_index],
        [
            pltpu.VMEM(porosity_level.shape, porosity_level.dtype),
            pltpu.SemaphoreType.DMA((5,)),
        ],
        where=pltpu.HBM,
    )
    got_outer = lax.ppermute(outer, "gx", swap_pairs(gx_count, 1))
    got_inner = lax.ppermute(inner, "gx", swap_pairs(gx_count, 0))
    inner, outer, adj_rim, field_rim = call(
        side_kernel,
        [
            ((full, 128), f32), ((full, 128), f32), ((19, depth, 8, tile_y), f32),
            ((FIELDS, depth, 8, tile_y), f32),
        ],
        [adj, fields, got_outer, got_inner],
    )
    got_inner = lax.ppermute(inner, "gy", swap_pairs(gy_count, 0))
    got_outer = lax.ppermute(outer, "gy", swap_pairs(gy_count, 1))
    grid, last = call(
        lambda *refs: step_kernel(owners, chunk, *refs),
        [((owners, chunk), f32), own],
        [adj, adj_rim, fields, field_rim, got_inner, got_outer, fwd, mask, index],
        [
            wide, wide, wide, wide, pltpu.VMEM((FIELDS, depth, full, tile_y), f32),
            pltpu.VMEM(*own),
        ],
    )
    received = lax.all_to_all(
        grid.reshape(owners, 1, chunk), BOTH, split_axis=0, concat_axis=0, tiled=True
    )
    (adjoint_start,) = call(final_kernel, [own], [last, fields], flops=10**6)
    owned = jnp.sum(received, axis=0).reshape(design_rows // owners, design_cols)
    return (adjoint_start, owned)


def solution(mesh):
    in_specs = (
        P(None, None, "gx", "gy"),
        P(None, None, "gx", "gy"),
        P(None, "gx", "gy"),
        P(None, "gx", "gy"),
        P("gx", "gy"),
    )
    out_specs = (P(None, None, "gx", "gy"), P(("gx", "gy"), None))
    return jax.shard_map(
        per_device, mesh=mesh, in_specs=in_specs, out_specs=out_specs, check_vma=False
    )
```

time: 137 us -> 31.8 us (0.23)
  blocking collectives: 43.2 us -> 0 us
  waiting for transfers between devices: 34.8 us -> 8.67 us
  other arithmetic: 18.6 us -> 0.05 us
  starting transfers between devices: 32.4 us -> 17 us
  local copies, waits for them, and re-layouts: 5.48 us -> 1.38 us
  Pallas kernels: 0 us -> 3.74 us
    unnamed x1 -> x0, blocking collectives: 43.2 us -> none
    ppermute x12 -> x4, waiting for transfers between devices: 34.8 us -> 2.34 us  [the longest x1 1.46 us: per_device(): got_inner = lax.ppermute(inner, 'gy', swap_pairs(gy_count, 0))]
    ppermute x12 -> x4, starting transfers between devices: 32.4 us -> 7.32 us  [the longest x1 4.36 us: per_device(): got_inner = lax.ppermute(inner, 'gx', swap_pairs(gx_count, 0))]
    scatter-add x1 -> x0, other arithmetic: 14.7 us -> none  [per_device(): jax.ops.segment_sum(column_sum.reshape(-1), design_index.reshape(-1), num...]
    all_to_all x0 -> x1, starting transfers between devices: none -> 9.72 us  [per_device(): lax.all_to_all(grid.reshape(owners, 1, chunk), BOTH, split_axis=0, concat...]
    all_to_all x0 -> x1, waiting for transfers between devices: none -> 6.32 us  [per_device(): lax.all_to_all(grid.reshape(owners, 1, chunk), BOTH, split_axis=0, concat...]
    pallas_call x0 -> x4, Pallas kernels: none -> 3.74 us  [call(): pl.pallas_call(kernel, out_shape=[pltpu.VMEM(shape, dtype) for shape, dty...]
    unnamed x38 -> x1, local copies, waits for them, and re-layouts: 3.65 us -> 0.72 us
  transfers between devices with their start and end apart: 12 -> 5, of which waited for: 9 -> 3; matrix products, arithmetic and copies ran while one was open for 1% -> 2% of each run, Pallas kernels for 0% -> 0%
where the time goes in v2:
time: 31.8 us; the launch traced here: 31.6 us
  starting transfers between devices  17 us (53%)
  waiting for transfers between devices  8.67 us (27%)
  Pallas kernels  3.74 us (12%)
  local copies, waits for them, and re-layouts  1.38 us (4%)
  between operations  0.68 us (2%)
    all_to_all x1, starting transfers between devices, per_device(): lax.all_to_all(grid.reshape(owners, 1, chunk), BOTH, split_axis=0, concat...  9.72 us
    all_to_all x1, waiting for transfers between devices, per_device(): lax.all_to_all(grid.reshape(owners, 1, chunk), BOTH, split_axis=0, concat...  6.32 us
    ppermute x1, starting transfers between devices, per_device(): got_inner = lax.ppermute(inner, 'gx', swap_pairs(gx_count, 0))  4.36 us
    pallas_call x4, Pallas kernels, call(): pl.pallas_call(kernel, out_shape=[pltpu.VMEM(shape, dtype) for shape, dty...  3.74 us
    ppermute x1, starting transfers between devices, per_device(): got_inner = lax.ppermute(inner, 'gy', swap_pairs(gy_count, 0))  1.64 us
    ppermute x1, waiting for transfers between devices, per_device(): got_inner = lax.ppermute(inner, 'gy', swap_pairs(gy_count, 0))  1.46 us
    ppermute x1, waiting for transfers between devices, per_device(): got_inner = lax.ppermute(inner, 'gx', swap_pairs(gx_count, 0))  0.88 us
    unnamed x1, local copies, waits for them, and re-layouts  0.72 us
  transfers between devices with their start and end apart: 5, of which 3 were waited for; matrix products, arithmetic and copies ran while one was open for 2% of the time, Pallas kernels for 0%

profile of v2, /device:TPU:0, one launch (start us, length us, event | category | flops | bytes accessed | tf_op | source)
XLA Modules:
  0.0 31.6 jit_solution(1652156938326623342)
XLA Ops:
  0.6 1.2 %shard_map.68 = (f32[12,8,128]{2,1,0:T(8,128)S(1)}, f32[12,8,128]{2,1,0:T(8,128)S(1)}, f32[5,2,16,128]{3,2,1,0:T(8,128)S(1)}, f32[19,2,16,128]{3,2,1,0:T(8,128)S...) custom-call(f32[19,2,16,128]{3,2,1,0:T(8,128)} %adj_hbm.1, ...), custom_call_target="tpu_custom_call" | custom-call | bytes 507904 | tf_op jit(solution)/shard_map/pallas_call | solution.py:395
  1.8 0.7 %collective-permute-start = (f32[12,8,128]{2,1,0:T(8,128)S(1)}, f32[12,8,128]{2,1,0:T(8,128)S(1)}, u32[]{:S(2)}, u32[]{:S(2)}) collective-permute-start(f32[12,8,128]{2,1,0:T(8,128)S(1)} %get-tuple-element.17), channel_id=1, source_target_pairs={{4,8},{8,4},{12,16},{16,12},{20,24},{24,20},{5,9},{9,5},{13,17},{1... | collective-permute-start | bytes 147464 | tf_op jit(solution)/shard_map/ppermute | solution.py:433
  2.5 4.4 %collective-permute-start.1 = (f32[12,8,128]{2,1,0:T(8,128)S(1)}, f32[12,8,128]{2,1,0:T(8,128)S(1)}, u32[]{:S(2)}, u32[]{:S(2)}) collective-permute-start(f32[12,8,128]{2,1,0:T(8,128)S(1)} %get-tuple-element.18), channel_id=1, source_target_pairs={{0,4},{4,0},{8,12},{12,8},{16,20},{20,16},{24,28},{28,24},{1,5},{5... | collective-permute-start | bytes 147464 | tf_op jit(solution)/shard_map/ppermute | solution.py:434
  6.8 0.0 collective-permute-done.got_outer
  6.8 0.9 %collective-permute-done.1.got_inner = f32[12,8,128]{2,1,0:T(8,128)S(1)} collective-permute-done((f32[12,8,128]{2,1,0:T(8,128)S(1)}, f32[12,8,128]{2,1,0:T(8,128)S(1)}, u32[]{:S(2)}, u32[]{:S(2)}) %collective-permute-start.1) | collective-permute-done | bytes 49184 | tf_op jit(solution)/shard_map/ppermute | solution.py:434
  7.7 0.4 %shard_map.69 = (f32[24,128]{1,0:T(8,128)S(1)}, f32[24,128]{1,0:T(8,128)S(1)}, f32[19,2,8,128]{3,2,1,0:T(8,128)S(1)}, f32[5,2,8,128]{3,2,1,0:T(8,128)S(1)}) custom-call(f32[19,2,16,128]{3,2,1,0:T(8,128)S(1)} %get-tuple-element.15.adj.refs_0_, f32[5,2,16,128]{3,2,1,0:T(8,128)S(1)} %get-tuple-element.16.fields.refs_2_, ...), custom_call_target="tpu_custom_call" | custom-call | bytes 491520 | tf_op jit(solution)/shard_map/pallas_call | solution.py:395
  8.1 1.6 %collective-permute-start.2 = (f32[24,128]{1,0:T(8,128)S(1)}, f32[24,128]{1,0:T(8,128)S(1)}, u32[]{:S(2)}, u32[]{:S(2)}) collective-permute-start(f32[24,128]{1,0:T(8,128)S(1)} %get-tuple-element.21), channel_id=1, source_target_pairs={{0,1},{1,0},{2,3},{3,2},{4,5},{5,4},{6,7},{7,6},{8,9},{9,8},{10,11... | collective-permute-start | bytes 36872 | tf_op jit(solution)/shard_map/ppermute | solution.py:443
  9.7 0.7 %collective-permute-start.3 = (f32[24,128]{1,0:T(8,128)S(1)}, f32[24,128]{1,0:T(8,128)S(1)}, u32[]{:S(2)}, u32[]{:S(2)}) collective-permute-start(f32[24,128]{1,0:T(8,128)S(1)} %get-tuple-element.22), channel_id=1, source_target_pairs={{1,2},{2,1},{5,6},{6,5},{9,10},{10,9},{13,14},{14,13},{17,18},{18,... | collective-permute-start | bytes 36872 | tf_op jit(solution)/shard_map/ppermute | solution.py:444
  10.4 1.5 %collective-permute-done.2.refs_4_ = f32[24,128]{1,0:T(8,128)S(1)} collective-permute-done((f32[24,128]{1,0:T(8,128)S(1)}, f32[24,128]{1,0:T(8,128)S(1)}, u32[]{:S(2)}, u32[]{:S(2)}) %collective-permute-start.2) | collective-permute-done | bytes 12320 | tf_op jit(solution)/shard_map/ppermute | solution.py:443
  11.9 0.0 collective-permute-done.3.refs_5_
  11.9 2.1 %shard_map.70 = (f32[32,128]{1,0:T(8,128)}, f32[19,2,16,128]{3,2,1,0:T(8,128)S(1)}) custom-call(f32[19,2,16,128]{3,2,1,0:T(8,128)S(1)} %get-tuple-element.15.adj.refs_0_, f32[19,2,8,128]{3,2,1,0:T(8,128)S(1)} %get-tuple-element.19.refs_1_, f32[5,2,16,128]{3,2,1,0:T(8,128)S(1)} %get-tuple-element.16.fields.refs_2_, ...), custom_call_target="tpu_custom_call" | custom-call | bytes 794624 | tf_op jit(solution)/shard_map/pallas_call | solution.py:395
  14.0 9.7 %all-to-all-start = ((f32[32,1,128]{2,1,0:T(1,128)}), f32[32,1,128]{2,1,0:T(1,128)S(1)}, u32[]{:S(2)}, u32[]{:S(2)}) async-start(f32[32,1,128]{2,1,0:T(1,128)} %bitcast.1), calls=%async_computation | async-start | bytes 32768 | tf_op jit(solution)/shard_map/all_to_all | solution.py:454
  23.7 0.1 shard_map.71
  23.8 0.7 %copy.8 = f32[19,2,16,128]{3,2,1,0:T(8,128)} copy(f32[19,2,16,128]{3,2,1,0:T(8,128)S(1)} %shard_map.71) | data formatting | bytes 622592
  24.5 6.3 %all-to-all-done = f32[32,1,128]{2,1,0:T(1,128)S(1)} async-done(((f32[32,1,128]{2,1,0:T(1,128)}), f32[32,1,128]{2,1,0:T(1,128)S(1)}, u32[]{:S(2)}, u32[]{:S(2)}) %all-to-all-start) | async-done | bytes 16416 | tf_op jit(solution)/shard_map/all_to_all | solution.py:454
  30.8 0.1 reduce_sum.9
  30.9 0.7 %reshape.13 = f32[4,32]{1,0:T(4,128)} reshape(f32[128]{0:T(128)S(1)} %reduce_sum.9) | data formatting | bytes 1024 | tf_op jit(solution)/shard_map/reshape | solution.py:458
Async XLA Ops:
  1.8 5.0 %collective-permute-start = (f32[12,8,128]{2,1,0:T(8,128)S(1)}, f32[12,8,128]{2,1,0:T(8,128)S(1)}, u32[]{:S(2)}, u32[]{:S(2)}) collective-permute-start(f32[12,8,128]{2,1,0:T(8,128)S(1)} %get-tuple-element.17), channel_id=1, source_target_pairs={{4,8},{8,4},{12,16},{16,12},{20,24},{24,20},{5,9},{9,5},{13,17},{1... | collective-permute-start | bytes 147464 | tf_op jit(solution)/shard_map/ppermute | solution.py:433
  2.5 5.2 %collective-permute-start.1 = (f32[12,8,128]{2,1,0:T(8,128)S(1)}, f32[12,8,128]{2,1,0:T(8,128)S(1)}, u32[]{:S(2)}, u32[]{:S(2)}) collective-permute-start(f32[12,8,128]{2,1,0:T(8,128)S(1)} %get-tuple-element.18), channel_id=1, source_target_pairs={{0,4},{4,0},{8,12},{12,8},{16,20},{20,16},{24,28},{28,24},{1,5},{5... | collective-permute-start | bytes 147464 | tf_op jit(solution)/shard_map/ppermute | solution.py:434
  8.1 3.8 %collective-permute-start.2 = (f32[24,128]{1,0:T(8,128)S(1)}, f32[24,128]{1,0:T(8,128)S(1)}, u32[]{:S(2)}, u32[]{:S(2)}) collective-permute-start(f32[24,128]{1,0:T(8,128)S(1)} %get-tuple-element.21), channel_id=1, source_target_pairs={{0,1},{1,0},{2,3},{3,2},{4,5},{5,4},{6,7},{7,6},{8,9},{9,8},{10,11... | collective-permute-start | bytes 36872 | tf_op jit(solution)/shard_map/ppermute | solution.py:443
  9.7 2.1 %collective-permute-start.3 = (f32[24,128]{1,0:T(8,128)S(1)}, f32[24,128]{1,0:T(8,128)S(1)}, u32[]{:S(2)}, u32[]{:S(2)}) collective-permute-start(f32[24,128]{1,0:T(8,128)S(1)} %get-tuple-element.22), channel_id=1, source_target_pairs={{1,2},{2,1},{5,6},{6,5},{9,10},{10,9},{13,14},{14,13},{17,18},{18,... | collective-permute-start | bytes 36872 | tf_op jit(solution)/shard_map/ppermute | solution.py:444
  14.0 16.9 %all-to-all-start = ((f32[32,1,128]{2,1,0:T(1,128)}), f32[32,1,128]{2,1,0:T(1,128)S(1)}, u32[]{:S(2)}, u32[]{:S(2)}) async-start(f32[32,1,128]{2,1,0:T(1,128)} %bitcast.1), calls=%async_computation | async-start | bytes 32768 | tf_op jit(solution)/shard_map/all_to_all | solution.py:454

commit v3 on v2

--- a/solution.py
+++ b/solution.py
@@ -202,8 +202,53 @@
     copies[4].wait()
 
 
-def side_kernel(adj, fields, got_outer, got_inner, inner, outer, adj_rim, field_rim):
-    depth = adj.shape[1]
+RIGHT = 16
+LEFT = 43
+
+
+def strip_of(pair):
+    lane = iota(pair[0].shape, 1)
+    parts = [turned(pair[z], side + z * Z_LANES, 1) for z in range(2) for side in (RIGHT, LEFT)]
+    strip = parts[3]
+    for n in (2, 1, 0):
+        strip = jnp.where(lane < 32 * (n + 1), parts[n], strip)
+    return strip
+
+
+def pack_sides(tiles):
+    low = high = None
+    for z in range(2):
+        for n in range(19 + FIELDS):
+            at = z * Z_LANES + STARTS[n]
+            tile = tiles(n, z)
+            up = turned(tile, at, 1)
+            down = turned(tile, at + WIDTHS[n], 1)
+            lane = iota(tile.shape, 1)
+            low = up if low is None else jnp.where(lane >= at, up, low)
+            high = down if high is None else jnp.where(lane >= at, down, high)
+    return low, high
+
+
+def edge_line(right, left):
+    lane = iota(right.shape, 1)
+    block = jnp.where(lane < 3, right, jnp.where(lane < 6, left, 0.0))
+    return jnp.sum(pltpu.roll(block, 0, 1, stride=8, stride_axis=0), axis=0, keepdims=True)
+
+
+def own_kernel(adj, fields, fwd, mask, index, low_own, high_own, fwd_strip, mask_strip, line):
+    low, high = pack_sides(lambda n, z: adj[n, z] if n < 19 else fields[n - 19, z])
+    low_own[...] = low
+    high_own[...] = high
+    for q in range(19):
+        fwd_strip[q] = strip_of([fwd[q, z].astype(jnp.float32) for z in range(2)])
+    mask_strip[...] = strip_of([mask[z].astype(jnp.float32) for z in range(2)])
+    where = index[...].astype(jnp.float32)
+    line[...] = jnp.broadcast_to(
+        edge_line(turned(where, -125, 1), turned(where, 3, 1)), line.shape
+    )
+
+
+def side_kernel(got_outer, got_inner, low_own, high_own, outer, inner, adj_rim, field_rim):
     even_x = is_even("gx")
     row = iota((8, 128), 0)
 
@@ -214,189 +259,229 @@
 
     for n, (up, down) in enumerate(MIRRORS):
         low, high = received(n)
-        for z in range(depth):
+        for z in range(2):
             adj_rim[up, z] = jnp.where(row < 4, turned(high, -3 * z, 0), turned(low, 1 - z, 0))
             adj_rim[down, z] = jnp.where(row < 4, turned(high, 2 - z, 0), turned(low, 5 - 3 * z, 0))
     for n in range(0, len(FLAT), 2):
         low, high = received(len(MIRRORS) + n // 2)
         for m, item in enumerate(FLAT[n : n + 2]):
-            for z in range(depth):
+            for z in range(2):
                 at = 4 * m + 2 * z
                 rim = jnp.where(row < 4, turned(high, -at, 0), turned(low, 6 - at, 0))
                 if item < 19:
                     adj_rim[item, z] = rim
                 else:
                     field_rim[item - 19, z] = rim
-    full = adj.shape[2] + 8
-    lane = iota((full, 128), 1)
-    low = high = None
-    for z in range(depth):
-        for n in range(19 + FIELDS):
-            at = z * Z_LANES + STARTS[n]
-            if n < 19:
-                tile = jnp.concatenate([adj[n, z], adj_rim[n, z]], axis=0)
-            else:
-                tile = jnp.concatenate([fields[n - 19, z], field_rim[n - 19, z]], axis=0)
-            up = turned(tile, at, 1)
-            down = turned(tile, at + WIDTHS[n], 1)
-            low = up if low is None else jnp.where(lane >= at, up, low)
-            high = down if high is None else jnp.where(lane >= at, down, high)
+    low, high = pack_sides(lambda n, z: adj_rim[n, z] if n < 19 else field_rim[n - 19, z])
+    low = jnp.concatenate([low_own[...], low], axis=0)
+    high = jnp.concatenate([high_own[...], high], axis=0)
     even_y = is_even("gy")
     inner[...] = jnp.where(even_y, high, low)
     outer[...] = jnp.where(even_y, low, high)
 
 
-def step_kernel(
-    owners, chunk, adj, adj_rim, fields, field_rim, got_inner, got_outer, fwd, mask, index,
-    grid, last, adj_m, adj_h, pull_m, pull_h, field_h, summed,
+def sensitivity_of(pulled, popul, velocity):
+    f_even, f_odd = split_pairs(popul)
+    density = popul[0]
+    for n in range(9):
+        density = density + f_even[n]
+    even, odd = split_pairs(pulled)
+    total, first, second = moments(even, odd, pulled[0])
+    flux = contract(second, velocity)
+    even_sum = even[0] * f_even[0]
+    odd_sum = odd[0] * f_odd[0]
+    for n in range(1, 9):
+        even_sum = even_sum + even[n] * f_even[n]
+        odd_sum = odd_sum + odd[n] * f_odd[n]
+    relaxed = (
+        total * (1.0 - 1.5 * dot3(velocity, velocity))
+        + 3.0 * dot3(velocity, first)
+        + 4.5 * dot3(velocity, flux)
+    )
+    half = 0.5 * relax_rate
+    return (
+        half * even_sum
+        + (half - 1.0) * odd_sum
+        + relax_rate * (popul[0] * pulled[0])
+        - (relax_rate / 36.0) * (density * relaxed)
+    )
+
+
+def hot_rows(values, owner, slot, owners, chunk):
+    top = values.astype(jnp.bfloat16).astype(jnp.float32)
+    hot = iota((owners, 128), 0) == owner
+    lhs = jnp.concatenate(
+        [
+            jnp.where(hot, top, 0.0).astype(jnp.bfloat16),
+            jnp.where(hot, values - top, 0.0).astype(jnp.bfloat16),
+        ],
+        axis=0,
+    )
+    rhs = jnp.where(iota((chunk, 128), 0) == slot, 1.0, 0.0).astype(jnp.bfloat16)
+    return lhs, rhs
+
+
+def hot_product(lhs, rhs):
+    return lax.dot_general(
+        lhs, rhs, (((1,), (1,)), ((), ())), preferred_element_type=jnp.float32
+    )
+
+
+def split_index(index, chunk):
+    if chunk & (chunk - 1):
+        owner = lax.div(index, jnp.full(index.shape, chunk, index.dtype))
+    else:
+        owner = index >> (chunk.bit_length() - 1)
+    return owner, index - owner * chunk
+
+
+def main_kernel(
+    owners, chunk, adj, adj_rim, fields, field_rim, fwd, mask, index,
+    grid, inside, strip, field_strip, state, pulls, summed,
 ):
-    depth, rows = adj.shape[1], adj.shape[2]
+    rows = adj.shape[2]
     full = rows + 8
-    lane = iota((full, 128), 1)
+    for step_num in range(STEPS):
+        final = step_num == STEPS - 1
+        for q in range(19):
+            shift_x, shift_y, shift_z = SPEEDS[q]
+            if step_num == 0:
+                start = [jnp.concatenate([adj[q, z], adj_rim[q, z]], axis=0) for z in range(2)]
+                strip[q] = strip_of(start)
+            for z in range(2):
+                src = (z + shift_z) % 2
+                main = start[src] if step_num == 0 else state[q, src]
+                main = turned(turned(main, -shift_x, 0), -shift_y, 1)
+                pulls[q, z] = main
+                own = main[:rows]
+                summed[q, z] = own if step_num == 0 else summed[q, z] + own
+        for z in range(2):
+            for t in range((rows if final else full) // 8):
+                at = slice(8 * t, 8 * t + 8)
+                if 8 * t < rows:
+                    here = [fields[k, z, at, :] for k in range(FIELDS)]
+                else:
+                    here = [field_rim[k, z] for k in range(FIELDS)]
+                out = collide([pulls[q, z, at, :] for q in range(19)], here[:3], here[3], here[4])
+                into = inside if final else state
+                for q in range(19):
+                    into[q, z, at, :] = out[q]
+    for k in range(FIELDS):
+        field_strip[k] = strip_of(
+            [jnp.concatenate([fields[k, z], field_rim[k, z]], axis=0) for z in range(2)]
+        )
+    column = None
+    for z in range(2):
+        term = sensitivity_of(
+            [summed[q, z] for q in range(19)],
+            [fwd[q, z].astype(jnp.float32) for q in range(19)],
+            [fields[k, z] for k in range(3)],
+        ) * mask[z].astype(jnp.float32)
+        column = term if column is None else column + term
+    lane = iota(column.shape, 1)
+    column = jnp.where((lane >= 3) & (lane < 125), column * (porous_max / (LEVELS - 1)), 0.0)
+    owner, slot = split_index(index[...], chunk)
+    acc = None
+    for x in range(0, rows, 2):
+        parts = [
+            hot_rows(column[r : r + 1], owner[r : r + 1], slot[r : r + 1], owners, chunk)
+            for r in (x, x + 1)
+        ]
+        part = hot_product(
+            jnp.concatenate([p[0] for p in parts], axis=1),
+            jnp.concatenate([p[1] for p in parts], axis=1),
+        )
+        acc = part if acc is None else acc + part
+    grid[...] = acc[:owners] + acc[owners:]
+
+
+def strip_kernel(
+    got_outer, got_inner, strip, field_strip, state, summed, pulls, field_state,
+):
+    full = strip.shape[1]
+    rows = full - 8
     even_y = is_even("gy")
     from_in = got_inner[...]
     from_out = got_outer[...]
     low = jnp.where(even_y, from_out, from_in)
     high = jnp.where(even_y, from_in, from_out)
-    for n in range(19 + FIELDS):
-        for z in range(depth):
-            at = z * Z_LANES + STARTS[n]
-            above = high if at == 0 else pltpu.roll(high, 128 - at, 1)
-            turn = (256 - WIDTHS[n] - at) % 128
-            below = low if turn == 0 else pltpu.roll(low, turn, 1)
-            halo = jnp.where(lane < 64, above, below)
-            if n < 19:
-                adj_h[n, z] = halo
-            else:
-                field_h[n - 19, z] = halo
-
+    lane = iota((full, 128), 1) & (Z_LANES - 1)
+    at_right = (lane >= RIGHT) & (lane < RIGHT + 3)
+    at_left = (lane >= LEFT - 3) & (lane < LEFT)
+
+    def joined(n, own):
+        right = turned(high, RIGHT - STARTS[n], 1)
+        left = turned(low, LEFT - WIDTHS[n] - STARTS[n], 1)
+        return jnp.where(at_left, left, jnp.where(at_right, right, own))
+
+    for k in range(FIELDS):
+        field_state[k] = joined(19 + k, field_strip[k])
     for step_num in range(STEPS):
         final = step_num == STEPS - 1
         for q in range(19):
             shift_x, shift_y, shift_z = SPEEDS[q]
-            for z in range(depth):
-                src = (z + shift_z) % depth
-                if step_num == 0:
-                    main = jnp.concatenate([adj[q, src], adj_rim[q, src]], axis=0)
-                else:
-                    main = adj_m[q, src]
-                side = adj_h[q, src]
-                if shift_x:
-                    main = pltpu.roll(main, (-shift_x) % full, 0)
-                    side = pltpu.roll(side, (-shift_x) % full, 0)
-                if shift_y:
-                    main = pltpu.roll(main, (-shift_y) % 128, 1)
-                    side = pltpu.roll(side, (-shift_y) % 128, 1)
-                    cross = lane == (127 if shift_y == 1 else 0)
-                    main, side = jnp.where(cross, side, main), jnp.where(cross, main, side)
-                own = main[:rows]
-                if final:
-                    last[q, z] = own
-                    summed[q, z] = summed[q, z] + own
-                else:
-                    pull_m[q, z] = main
-                    pull_h[q, z] = side
-                    summed[q, z] = own if step_num == 0 else summed[q, z] + own
-        if not final:
-            for z in range(depth):
-                for t in range(full // 8):
-                    at = slice(8 * t, 8 * t + 8)
-                    pulled = [pull_m[q, z, at, :] for q in range(19)]
-                    if 8 * t < rows:
-                        here = [fields[k, z, at, :] for k in range(FIELDS)]
-                    else:
-                        here = [field_rim[k, z] for k in range(FIELDS)]
-                    out = collide(pulled, here[:3], here[3], here[4])
-                    for q in range(19):
-                        adj_m[q, z, at, :] = out[q]
-                    pulled = [pull_h[q, z, at, :] for q in range(19)]
-                    here = [field_h[k, z, at, :] for k in range(FIELDS)]
-                    out = collide(pulled, here[:3], here[3], here[4])
-                    for q in range(19):
-                        adj_h[q, z, at, :] = out[q]
-
-    column = None
-    for z in range(depth):
-        popul = [fwd[q, z].astype(jnp.float32) for q in range(19)]
-        f_even, f_odd = split_pairs(popul)
-        density = popul[0]
-        for n in range(9):
-            density = density + f_even[n]
-        pulled = [summed[q, z] for q in range(19)]
-        even, odd = split_pairs(pulled)
-        total, first, second = moments(even, odd, pulled[0])
-        velocity = [fields[k, z] for k in range(3)]
-        flux = contract(second, velocity)
-        even_sum = even[0] * f_even[0]
-        odd_sum = odd[0] * f_odd[0]
-        for n in range(1, 9):
-            even_sum = even_sum + even[n] * f_even[n]
-            odd_sum = odd_sum + odd[n] * f_odd[n]
-        relaxed = (
-            total * (1.0 - 1.5 * dot3(velocity, velocity))
-            + 3.0 * dot3(velocity, first)
-            + 4.5 * dot3(velocity, flux)
-        )
-        half = 0.5 * relax_rate
-        sensitivity = (
-            half * even_sum
-            + (half - 1.0) * odd_sum
-            + relax_rate * (popul[0] * pulled[0])
-            - (relax_rate / 36.0) * (density * relaxed)
-        )
-        term = sensitivity * mask[z].astype(jnp.float32)
-        column = term if column is None else column + term
-    column = column * (porous_max / (LEVELS - 1))
-    top = column.astype(jnp.bfloat16).astype(jnp.float32)
-    rest = column - top
-    owner = lax.div(index[...], chunk) if chunk & (chunk - 1) else index[...] >> (chunk.bit_length() - 1)
-    slot = index[...] - owner * chunk
-    owner_row = iota((owners, 128), 0)
-    slot_row = iota((chunk, 128), 0)
-    acc = None
-    for x in range(0, rows, 2):
-        lhs = []
-        rhs = []
-        for r in (x, x + 1):
-            hot = owner_row == owner[r : r + 1, :]
-            lhs.append(
-                jnp.concatenate(
-                    [
-                        jnp.where(hot, top[r : r + 1, :], 0.0).astype(jnp.bfloat16),
-                        jnp.where(hot, rest[r : r + 1, :], 0.0).astype(jnp.bfloat16),
-                    ],
-                    axis=0,
-                )
+            tile = joined(q, strip[q]) if step_num == 0 else state[q]
+            tile = turned(turned(tile, -shift_x, 0), Z_LANES * (shift_z % 2) - shift_y, 1)
+            own = tile[:rows]
+            pulls[q] = tile
+            summed[q] = own if step_num == 0 else summed[q] + own
+        for t in range((rows if final else full) // 8):
+            at = slice(8 * t, 8 * t + 8)
+            here = [field_state[k, at, :] for k in range(FIELDS)]
+            result = collide([pulls[q, at, :] for q in range(19)], here[:3], here[3], here[4])
+            for q in range(19):
+                state[q, at, :] = result[q]
+
+
+def sum_kernel(
+    owners, chunk, summed, field_strip, fwd_strip, mask_strip, line, grid_inside, after, grid
+):
+    rows = summed.shape[1]
+    column = sensitivity_of(
+        [summed[q] for q in range(19)],
+        [fwd_strip[q] for q in range(19)],
+        [field_strip[k, :rows, :] for k in range(3)],
+    ) * mask_strip[...]
+    column = (column + turned(column, Z_LANES, 1)) * (porous_max / (LEVELS - 1))
+    values = edge_line(turned(column, 3 - RIGHT, 1), turned(column, 3 - LEFT, 1))
+    owner, slot = split_index(line[0:1, :].astype(jnp.int32), chunk)
+    acc = hot_product(*hot_rows(values, owner, slot, owners, chunk))
+    grid[...] = grid_inside[...] + (acc[:owners] + acc[owners:])
+
+
+def merge_kernel(state, inside, out):
+    rows = inside.shape[2]
+    lane = iota((rows, 128), 1)
+    spot = lane & (Z_LANES - 1)
+    for q in range(19):
+        edge = state[q, :rows, :]
+        edge = jnp.where(spot < RIGHT, edge, turned(edge, RIGHT - LEFT, 1))
+        for z in range(2):
+            out[q, z] = jnp.where(
+                (lane >= 125) | (lane < 3), turned(edge, -RIGHT - z * Z_LANES, 1), inside[q, z]
             )
-            rhs.append(jnp.where(slot_row == slot[r : r + 1, :], 1.0, 0.0).astype(jnp.bfloat16))
-        part = lax.dot_general(
-            jnp.concatenate(lhs, axis=1),
-            jnp.concatenate(rhs, axis=1),
-            (((1,), (1,)), ((), ())),
-            preferred_element_type=jnp.float32,
-        )
-        acc = part if acc is None else acc + part
-    grid[...] = acc[:owners] + acc[owners:]
-
-
-def final_kernel(last, fields, out):
-    depth, rows = last.shape[1], last.shape[2]
-    for z in range(depth):
-        for t in range(rows // 8):
-            at = slice(8 * t, 8 * t + 8)
-            here = [fields[k, z, at, :] for k in range(FIELDS)]
-            result = collide([last[q, z, at, :] for q in range(19)], here[:3], here[3], here[4])
-            for q in range(19):
-                out[q, z, at, :] = result[q]
-
-
-def call(kernel, out_types, args, scratch=(), flops=0, where=pltpu.VMEM):
+
+
+def tail_kernel(received, out, adjoint_start, owned, block, sems):
+    copy_out = pltpu.make_async_copy(out, adjoint_start, sems.at[0])
+    copy_out.start()
+    total = jnp.sum(received[...], axis=0, keepdims=True)
+    cols = block.shape[1]
+    for r in range(block.shape[0]):
+        block[r : r + 1, :] = turned(total, -r * cols, 1)[:, :cols]
+    copy_owned = pltpu.make_async_copy(block, owned, sems.at[1])
+    copy_owned.start()
+    copy_owned.wait()
+    copy_out.wait()
+
+
+def call(kernel, out_types, args, scratch=(), flops=0, where=pltpu.VMEM, to=pltpu.VMEM):
     moved = sum(a.size * a.dtype.itemsize for a in args)
     return pl.pallas_call(
         kernel,
-        out_shape=[pltpu.VMEM(shape, dtype) for shape, dtype in out_types],
+        out_shape=[to(shape, dtype) for shape, dtype in out_types],
         in_specs=[pl.BlockSpec(memory_space=where)] * len(args),
-        out_specs=[pl.BlockSpec(memory_space=pltpu.VMEM)] * len(out_types),
+        out_specs=[pl.BlockSpec(memory_space=to)] * len(out_types),
         scratch_shapes=list(scratch),
         compiler_params=pltpu.CompilerParams(vmem_limit_bytes=16 << 20),
         cost_estimate=pl.CostEstimate(flops=flops, bytes_accessed=moved, transcendentals=0),
@@ -432,31 +517,55 @@
     )
     got_outer = lax.ppermute(outer, "gx", swap_pairs(gx_count, 1))
     got_inner = lax.ppermute(inner, "gx", swap_pairs(gx_count, 0))
-    inner, outer, adj_rim, field_rim = call(
+    flat = ((tile_x, 128), f32)
+    low_own, high_own, fwd_strip, mask_strip, line = call(
+        own_kernel,
+        [flat, flat, ((19, tile_x, 128), f32), flat, ((8, 128), f32)],
+        [adj, fields, fwd, mask, index],
+        flops=10**6,
+    )
+    outer, inner, adj_rim, field_rim = call(
         side_kernel,
         [
             ((full, 128), f32), ((full, 128), f32), ((19, depth, 8, tile_y), f32),
             ((FIELDS, depth, 8, tile_y), f32),
         ],
-        [adj, fields, got_outer, got_inner],
-    )
+        [got_outer, got_inner, low_own, high_own],
+    )
+    got_outer = lax.ppermute(outer, "gy", swap_pairs(gy_count, 1))
     got_inner = lax.ppermute(inner, "gy", swap_pairs(gy_count, 0))
-    got_outer = lax.ppermute(outer, "gy", swap_pairs(gy_count, 1))
-    grid, last = call(
-        lambda *refs: step_kernel(owners, chunk, *refs),
-        [((owners, chunk), f32), own],
-        [adj, adj_rim, fields, field_rim, got_inner, got_outer, fwd, mask, index],
-        [
-            wide, wide, wide, wide, pltpu.VMEM((FIELDS, depth, full, tile_y), f32),
-            pltpu.VMEM(*own),
-        ],
+    grid, inside, strip, field_strip = call(
+        lambda *refs: main_kernel(owners, chunk, *refs),
+        [((owners, chunk), f32), own, ((19, full, 128), f32), ((FIELDS, full, 128), f32)],
+        [adj, adj_rim, fields, field_rim, fwd, mask, index],
+        [wide, wide, pltpu.VMEM(*own)],
+        flops=10**6,
+    )
+    state, summed = call(
+        strip_kernel,
+        [((19, full, 128), f32), ((19, tile_x, 128), f32)],
+        [got_outer, got_inner, strip, field_strip],
+        [pltpu.VMEM((19, full, 128), f32), pltpu.VMEM((FIELDS, full, 128), f32)],
+    )
+    (out,) = call(merge_kernel, [own], [state, inside])
+    (grid,) = call(
+        lambda *refs: sum_kernel(owners, chunk, *refs),
+        [((owners, chunk), f32)],
+        [summed, field_strip, fwd_strip, mask_strip, line, grid, out],
     )
     received = lax.all_to_all(
         grid.reshape(owners, 1, chunk), BOTH, split_axis=0, concat_axis=0, tiled=True
     )
-    (adjoint_start,) = call(final_kernel, [own], [last, fields], flops=10**6)
-    owned = jnp.sum(received, axis=0).reshape(design_rows // owners, design_cols)
-    return (adjoint_start, owned)
+    block = ((design_rows // owners, design_cols), f32)
+    return tuple(
+        call(
+            tail_kernel,
+            [own, block],
+            [received.reshape(owners, chunk), out],
+            [pltpu.VMEM(*block), pltpu.SemaphoreType.DMA((2,))],
+            to=pltpu.HBM,
+        )
+    )
 
 
 def solution(mesh):

time: 31.8 us -> 29.6 us (0.931)
  blocking collectives: 0 us -> 12.7 us
  waiting for transfers between devices: 8.67 us -> 1.06 us
  starting transfers between devices: 17 us -> 10.2 us
  local copies, waits for them, and re-layouts: 1.38 us -> 0 us
  Pallas kernels: 3.74 us -> 4.82 us
    all_to_all x0 -> x1, blocking collectives: none -> 12.7 us  [per_device(): lax.all_to_all(grid.reshape(owners, 1, chunk), BOTH, split_axis=0, concat...]
    all_to_all x1 -> x0, starting transfers between devices: 9.72 us -> none  [per_device(): lax.all_to_all(grid.reshape(owners, 1, chunk), BOTH, split_axis=0, concat...]
    all_to_all x1 -> x0, waiting for transfers between devices: 6.32 us -> none  [per_device(): lax.all_to_all(grid.reshape(owners, 1, chunk), BOTH, split_axis=0, concat...]
    ppermute x1, starting transfers between devices: 1.64 us -> 4.46 us  [per_device(): got_inner = lax.ppermute(inner, 'gy', swap_pairs(gy_count, 0))]
    pallas_call x4 -> x8, Pallas kernels: 3.74 us -> 4.82 us  [call(): pl.pallas_call(kernel, out_shape=[to(shape, dtype) for shape, dtype in ou...]
    ppermute x1, waiting for transfers between devices: 1.46 us -> 0.59 us  [per_device(): got_inner = lax.ppermute(inner, 'gy', swap_pairs(gy_count, 0))]
    unnamed x1 -> x0, local copies, waits for them, and re-layouts: 0.72 us -> none
    reshape x1 -> x0, local copies, waits for them, and re-layouts: 0.66 us -> none  [per_device(): jnp.sum(received, axis=0).reshape(design_rows // owners, design_cols)]
  transfers between devices with their start and end apart: 5 -> 4, of which waited for: 3 -> 2; matrix products, arithmetic and copies ran while one was open for 2% -> 0% of each run, Pallas kernels for 0% -> 5%
where the time goes in v3:
time: 29.6 us; the launch traced here: 29.4 us
  blocking collectives  12.7 us (43%)
  starting transfers between devices  10.2 us (34%)
  Pallas kernels  4.82 us (16%)
  waiting for transfers between devices  1.06 us (4%)
  between operations  0.69 us (2%)
    all_to_all x1, blocking collectives, per_device(): lax.all_to_all(grid.reshape(owners, 1, chunk), BOTH, split_axis=0, concat...  12.7 us
    pallas_call x8, Pallas kernels, call(): pl.pallas_call(kernel, out_shape=[to(shape, dtype) for shape, dtype in ou...  4.82 us
    ppermute x1, starting transfers between devices, per_device(): got_inner = lax.ppermute(inner, 'gy', swap_pairs(gy_count, 0))  4.46 us
    ppermute x1, starting transfers between devices, per_device(): got_inner = lax.ppermute(inner, 'gx', swap_pairs(gx_count, 0))  4.36 us
    ppermute x1, starting transfers between devices, per_device(): got_outer = lax.ppermute(outer, 'gx', swap_pairs(gx_count, 1))  0.66 us
    ppermute x1, starting transfers between devices, per_device(): got_outer = lax.ppermute(outer, 'gy', swap_pairs(gy_count, 1))  0.66 us
  transfers between devices with their start and end apart: 4, of which 2 were waited for; matrix products, arithmetic and copies ran while one was open for 0% of the time, Pallas kernels for 5%

profile of v3, /device:TPU:0, one launch (start us, length us, event | category | flops | bytes accessed | tf_op | source)
XLA Modules:
  0.0 29.4 jit_solution(15857139633702020403)
XLA Ops:
  0.6 1.2 %shard_map.68 = (f32[12,8,128]{2,1,0:T(8,128)S(1)}, f32[12,8,128]{2,1,0:T(8,128)S(1)}, f32[5,2,16,128]{3,2,1,0:T(8,128)S(1)}, f32[19,2,16,128]{3,2,1,0:T(8,128)S...) custom-call(f32[19,2,16,128]{3,2,1,0:T(8,128)} %adj_hbm.1, ...), custom_call_target="tpu_custom_call" | custom-call | bytes 507904 | tf_op jit(solution)/shard_map/pallas_call | solution.py:480
  1.8 0.7 %collective-permute-start = (f32[12,8,128]{2,1,0:T(8,128)S(1)}, f32[12,8,128]{2,1,0:T(8,128)S(1)}, u32[]{:S(2)}, u32[]{:S(2)}) collective-permute-start(f32[12,8,128]{2,1,0:T(8,128)S(1)} %get-tuple-element.24), channel_id=1, source_target_pairs={{4,8},{8,4},{12,16},{16,12},{20,24},{24,20},{5,9},{9,5},{13,17},{1... | collective-permute-start | bytes 147464 | tf_op jit(solution)/shard_map/ppermute | solution.py:518
  2.5 4.4 %collective-permute-start.1 = (f32[12,8,128]{2,1,0:T(8,128)S(1)}, f32[12,8,128]{2,1,0:T(8,128)S(1)}, u32[]{:S(2)}, u32[]{:S(2)}) collective-permute-start(f32[12,8,128]{2,1,0:T(8,128)S(1)} %get-tuple-element.25), channel_id=1, source_target_pairs={{0,4},{4,0},{8,12},{12,8},{16,20},{20,16},{24,28},{28,24},{1,5},{5... | collective-permute-start | bytes 147464 | tf_op jit(solution)/shard_map/ppermute | solution.py:519
  6.8 0.4 %shard_map.69 = (f32[16,128]{1,0:T(8,128)S(1)}, f32[16,128]{1,0:T(8,128)S(1)}, f32[19,16,128]{2,1,0:T(8,128)S(1)}, f32[16,128]{1,0:T(8,128)S(1)}, f32[8,128]{1,0:T(8,128)S(1)}) custom-call(f32[19,2,16,128]{3,2,1,0:T(8,128)S(1)} %get-tuple-element.26.adj.refs_0_, f32[5,2,16,128]{3,2,1,0:T(8,128)S(1)} %get-tuple-element.27.fields.refs_2_, ...), custom_call_target="tpu_custom_call" | custom-call | flops 1000000 | bytes 573440 | tf_op jit(solution)/shard_map/pallas_call | solution.py:480
  7.2 0.0 collective-permute-done.got_outer
  7.3 0.5 %collective-permute-done.1.got_inner = f32[12,8,128]{2,1,0:T(8,128)S(1)} collective-permute-done((f32[12,8,128]{2,1,0:T(8,128)S(1)}, f32[12,8,128]{2,1,0:T(8,128)S(1)}, u32[]{:S(2)}, u32[]{:S(2)}) %collective-permute-start.1) | collective-permute-done | bytes 49184 | tf_op jit(solution)/shard_map/ppermute | solution.py:519
  7.7 0.2 shard_map.70
  7.9 0.7 %collective-permute-start.2 = (f32[24,128]{1,0:T(8,128)S(1)}, f32[24,128]{1,0:T(8,128)S(1)}, u32[]{:S(2)}, u32[]{:S(2)}) collective-permute-start(f32[24,128]{1,0:T(8,128)S(1)} %get-tuple-element.33), channel_id=1, source_target_pairs={{1,2},{2,1},{5,6},{6,5},{9,10},{10,9},{13,14},{14,13},{17,18},{18,... | collective-permute-start | bytes 36872 | tf_op jit(solution)/shard_map/ppermute | solution.py:535
  8.6 4.5 %collective-permute-start.3 = (f32[24,128]{1,0:T(8,128)S(1)}, f32[24,128]{1,0:T(8,128)S(1)}, u32[]{:S(2)}, u32[]{:S(2)}) collective-permute-start(f32[24,128]{1,0:T(8,128)S(1)} %get-tuple-element.34), channel_id=1, source_target_pairs={{0,1},{1,0},{2,3},{3,2},{4,5},{5,4},{6,7},{7,6},{8,9},{9,8},{10,11... | collective-permute-start | bytes 36872 | tf_op jit(solution)/shard_map/ppermute | solution.py:536
  13.0 1.1 %shard_map.71 = (f32[32,128]{1,0:T(8,128)S(1)}, f32[19,2,16,128]{3,2,1,0:T(8,128)S(1)}, f32[19,24,128]{2,1,0:T(8,128)S(1)}, f32[5,24,128]{2,1,0:T(8,128)S(1)}) custom-call(f32[19,2,16,128]{3,2,1,0:T(8,128)S(1)} %get-tuple-element.26.adj.refs_0_, f32[19,2,8,128]{3,2,1,0:T(8,128)S(1)} %get-tuple-element.35.refs_1_, ...), custom_call_target="tpu_custom_call" | custom-call | flops 1000000 | bytes 770048 | tf_op jit(solution)/shard_map/pallas_call | solution.py:480
  14.1 0.0 collective-permute-done.2.got_outer
  14.1 0.6 %collective-permute-done.3.got_inner = f32[24,128]{1,0:T(8,128)S(1)} collective-permute-done((f32[24,128]{1,0:T(8,128)S(1)}, f32[24,128]{1,0:T(8,128)S(1)}, u32[]{:S(2)}, u32[]{:S(2)}) %collective-permute-start.3) | collective-permute-done | bytes 12320 | tf_op jit(solution)/shard_map/ppermute | solution.py:536
  14.7 0.7 %shard_map.72 = (f32[19,24,128]{2,1,0:T(8,128)S(1)}, f32[19,16,128]{2,1,0:T(8,128)S(1)}) custom-call(f32[24,128]{1,0:T(8,128)S(1)} %collective-permute-done.2.got_outer, f32[24,128]{1,0:T(8,128)S(1)} %collective-permute-done.3.got_inner, f32[19,24,128]{2,1,0:T(8,128)S(1)} %get-tuple-element.37.strip, f32[5,24,128]{2,1,0:T(8,128)S(1)} %get-tuple-element.38.field_strip.refs_1_), custom_call_target="tpu_custom_call" | custom-call | bytes 319488 | tf_op jit(solution)/shard_map/pallas_call | solution.py:480
  15.4 0.2 shard_map.73.refs_6_.out
  15.6 0.4 %shard_map.74 = f32[32,128]{1,0:T(8,128)S(1)} custom-call(f32[19,16,128]{2,1,0:T(8,128)S(1)} %get-tuple-element.39.refs_0_, f32[5,24,128]{2,1,0:T(8,128)S(1)} %get-tuple-element.38.field_strip.refs_1_, f32[19,16,128]{2,1,0:T(8,128)S(1)} %get-tuple-element.40.refs_2_, f32[16,128]{1,0:T(8,128)S(1)} %get-tuple-element.41.refs_3_, ...), custom_call_target="tpu_custom_call" | custom-call | bytes 712704 | tf_op jit(solution)/shard_map/pallas_call | solution.py:480
  16.0 12.7 %all_to_all.5 = f32[32,1,128]{2,1,0:T(1,128)S(1)} all-to-all(f32[32,1,128]{2,1,0:T(1,128)S(1)} %bitcast.4), channel_id=1, replica_groups=mesh['gx'=8,'gy'=4] {'gx','gy'}, dimensions={0} | all-to-all | bytes 32768 | tf_op jit(solution)/shard_map/all_to_all | solution.py:556
  28.7 0.7 %shard_map.75 = (f32[19,2,16,128]{3,2,1,0:T(8,128)}, f32[4,32]{1,0:T(4,128)}) custom-call(f32[32,128]{1,0:T(8,128)S(1)} %bitcast.5, f32[19,2,16,128]{3,2,1,0:T(8,128)S(1)} %shard_map.73.refs_6_.out), custom_call_target="tpu_custom_call" | custom-call | bytes 327680 | tf_op jit(solution)/shard_map/pallas_call | solution.py:480
Async XLA Ops:
  1.8 5.4 %collective-permute-start = (f32[12,8,128]{2,1,0:T(8,128)S(1)}, f32[12,8,128]{2,1,0:T(8,128)S(1)}, u32[]{:S(2)}, u32[]{:S(2)}) collective-permute-start(f32[12,8,128]{2,1,0:T(8,128)S(1)} %get-tuple-element.24), channel_id=1, source_target_pairs={{4,8},{8,4},{12,16},{16,12},{20,24},{24,20},{5,9},{9,5},{13,17},{1... | collective-permute-start | bytes 147464 | tf_op jit(solution)/shard_map/ppermute | solution.py:518
  2.5 5.2 %collective-permute-start.1 = (f32[12,8,128]{2,1,0:T(8,128)S(1)}, f32[12,8,128]{2,1,0:T(8,128)S(1)}, u32[]{:S(2)}, u32[]{:S(2)}) collective-permute-start(f32[12,8,128]{2,1,0:T(8,128)S(1)} %get-tuple-element.25), channel_id=1, source_target_pairs={{0,4},{4,0},{8,12},{12,8},{16,20},{20,16},{24,28},{28,24},{1,5},{5... | collective-permute-start | bytes 147464 | tf_op jit(solution)/shard_map/ppermute | solution.py:519
  7.9 6.2 %collective-permute-start.2 = (f32[24,128]{1,0:T(8,128)S(1)}, f32[24,128]{1,0:T(8,128)S(1)}, u32[]{:S(2)}, u32[]{:S(2)}) collective-permute-start(f32[24,128]{1,0:T(8,128)S(1)} %get-tuple-element.33), channel_id=1, source_target_pairs={{1,2},{2,1},{5,6},{6,5},{9,10},{10,9},{13,14},{14,13},{17,18},{18,... | collective-permute-start | bytes 36872 | tf_op jit(solution)/shard_map/ppermute | solution.py:535
  8.6 6.1 %collective-permute-start.3 = (f32[24,128]{1,0:T(8,128)S(1)}, f32[24,128]{1,0:T(8,128)S(1)}, u32[]{:S(2)}, u32[]{:S(2)}) collective-permute-start(f32[24,128]{1,0:T(8,128)S(1)} %get-tuple-element.34), channel_id=1, source_target_pairs={{0,1},{1,0},{2,3},{3,2},{4,5},{5,4},{6,7},{7,6},{8,9},{9,8},{10,11... | collective-permute-start | bytes 36872 | tf_op jit(solution)/shard_map/ppermute | solution.py:536

commit v4 on v3

--- a/solution.py
+++ b/solution.py
@@ -34,9 +34,13 @@
 SPEEDS = lattice_table()
 PAIRS = ((1, 2), (3, 4), (5, 6), (7, 10), (8, 9), (11, 14), (12, 13), (15, 18), (16, 17))
 
+Z_LANES = 64
 WIDTHS = [3 if SPEEDS[q][1] != 0 else 2 for q in range(19)] + [2] * FIELDS
-STARTS = [sum(WIDTHS[:n]) for n in range(19 + FIELDS)]
-Z_LANES = 64
+DEEP = [n for n in range(19) if WIDTHS[n] == 3]
+THIN = [n for n in range(19 + FIELDS) if WIDTHS[n] == 2]
+STARTS = [
+    3 * DEEP.index(n) if n in DEEP else Z_LANES // 2 + 2 * THIN.index(n) for n in range(19 + FIELDS)
+]
 
 
 def swap_pairs(count, parity):
@@ -203,7 +207,7 @@
 
 
 RIGHT = 16
-LEFT = 43
+LEFT = 51
 
 
 def strip_of(pair):
@@ -218,7 +222,7 @@
 def pack_sides(tiles):
     low = high = None
     for z in range(2):
-        for n in range(19 + FIELDS):
+        for n in DEEP + THIN:
             at = z * Z_LANES + STARTS[n]
             tile = tiles(n, z)
             up = turned(tile, at, 1)
@@ -347,14 +351,17 @@
             shift_x, shift_y, shift_z = SPEEDS[q]
             if step_num == 0:
                 start = [jnp.concatenate([adj[q, z], adj_rim[q, z]], axis=0) for z in range(2)]
-                strip[q] = strip_of(start)
+            both = []
             for z in range(2):
                 src = (z + shift_z) % 2
                 main = start[src] if step_num == 0 else state[q, src]
                 main = turned(turned(main, -shift_x, 0), -shift_y, 1)
                 pulls[q, z] = main
+                both.append(main)
                 own = main[:rows]
                 summed[q, z] = own if step_num == 0 else summed[q, z] + own
+            if step_num == 0:
+                strip[q] = strip_of(both)
         for z in range(2):
             for t in range((rows if final else full) // 8):
                 at = slice(8 * t, 8 * t + 8)
@@ -396,7 +403,8 @@
 
 
 def strip_kernel(
-    got_outer, got_inner, strip, field_strip, state, summed, pulls, field_state,
+    got_outer, got_inner, strip, field_strip, fwd_strip, mask_strip, inside,
+    column, out, state, summed, pulls, field_state,
 ):
     full = strip.shape[1]
     rows = full - 8
@@ -406,13 +414,22 @@
     low = jnp.where(even_y, from_out, from_in)
     high = jnp.where(even_y, from_in, from_out)
     lane = iota((full, 128), 1) & (Z_LANES - 1)
-    at_right = (lane >= RIGHT) & (lane < RIGHT + 3)
-    at_left = (lane >= LEFT - 3) & (lane < LEFT)
-
-    def joined(n, own):
-        right = turned(high, RIGHT - STARTS[n], 1)
-        left = turned(low, LEFT - WIDTHS[n] - STARTS[n], 1)
-        return jnp.where(at_left, left, jnp.where(at_right, right, own))
+    half = Z_LANES // 2
+    deep = jnp.where(lane < half, high, turned(low, LEFT - 3 - RIGHT, 1))
+    thin = jnp.where(lane >= half, high, turned(low, LEFT - 2 - RIGHT, 1))
+    moved = {
+        (width, shift): turned(both, -shift, 0)
+        for width, both in ((3, deep), (2, thin))
+        for shift in (-1, 0, 1)
+    }
+
+    def joined(n, own, shift_x=0, shift_y=0, shift_z=0):
+        width = WIDTHS[n]
+        turn = RIGHT - STARTS[n] - shift_y + Z_LANES * (shift_z % 2)
+        right = RIGHT - shift_y
+        left = LEFT - width - shift_y
+        inside = ((lane >= right) & (lane < right + width)) | ((lane >= left) & (lane < left + width))
+        return jnp.where(inside, turned(moved[width, shift_x], turn, 1), own)
 
     for k in range(FIELDS):
         field_state[k] = joined(19 + k, field_strip[k])
@@ -420,8 +437,11 @@
         final = step_num == STEPS - 1
         for q in range(19):
             shift_x, shift_y, shift_z = SPEEDS[q]
-            tile = joined(q, strip[q]) if step_num == 0 else state[q]
-            tile = turned(turned(tile, -shift_x, 0), Z_LANES * (shift_z % 2) - shift_y, 1)
+            if step_num == 0:
+                tile = joined(q, strip[q], shift_x, shift_y, shift_z)
+            else:
+                tile = turned(state[q], -shift_x, 0)
+                tile = turned(tile, Z_LANES * (shift_z % 2) - shift_y, 1)
             own = tile[:rows]
             pulls[q] = tile
             summed[q] = own if step_num == 0 else summed[q] + own
@@ -431,35 +451,30 @@
             result = collide([pulls[q, at, :] for q in range(19)], here[:3], here[3], here[4])
             for q in range(19):
                 state[q, at, :] = result[q]
-
-
-def sum_kernel(
-    owners, chunk, summed, field_strip, fwd_strip, mask_strip, line, grid_inside, after, grid
-):
-    rows = summed.shape[1]
-    column = sensitivity_of(
+    term = sensitivity_of(
         [summed[q] for q in range(19)],
         [fwd_strip[q] for q in range(19)],
         [field_strip[k, :rows, :] for k in range(3)],
     ) * mask_strip[...]
-    column = (column + turned(column, Z_LANES, 1)) * (porous_max / (LEVELS - 1))
-    values = edge_line(turned(column, 3 - RIGHT, 1), turned(column, 3 - LEFT, 1))
-    owner, slot = split_index(line[0:1, :].astype(jnp.int32), chunk)
-    acc = hot_product(*hot_rows(values, owner, slot, owners, chunk))
-    grid[...] = grid_inside[...] + (acc[:owners] + acc[owners:])
-
-
-def merge_kernel(state, inside, out):
-    rows = inside.shape[2]
-    lane = iota((rows, 128), 1)
-    spot = lane & (Z_LANES - 1)
+    column[...] = (term + turned(term, Z_LANES, 1)) * (porous_max / (LEVELS - 1))
+    own_lane = iota((rows, 128), 1)
+    spot = own_lane & (Z_LANES - 1)
     for q in range(19):
         edge = state[q, :rows, :]
         edge = jnp.where(spot < RIGHT, edge, turned(edge, RIGHT - LEFT, 1))
         for z in range(2):
             out[q, z] = jnp.where(
-                (lane >= 125) | (lane < 3), turned(edge, -RIGHT - z * Z_LANES, 1), inside[q, z]
+                (own_lane >= 125) | (own_lane < 3),
+                turned(edge, -RIGHT - z * Z_LANES, 1),
+                inside[q, z],
             )
+
+
+def sum_kernel(owners, chunk, column, line, grid_inside, after, grid):
+    values = edge_line(turned(column[...], 3 - RIGHT, 1), turned(column[...], 3 - LEFT, 1))
+    owner, slot = split_index(line[0:1, :].astype(jnp.int32), chunk)
+    acc = hot_product(*hot_rows(values, owner, slot, owners, chunk))
+    grid[...] = grid_inside[...] + (acc[:owners] + acc[owners:])
 
 
 def tail_kernel(received, out, adjoint_start, owned, block, sems):
@@ -541,17 +556,19 @@
         [wide, wide, pltpu.VMEM(*own)],
         flops=10**6,
     )
-    state, summed = call(
+    column, out = call(
         strip_kernel,
-        [((19, full, 128), f32), ((19, tile_x, 128), f32)],
-        [got_outer, got_inner, strip, field_strip],
-        [pltpu.VMEM((19, full, 128), f32), pltpu.VMEM((FIELDS, full, 128), f32)],
-    )
-    (out,) = call(merge_kernel, [own], [state, inside])
+        [flat, own],
+        [got_outer, got_inner, strip, field_strip, fwd_strip, mask_strip, inside],
+        [
+            pltpu.VMEM((19, full, 128), f32), pltpu.VMEM((19, tile_x, 128), f32),
+            pltpu.VMEM((19, full, 128), f32), pltpu.VMEM((FIELDS, full, 128), f32),
+        ],
+    )
     (grid,) = call(
         lambda *refs: sum_kernel(owners, chunk, *refs),
         [((owners, chunk), f32)],
-        [summed, field_strip, fwd_strip, mask_strip, line, grid, out],
+        [column, line, grid, out],
     )
     received = lax.all_to_all(
         grid.reshape(owners, 1, chunk), BOTH, split_axis=0, concat_axis=0, tiled=True

time: 29.6 us -> 29.3 us (0.990)
    pallas_call x8 -> x7, Pallas kernels: 4.82 us -> 4.6 us  [call(): pl.pallas_call(kernel, out_shape=[to(shape, dtype) for shape, dtype in ou...]
where the time goes in v4:
time: 29.3 us; the launch traced here: 29.1 us
  blocking collectives  12.7 us (43%)
  starting transfers between devices  10.2 us (35%)
  Pallas kernels  4.6 us (16%)
  waiting for transfers between devices  0.99 us (3%)
  between operations  0.69 us (2%)
    all_to_all x1, blocking collectives, per_device(): lax.all_to_all(grid.reshape(owners, 1, chunk), BOTH, split_axis=0, concat...  12.7 us
    pallas_call x7, Pallas kernels, call(): pl.pallas_call(kernel, out_shape=[to(shape, dtype) for shape, dtype in ou...  4.6 us
    ppermute x1, starting transfers between devices, per_device(): got_inner = lax.ppermute(inner, 'gy', swap_pairs(gy_count, 0))  4.46 us
    ppermute x1, starting transfers between devices, per_device(): got_inner = lax.ppermute(inner, 'gx', swap_pairs(gx_count, 0))  4.36 us
    ppermute x1, starting transfers between devices, per_device(): got_outer = lax.ppermute(outer, 'gx', swap_pairs(gx_count, 1))  0.66 us
    ppermute x1, starting transfers between devices, per_device(): got_outer = lax.ppermute(outer, 'gy', swap_pairs(gy_count, 1))  0.66 us
  transfers between devices with their start and end apart: 4, of which 2 were waited for; matrix products, arithmetic and copies ran while one was open for 0% of the time, Pallas kernels for 5%

profile of v4, /device:TPU:0, one launch (start us, length us, event | category | flops | bytes accessed | tf_op | source)
XLA Modules:
  0.0 29.1 jit_solution(10562536893559583472)
XLA Ops:
  0.6 1.2 %shard_map.68 = (f32[12,8,128]{2,1,0:T(8,128)S(1)}, f32[12,8,128]{2,1,0:T(8,128)S(1)}, f32[5,2,16,128]{3,2,1,0:T(8,128)S(1)}, f32[19,2,16,128]{3,2,1,0:T(8,128)S...) custom-call(f32[19,2,16,128]{3,2,1,0:T(8,128)} %adj_hbm.1, ...), custom_call_target="tpu_custom_call" | custom-call | bytes 507904 | tf_op jit(solution)/shard_map/pallas_call | solution.py:495
  1.8 0.7 %collective-permute-start = (f32[12,8,128]{2,1,0:T(8,128)S(1)}, f32[12,8,128]{2,1,0:T(8,128)S(1)}, u32[]{:S(2)}, u32[]{:S(2)}) collective-permute-start(f32[12,8,128]{2,1,0:T(8,128)S(1)} %get-tuple-element.24), channel_id=1, source_target_pairs={{4,8},{8,4},{12,16},{16,12},{20,24},{24,20},{5,9},{9,5},{13,17},{1... | collective-permute-start | bytes 147464 | tf_op jit(solution)/shard_map/ppermute | solution.py:533
  2.5 4.4 %collective-permute-start.1 = (f32[12,8,128]{2,1,0:T(8,128)S(1)}, f32[12,8,128]{2,1,0:T(8,128)S(1)}, u32[]{:S(2)}, u32[]{:S(2)}) collective-permute-start(f32[12,8,128]{2,1,0:T(8,128)S(1)} %get-tuple-element.25), channel_id=1, source_target_pairs={{0,4},{4,0},{8,12},{12,8},{16,20},{20,16},{24,28},{28,24},{1,5},{5... | collective-permute-start | bytes 147464 | tf_op jit(solution)/shard_map/ppermute | solution.py:534
  6.8 0.4 %shard_map.69 = (f32[16,128]{1,0:T(8,128)S(1)}, f32[16,128]{1,0:T(8,128)S(1)}, f32[19,16,128]{2,1,0:T(8,128)S(1)}, f32[16,128]{1,0:T(8,128)S(1)}, f32[8,128]{1,0:T(8,128)S(1)}) custom-call(f32[19,2,16,128]{3,2,1,0:T(8,128)S(1)} %get-tuple-element.26.adj.refs_0_, f32[5,2,16,128]{3,2,1,0:T(8,128)S(1)} %get-tuple-element.27.fields.refs_2_, ...), custom_call_target="tpu_custom_call" | custom-call | flops 1000000 | bytes 573440 | tf_op jit(solution)/shard_map/pallas_call | solution.py:495
  7.2 0.0 collective-permute-done.got_outer
  7.3 0.5 %collective-permute-done.1.got_inner = f32[12,8,128]{2,1,0:T(8,128)S(1)} collective-permute-done((f32[12,8,128]{2,1,0:T(8,128)S(1)}, f32[12,8,128]{2,1,0:T(8,128)S(1)}, u32[]{:S(2)}, u32[]{:S(2)}) %collective-permute-start.1) | collective-permute-done | bytes 49184 | tf_op jit(solution)/shard_map/ppermute | solution.py:534
  7.7 0.2 shard_map.70
  7.9 0.7 %collective-permute-start.2 = (f32[24,128]{1,0:T(8,128)S(1)}, f32[24,128]{1,0:T(8,128)S(1)}, u32[]{:S(2)}, u32[]{:S(2)}) collective-permute-start(f32[24,128]{1,0:T(8,128)S(1)} %get-tuple-element.33), channel_id=1, source_target_pairs={{1,2},{2,1},{5,6},{6,5},{9,10},{10,9},{13,14},{14,13},{17,18},{18,... | collective-permute-start | bytes 36872 | tf_op jit(solution)/shard_map/ppermute | solution.py:550
  8.6 4.5 %collective-permute-start.3 = (f32[24,128]{1,0:T(8,128)S(1)}, f32[24,128]{1,0:T(8,128)S(1)}, u32[]{:S(2)}, u32[]{:S(2)}) collective-permute-start(f32[24,128]{1,0:T(8,128)S(1)} %get-tuple-element.34), channel_id=1, source_target_pairs={{0,1},{1,0},{2,3},{3,2},{4,5},{5,4},{6,7},{7,6},{8,9},{9,8},{10,11... | collective-permute-start | bytes 36872 | tf_op jit(solution)/shard_map/ppermute | solution.py:551
  13.0 1.1 %shard_map.71 = (f32[32,128]{1,0:T(8,128)S(1)}, f32[19,2,16,128]{3,2,1,0:T(8,128)S(1)}, f32[19,24,128]{2,1,0:T(8,128)S(1)}, f32[5,24,128]{2,1,0:T(8,128)S(1)}) custom-call(f32[19,2,16,128]{3,2,1,0:T(8,128)S(1)} %get-tuple-element.26.adj.refs_0_, f32[19,2,8,128]{3,2,1,0:T(8,128)S(1)} %get-tuple-element.35.refs_1_, ...), custom_call_target="tpu_custom_call" | custom-call | flops 1000000 | bytes 770048 | tf_op jit(solution)/shard_map/pallas_call | solution.py:495
  14.2 0.0 collective-permute-done.2.got_outer
  14.2 0.5 %collective-permute-done.3.got_inner = f32[24,128]{1,0:T(8,128)S(1)} collective-permute-done((f32[24,128]{1,0:T(8,128)S(1)}, f32[24,128]{1,0:T(8,128)S(1)}, u32[]{:S(2)}, u32[]{:S(2)}) %collective-permute-start.3) | collective-permute-done | bytes 12320 | tf_op jit(solution)/shard_map/ppermute | solution.py:551
  14.7 0.7 %shard_map.72 = (f32[16,128]{1,0:T(8,128)S(1)}, f32[19,2,16,128]{3,2,1,0:T(8,128)S(1)}) custom-call(f32[24,128]{1,0:T(8,128)S(1)} %collective-permute-done.2.got_outer, f32[24,128]{1,0:T(8,128)S(1)} %collective-permute-done.3.got_inner, f32[19,24,128]{2,1,0:T(8,128)S(1)} %get-tuple-element.37.strip, f32[5,24,128]{2,1,0:T(8,128)S(1)} %get-tuple-element.38.field_strip, ...), custom_call_target="tpu_custom_call" | custom-call | bytes 794624 | tf_op jit(solution)/shard_map/pallas_call | solution.py:495
  15.5 0.2 shard_map.73
  15.7 12.7 %all_to_all.5 = f32[32,1,128]{2,1,0:T(1,128)S(1)} all-to-all(f32[32,1,128]{2,1,0:T(1,128)S(1)} %bitcast.5), channel_id=1, replica_groups=mesh['gx'=8,'gy'=4] {'gx','gy'}, dimensions={0} | all-to-all | bytes 32768 | tf_op jit(solution)/shard_map/all_to_all | solution.py:573
  28.4 0.7 %shard_map.74 = (f32[19,2,16,128]{3,2,1,0:T(8,128)}, f32[4,32]{1,0:T(4,128)}) custom-call(f32[32,128]{1,0:T(8,128)S(1)} %bitcast.4, f32[19,2,16,128]{3,2,1,0:T(8,128)S(1)} %get-tuple-element.45.refs_3_.out), custom_call_target="tpu_custom_call" | custom-call | bytes 327680 | tf_op jit(solution)/shard_map/pallas_call | solution.py:495
Async XLA Ops:
  1.8 5.4 %collective-permute-start = (f32[12,8,128]{2,1,0:T(8,128)S(1)}, f32[12,8,128]{2,1,0:T(8,128)S(1)}, u32[]{:S(2)}, u32[]{:S(2)}) collective-permute-start(f32[12,8,128]{2,1,0:T(8,128)S(1)} %get-tuple-element.24), channel_id=1, source_target_pairs={{4,8},{8,4},{12,16},{16,12},{20,24},{24,20},{5,9},{9,5},{13,17},{1... | collective-permute-start | bytes 147464 | tf_op jit(solution)/shard_map/ppermute | solution.py:533
  2.5 5.2 %collective-permute-start.1 = (f32[12,8,128]{2,1,0:T(8,128)S(1)}, f32[12,8,128]{2,1,0:T(8,128)S(1)}, u32[]{:S(2)}, u32[]{:S(2)}) collective-permute-start(f32[12,8,128]{2,1,0:T(8,128)S(1)} %get-tuple-element.25), channel_id=1, source_target_pairs={{0,4},{4,0},{8,12},{12,8},{16,20},{20,16},{24,28},{28,24},{1,5},{5... | collective-permute-start | bytes 147464 | tf_op jit(solution)/shard_map/ppermute | solution.py:534
  7.9 6.3 %collective-permute-start.2 = (f32[24,128]{1,0:T(8,128)S(1)}, f32[24,128]{1,0:T(8,128)S(1)}, u32[]{:S(2)}, u32[]{:S(2)}) collective-permute-start(f32[24,128]{1,0:T(8,128)S(1)} %get-tuple-element.33), channel_id=1, source_target_pairs={{1,2},{2,1},{5,6},{6,5},{9,10},{10,9},{13,14},{14,13},{17,18},{18,... | collective-permute-start | bytes 36872 | tf_op jit(solution)/shard_map/ppermute | solution.py:550
  8.6 6.1 %collective-permute-start.3 = (f32[24,128]{1,0:T(8,128)S(1)}, f32[24,128]{1,0:T(8,128)S(1)}, u32[]{:S(2)}, u32[]{:S(2)}) collective-permute-start(f32[24,128]{1,0:T(8,128)S(1)} %get-tuple-element.34), channel_id=1, source_target_pairs={{0,1},{1,0},{2,3},{3,2},{4,5},{5,4},{6,7},{7,6},{8,9},{9,8},{10,11... | collective-permute-start | bytes 36872 | tf_op jit(solution)/shard_map/ppermute | solution.py:551

commit v5 on v4

--- a/solution.py
+++ b/solution.py
@@ -137,73 +137,83 @@
     return tile if shift == 0 else pltpu.roll(tile, shift, axis)
 
 
+def flow_fields(popul, level, mask):
+    even, odd = split_pairs(popul)
+    density = popul[0]
+    for n in range(9):
+        density = density + even[n]
+    o_x, o_y, o_z, o_xy, o_xw, o_xz, o_xv, o_yz, o_yv = odd
+    per_mass = 1.0 / density
+    porosity = jnp.where(mask == 1, level.astype(jnp.float32) * (porous_max / (LEVELS - 1)), 1.0)
+    return (
+        (o_x + ((o_xy + o_xw) + (o_xz + o_xv))) * per_mass,
+        (o_y + ((o_xy - o_xw) + (o_yz + o_yv))) * per_mass,
+        (o_z + ((o_xz - o_xv) + (o_yz - o_yv))) * per_mass,
+        1.0 - porosity,
+        porosity,
+    )
+
+
 def edge_kernel(
-    adj_hbm, fwd_hbm, level_hbm, mask_hbm, index_hbm,
-    outer, inner, fields, adj, fwd, mask, index, level, sems,
+    adj_hbm, fwd_hbm, level_hbm, mask_hbm, outer, inner, adj, fwd_top, fwd_end, level, mask,
+    fields, sems,
 ):
+    rows = adj_hbm.shape[2]
     copies = [
         pltpu.make_async_copy(src, dst, sems.at[n])
         for n, (src, dst) in enumerate(
             (
-                (fwd_hbm, fwd), (mask_hbm, mask), (level_hbm, level),
-                (adj_hbm, adj), (index_hbm, index),
+                (fwd_hbm.at[:, :, pl.ds(0, 2), :], fwd_top),
+                (fwd_hbm.at[:, :, pl.ds(rows - 2, 2), :], fwd_end),
+                (mask_hbm, mask),
+                (level_hbm, level),
+                (adj_hbm.at[:, :, pl.ds(0, 3), :], adj.at[:, :, pl.ds(0, 3), :]),
+                (adj_hbm.at[:, :, pl.ds(rows - 3, 3), :], adj.at[:, :, pl.ds(5, 3), :]),
             )
         )
     ]
     for copy in copies:
         copy.start()
-    for copy in copies[:3]:
+    for copy in copies[:4]:
         copy.wait()
-    depth, rows = adj.shape[1], adj.shape[2]
-    for z in range(depth):
-        popul = [fwd[q, z].astype(jnp.float32) for q in range(19)]
-        even, odd = split_pairs(popul)
-        density = popul[0]
-        for n in range(9):
-            density = density + even[n]
-        o_x, o_y, o_z, o_xy, o_xw, o_xz, o_xv, o_yz, o_yv = odd
-        per_mass = 1.0 / density
-        fields[0, z] = (o_x + ((o_xy + o_xw) + (o_xz + o_xv))) * per_mass
-        fields[1, z] = (o_y + ((o_xy - o_xw) + (o_yz + o_yv))) * per_mass
-        fields[2, z] = (o_z + ((o_xz - o_xv) + (o_yz - o_yv))) * per_mass
-        porosity = jnp.where(
-            mask[z] == 1, level[z].astype(jnp.float32) * (porous_max / (LEVELS - 1)), 1.0
-        )
-        fields[3, z] = 1.0 - porosity
-        fields[4, z] = porosity
-    copies[3].wait()
+    for z in range(2):
+        for fwd, at, to in ((fwd_top, 0, 0), (fwd_end, rows - 2, 6)):
+            values = flow_fields(
+                [fwd[q, z].astype(jnp.float32) for q in range(19)],
+                level[z, at : at + 2, :],
+                mask[z, at : at + 2, :],
+            )
+            for k in range(FIELDS):
+                fields[k, z, to : to + 2, :] = values[k]
+    for copy in copies[4:]:
+        copy.wait()
     even_x = is_even("gx")
     row = iota((8, 128), 0)
 
-    def top(n, z):
-        return adj[n, z, 0:8, :] if n < 19 else fields[n - 19, z, 0:8, :]
-
-    def bottom(n, z):
-        at = slice(rows - 8, rows)
-        return adj[n, z, at, :] if n < 19 else fields[n - 19, z, at, :]
+    def tile_of(n, z):
+        return adj[n, z] if n < 19 else fields[n - 19, z]
 
     for n, (up, down) in enumerate(MIRRORS):
-        low = jnp.where(row < 3, top(up, 0), turned(top(up, 1), 3, 0))
-        low = jnp.where(row < 6, low, turned(top(down, 0), 6, 0))
-        low = jnp.where(row < 7, low, turned(top(down, 1), 7, 0))
-        high = jnp.where(row < 3, turned(bottom(down, 0), 3, 0), turned(bottom(down, 1), 6, 0))
-        high = jnp.where(row < 6, high, turned(bottom(up, 0), 7, 0))
-        high = jnp.where(row < 7, high, bottom(up, 1))
+        low = jnp.where(row < 3, tile_of(up, 0), turned(tile_of(up, 1), 3, 0))
+        low = jnp.where(row < 6, low, turned(tile_of(down, 0), 6, 0))
+        low = jnp.where(row < 7, low, turned(tile_of(down, 1), 7, 0))
+        high = jnp.where(row < 3, turned(tile_of(down, 0), 3, 0), turned(tile_of(down, 1), 6, 0))
+        high = jnp.where(row < 6, high, turned(tile_of(up, 0), 7, 0))
+        high = jnp.where(row < 7, high, tile_of(up, 1))
         inner[n] = jnp.where(even_x, high, low)
         outer[n] = jnp.where(even_x, low, high)
     for n in range(0, len(FLAT), 2):
         low = high = None
         for m, item in enumerate(FLAT[n : n + 2]):
-            for z in range(depth):
+            for z in range(2):
                 at = 4 * m + 2 * z
-                up = turned(top(item, z), at, 0)
-                down = turned(bottom(item, z), at + 2, 0)
+                up = turned(tile_of(item, z), at, 0)
+                down = turned(tile_of(item, z), at + 2, 0)
                 low = up if low is None else jnp.where(row < at, low, up)
                 high = down if high is None else jnp.where(row < at, high, down)
         tile = len(MIRRORS) + n // 2
         inner[tile] = jnp.where(even_x, high, low)
         outer[tile] = jnp.where(even_x, low, high)
-    copies[4].wait()
 
 
 RIGHT = 16
@@ -239,10 +249,29 @@
     return jnp.sum(pltpu.roll(block, 0, 1, stride=8, stride_axis=0), axis=0, keepdims=True)
 
 
-def own_kernel(adj, fields, fwd, mask, index, low_own, high_own, fwd_strip, mask_strip, line):
-    low, high = pack_sides(lambda n, z: adj[n, z] if n < 19 else fields[n - 19, z])
-    low_own[...] = low
-    high_own[...] = high
+def own_kernel(
+    adj_hbm, fwd_hbm, level_hbm, mask_hbm, index_hbm, after,
+    adj, fwd, mask, index, fields, low_own, high_own, fwd_strip, mask_strip, line, level, sems,
+):
+    copies = [
+        pltpu.make_async_copy(src, dst, sems.at[n])
+        for n, (src, dst) in enumerate(
+            (
+                (fwd_hbm, fwd), (mask_hbm, mask), (level_hbm, level), (index_hbm, index),
+                (adj_hbm, adj),
+            )
+        )
+    ]
+    for copy in copies:
+        copy.start()
+    for copy in copies[:4]:
+        copy.wait()
+    for z in range(2):
+        values = flow_fields(
+            [fwd[q, z].astype(jnp.float32) for q in range(19)], level[z], mask[z]
+        )
+        for k in range(FIELDS):
+            fields[k, z] = values[k]
     for q in range(19):
         fwd_strip[q] = strip_of([fwd[q, z].astype(jnp.float32) for z in range(2)])
     mask_strip[...] = strip_of([mask[z].astype(jnp.float32) for z in range(2)])
@@ -250,6 +279,10 @@
     line[...] = jnp.broadcast_to(
         edge_line(turned(where, -125, 1), turned(where, 3, 1)), line.shape
     )
+    copies[4].wait()
+    low, high = pack_sides(lambda n, z: adj[n, z] if n < 19 else fields[n - 19, z])
+    low_own[...] = low
+    high_own[...] = high
 
 
 def side_kernel(got_outer, got_inner, low_own, high_own, outer, inner, adj_rim, field_rim):
@@ -490,17 +523,18 @@
     copy_out.wait()
 
 
-def call(kernel, out_types, args, scratch=(), flops=0, where=pltpu.VMEM, to=pltpu.VMEM):
+def call(kernel, out_types, args, scratch=(), flops=0, from_hbm=0, to=pltpu.VMEM):
     moved = sum(a.size * a.dtype.itemsize for a in args)
+    spaces = [pltpu.HBM] * from_hbm + [pltpu.VMEM] * (len(args) - from_hbm)
     return pl.pallas_call(
         kernel,
         out_shape=[to(shape, dtype) for shape, dtype in out_types],
-        in_specs=[pl.BlockSpec(memory_space=where)] * len(args),
+        in_specs=[pl.BlockSpec(memory_space=space) for space in spaces],
         out_specs=[pl.BlockSpec(memory_space=to)] * len(out_types),
         scratch_shapes=list(scratch),
         compiler_params=pltpu.CompilerParams(vmem_limit_bytes=16 << 20),
         cost_estimate=pl.CostEstimate(flops=flops, bytes_accessed=moved, transcendentals=0),
-    )(*[pltpu.with_memory_space_constraint(a, where) for a in args])
+    )(*[pltpu.with_memory_space_constraint(a, space) for a, space in zip(args, spaces)])
 
 
 def per_device(adjoint_end, forward_pop, porosity_level, fluid_mask, design_index):
@@ -516,28 +550,39 @@
     own = ((19, depth, tile_x, tile_y), f32)
     wide = pltpu.VMEM((19, depth, full, tile_y), f32)
 
-    outer, inner, fields, adj, fwd, mask, index = call(
+    message = ((X_TILES, 8, tile_y), f32)
+    static = [porosity_level, fluid_mask]
+    outer, inner = call(
         edge_kernel,
+        [message, message],
+        [adjoint_end, forward_pop, *static],
         [
-            ((X_TILES, 8, tile_y), f32), ((X_TILES, 8, tile_y), f32),
-            ((FIELDS, depth, tile_x, tile_y), f32), own, (forward_pop.shape, forward_pop.dtype),
-            (fluid_mask.shape, fluid_mask.dtype), (design_index.shape, design_index.dtype),
+            pltpu.VMEM((19, depth, 8, tile_y), f32),
+            pltpu.VMEM((19, depth, 2, tile_y), forward_pop.dtype),
+            pltpu.VMEM((19, depth, 2, tile_y), forward_pop.dtype),
+            *[pltpu.VMEM(a.shape, a.dtype) for a in static],
+            pltpu.VMEM((FIELDS, depth, 8, tile_y), f32),
+            pltpu.SemaphoreType.DMA((6,)),
         ],
-        [adjoint_end, forward_pop, porosity_level, fluid_mask, design_index],
+        from_hbm=4,
+    )
+    got_outer = lax.ppermute(outer, "gx", swap_pairs(gx_count, 1))
+    got_inner = lax.ppermute(inner, "gx", swap_pairs(gx_count, 0))
+    flat = ((tile_x, 128), f32)
+    adj, fwd, mask, index, fields, low_own, high_own, fwd_strip, mask_strip, line = call(
+        own_kernel,
+        [
+            own, (forward_pop.shape, forward_pop.dtype), (fluid_mask.shape, fluid_mask.dtype),
+            (design_index.shape, design_index.dtype), ((FIELDS, depth, tile_x, tile_y), f32),
+            flat, flat, ((19, tile_x, 128), f32), flat, ((8, 128), f32),
+        ],
+        [adjoint_end, forward_pop, *static, design_index, outer],
         [
             pltpu.VMEM(porosity_level.shape, porosity_level.dtype),
             pltpu.SemaphoreType.DMA((5,)),
         ],
-        where=pltpu.HBM,
-    )
-    got_outer = lax.ppermute(outer, "gx", swap_pairs(gx_count, 1))
-    got_inner = lax.ppermute(inner, "gx", swap_pairs(gx_count, 0))
-    flat = ((tile_x, 128), f32)
-    low_own, high_own, fwd_strip, mask_strip, line = call(
-        own_kernel,
-        [flat, flat, ((19, tile_x, 128), f32), flat, ((8, 128), f32)],
-        [adj, fields, fwd, mask, index],
         flops=10**6,
+        from_hbm=5,
     )
     outer, inner, adj_rim, field_rim = call(
         side_kernel,

time: 29.3 us -> 29 us (0.990)
  starting transfers between devices: 10.2 us -> 7.32 us
  blocking collectives: 12.7 us -> 14.7 us
  Pallas kernels: 4.6 us -> 5.52 us
  waiting for transfers between devices: 0.99 us -> 0.54 us
    ppermute x1, starting transfers between devices: 4.36 us -> 0.52 us  [per_device(): got_inner = lax.ppermute(inner, 'gx', swap_pairs(gx_count, 0))]
    all_to_all x1, blocking collectives: 12.7 us -> 14.7 us  [per_device(): lax.all_to_all(grid.reshape(owners, 1, chunk), BOTH, split_axis=0, concat...]
    ppermute x1, starting transfers between devices: 4.46 us -> 5.48 us  [per_device(): got_inner = lax.ppermute(inner, 'gy', swap_pairs(gy_count, 0))]
    pallas_call x7, Pallas kernels: 4.6 us -> 5.52 us  [call(): pl.pallas_call(kernel, out_shape=[to(shape, dtype) for shape, dtype in ou...]
    ppermute x1, waiting for transfers between devices: 0.46 us -> 0.01 us  [per_device(): got_inner = lax.ppermute(inner, 'gx', swap_pairs(gx_count, 0))]
  transfers between devices with their start and end apart: 4 -> 4, of which waited for: 2 -> 1; matrix products, arithmetic and copies ran while one was open for 0% -> 0% of each run, Pallas kernels for 5% -> 9%
where the time goes in v5:
time: 29 us; the launch traced here: 28.8 us
  blocking collectives  14.7 us (51%)
  starting transfers between devices  7.32 us (25%)
  Pallas kernels  5.52 us (19%)
  between operations  0.7 us (2%)
  waiting for transfers between devices  0.54 us (2%)
    all_to_all x1, blocking collectives, per_device(): lax.all_to_all(grid.reshape(owners, 1, chunk), BOTH, split_axis=0, concat...  14.7 us
    pallas_call x7, Pallas kernels, call(): pl.pallas_call(kernel, out_shape=[to(shape, dtype) for shape, dtype in ou...  5.52 us
    ppermute x1, starting transfers between devices, per_device(): got_inner = lax.ppermute(inner, 'gy', swap_pairs(gy_count, 0))  5.48 us
    ppermute x1, starting transfers between devices, per_device(): got_outer = lax.ppermute(outer, 'gy', swap_pairs(gy_count, 1))  0.66 us
    ppermute x1, starting transfers between devices, per_device(): got_outer = lax.ppermute(outer, 'gx', swap_pairs(gx_count, 1))  0.65 us
  transfers between devices with their start and end apart: 4, of which 1 were waited for; matrix products, arithmetic and copies ran while one was open for 0% of the time, Pallas kernels for 9%

profile of v5, /device:TPU:0, one launch (start us, length us, event | category | flops | bytes accessed | tf_op | source)
XLA Modules:
  0.0 28.8 jit_solution(669560563713593872)
XLA Ops:
  0.6 1.0 %shard_map.68 = (f32[12,8,128]{2,1,0:T(8,128)S(1)}, f32[12,8,128]{2,1,0:T(8,128)S(1)}) custom-call(f32[19,2,16,128]{3,2,1,0:T(8,128)} %adj_hbm.3, bf16[19,2,16,128]{3,2,1,0:T(8,128)(2,1)} %fwd_hbm.3, s32[2,16,128]{2,1,0:T(8,128)} %level_hbm.3, s32[2,16,128]{2,1,0:T(8,128)} %mask_hbm.3), custom_call_target="tpu_custom_call" | custom-call | bytes 499712 | tf_op jit(solution)/shard_map/pallas_call | solution.py:529
  1.6 0.5 %collective-permute-start.1 = (f32[12,8,128]{2,1,0:T(8,128)S(1)}, f32[12,8,128]{2,1,0:T(8,128)S(1)}, u32[]{:S(2)}, u32[]{:S(2)}) collective-permute-start(f32[12,8,128]{2,1,0:T(8,128)S(1)} %get-tuple-element.25), channel_id=1, source_target_pairs={{0,4},{4,0},{8,12},{12,8},{16,20},{20,16},{24,28},{28,24},{1,5},{5... | collective-permute-start | bytes 147464 | tf_op jit(solution)/shard_map/ppermute | solution.py:570
  2.2 0.7 %collective-permute-start = (f32[12,8,128]{2,1,0:T(8,128)S(1)}, f32[12,8,128]{2,1,0:T(8,128)S(1)}, u32[]{:S(2)}, u32[]{:S(2)}) collective-permute-start(f32[12,8,128]{2,1,0:T(8,128)S(1)} %get-tuple-element.24.after), channel_id=1, source_target_pairs={{4,8},{8,4},{12,16},{16,12},{20,24},{24,20},{5,9},{9,5},{13,17},{1... | collective-permute-start | bytes 147464 | tf_op jit(solution)/shard_map/ppermute | solution.py:569
  2.8 1.5 %shard_map.69 = (f32[19,2,16,128]{3,2,1,0:T(8,128)S(1)}, bf16[19,2,16,128]{3,2,1,0:T(8,128)(2,1)S(1)}, s32[2,16,128]{2,1,0:T(8,128)S(1)}, s32[16,128]{1,0:T(8,12...) custom-call(f32[19,2,16,128]{3,2,1,0:T(8,128)} %adj_hbm.3, ...), custom_call_target="tpu_custom_call" | custom-call | flops 1000000 | bytes 557056 | tf_op jit(solution)/shard_map/pallas_call | solution.py:529
  4.3 0.0 collective-permute-done.1.got_inner
  4.3 0.0 collective-permute-done.got_outer
  4.3 0.2 shard_map.70
  4.5 0.7 %collective-permute-start.2 = (f32[24,128]{1,0:T(8,128)S(1)}, f32[24,128]{1,0:T(8,128)S(1)}, u32[]{:S(2)}, u32[]{:S(2)}) collective-permute-start(f32[24,128]{1,0:T(8,128)S(1)} %get-tuple-element.28), channel_id=1, source_target_pairs={{1,2},{2,1},{5,6},{6,5},{9,10},{10,9},{13,14},{14,13},{17,18},{18,... | collective-permute-start | bytes 36872 | tf_op jit(solution)/shard_map/ppermute | solution.py:595
  5.2 5.5 %collective-permute-start.3 = (f32[24,128]{1,0:T(8,128)S(1)}, f32[24,128]{1,0:T(8,128)S(1)}, u32[]{:S(2)}, u32[]{:S(2)}) collective-permute-start(f32[24,128]{1,0:T(8,128)S(1)} %get-tuple-element.29), channel_id=1, source_target_pairs={{0,1},{1,0},{2,3},{3,2},{4,5},{5,4},{6,7},{7,6},{8,9},{9,8},{10,11... | collective-permute-start | bytes 36872 | tf_op jit(solution)/shard_map/ppermute | solution.py:596
  10.7 1.1 %shard_map.71 = (f32[32,128]{1,0:T(8,128)S(1)}, f32[19,2,16,128]{3,2,1,0:T(8,128)S(1)}, f32[19,24,128]{2,1,0:T(8,128)S(1)}, f32[5,24,128]{2,1,0:T(8,128)S(1)}) custom-call(f32[19,2,16,128]{3,2,1,0:T(8,128)S(1)} %get-tuple-element.30.refs_0_, f32[19,2,8,128]{3,2,1,0:T(8,128)S(1)} %get-tuple-element.31.refs_1_, ...), custom_call_target="tpu_custom_call" | custom-call | flops 1000000 | bytes 770048 | tf_op jit(solution)/shard_map/pallas_call | solution.py:529
  11.8 0.0 collective-permute-done.2.got_outer
  11.8 0.5 %collective-permute-done.3.got_inner = f32[24,128]{1,0:T(8,128)S(1)} collective-permute-done((f32[24,128]{1,0:T(8,128)S(1)}, f32[24,128]{1,0:T(8,128)S(1)}, u32[]{:S(2)}, u32[]{:S(2)}) %collective-permute-start.3) | collective-permute-done | bytes 12320 | tf_op jit(solution)/shard_map/ppermute | solution.py:596
  12.3 0.7 %shard_map.72 = (f32[16,128]{1,0:T(8,128)S(1)}, f32[19,2,16,128]{3,2,1,0:T(8,128)S(1)}) custom-call(f32[24,128]{1,0:T(8,128)S(1)} %collective-permute-done.2.got_outer, f32[24,128]{1,0:T(8,128)S(1)} %collective-permute-done.3.got_inner, f32[19,24,128]{2,1,0:T(8,128)S(1)} %get-tuple-element.37.strip, f32[5,24,128]{2,1,0:T(8,128)S(1)} %get-tuple-element.38.field_strip, ...), custom_call_target="tpu_custom_call" | custom-call | bytes 794624 | tf_op jit(solution)/shard_map/pallas_call | solution.py:529
  13.1 0.2 shard_map.73
  13.3 14.7 %all_to_all.5 = f32[32,1,128]{2,1,0:T(1,128)S(1)} all-to-all(f32[32,1,128]{2,1,0:T(1,128)S(1)} %bitcast.5), channel_id=1, replica_groups=mesh['gx'=8,'gy'=4] {'gx','gy'}, dimensions={0} | all-to-all | bytes 32768 | tf_op jit(solution)/shard_map/all_to_all | solution.py:618
  28.0 0.7 %shard_map.74 = (f32[19,2,16,128]{3,2,1,0:T(8,128)}, f32[4,32]{1,0:T(4,128)}) custom-call(f32[32,128]{1,0:T(8,128)S(1)} %bitcast.4, f32[19,2,16,128]{3,2,1,0:T(8,128)S(1)} %get-tuple-element.45.refs_3_.out), custom_call_target="tpu_custom_call" | custom-call | bytes 327680 | tf_op jit(solution)/shard_map/pallas_call | solution.py:529
Async XLA Ops:
  1.6 2.7 %collective-permute-start.1 = (f32[12,8,128]{2,1,0:T(8,128)S(1)}, f32[12,8,128]{2,1,0:T(8,128)S(1)}, u32[]{:S(2)}, u32[]{:S(2)}) collective-permute-start(f32[12,8,128]{2,1,0:T(8,128)S(1)} %get-tuple-element.25), channel_id=1, source_target_pairs={{0,4},{4,0},{8,12},{12,8},{16,20},{20,16},{24,28},{28,24},{1,5},{5... | collective-permute-start | bytes 147464 | tf_op jit(solution)/shard_map/ppermute | solution.py:570
  2.2 2.2 %collective-permute-start = (f32[12,8,128]{2,1,0:T(8,128)S(1)}, f32[12,8,128]{2,1,0:T(8,128)S(1)}, u32[]{:S(2)}, u32[]{:S(2)}) collective-permute-start(f32[12,8,128]{2,1,0:T(8,128)S(1)} %get-tuple-element.24.after), channel_id=1, source_target_pairs={{4,8},{8,4},{12,16},{16,12},{20,24},{24,20},{5,9},{9,5},{13,17},{1... | collective-permute-start | bytes 147464 | tf_op jit(solution)/shard_map/ppermute | solution.py:569
  4.5 7.3 %collective-permute-start.2 = (f32[24,128]{1,0:T(8,128)S(1)}, f32[24,128]{1,0:T(8,128)S(1)}, u32[]{:S(2)}, u32[]{:S(2)}) collective-permute-start(f32[24,128]{1,0:T(8,128)S(1)} %get-tuple-element.28), channel_id=1, source_target_pairs={{1,2},{2,1},{5,6},{6,5},{9,10},{10,9},{13,14},{14,13},{17,18},{18,... | collective-permute-start | bytes 36872 | tf_op jit(solution)/shard_map/ppermute | solution.py:595
  5.2 7.2 %collective-permute-start.3 = (f32[24,128]{1,0:T(8,128)S(1)}, f32[24,128]{1,0:T(8,128)S(1)}, u32[]{:S(2)}, u32[]{:S(2)}) collective-permute-start(f32[24,128]{1,0:T(8,128)S(1)} %get-tuple-element.29), channel_id=1, source_target_pairs={{0,1},{1,0},{2,3},{3,2},{4,5},{5,4},{6,7},{7,6},{8,9},{9,8},{10,11... | collective-permute-start | bytes 36872 | tf_op jit(solution)/shard_map/ppermute | solution.py:596

commit v6 on v5

--- a/solution.py
+++ b/solution.py
@@ -217,7 +217,7 @@
 
 
 RIGHT = 16
-LEFT = 51
+LEFT = 50
 
 
 def strip_of(pair):
@@ -243,9 +243,11 @@
     return low, high
 
 
-def edge_line(right, left):
-    lane = iota(right.shape, 1)
-    block = jnp.where(lane < 3, right, jnp.where(lane < 6, left, 0.0))
+def edge_line(block):
+    lane = iota(block.shape, 1)
+    right = (lane >= RIGHT - 3) & (lane < RIGHT)
+    left = (lane >= LEFT) & (lane < LEFT + 3)
+    block = jnp.where(right | left, block, 0.0)
     return jnp.sum(pltpu.roll(block, 0, 1, stride=8, stride_axis=0), axis=0, keepdims=True)
 
 
@@ -276,9 +278,9 @@
         fwd_strip[q] = strip_of([fwd[q, z].astype(jnp.float32) for z in range(2)])
     mask_strip[...] = strip_of([mask[z].astype(jnp.float32) for z in range(2)])
     where = index[...].astype(jnp.float32)
-    line[...] = jnp.broadcast_to(
-        edge_line(turned(where, -125, 1), turned(where, 3, 1)), line.shape
-    )
+    lane = iota(where.shape, 1)
+    where = jnp.where(lane < Z_LANES // 2, turned(where, RIGHT, 1), turned(where, LEFT, 1))
+    line[...] = jnp.broadcast_to(edge_line(where), line.shape)
     copies[4].wait()
     low, high = pack_sides(lambda n, z: adj[n, z] if n < 19 else fields[n - 19, z])
     low_own[...] = low
@@ -448,7 +450,7 @@
     high = jnp.where(even_y, from_in, from_out)
     lane = iota((full, 128), 1) & (Z_LANES - 1)
     half = Z_LANES // 2
-    deep = jnp.where(lane < half, high, turned(low, LEFT - 3 - RIGHT, 1))
+    deep = jnp.where(lane < 3 * len(DEEP), high, turned(low, LEFT - 3 - RIGHT, 1))
     thin = jnp.where(lane >= half, high, turned(low, LEFT - 2 - RIGHT, 1))
     moved = {
         (width, shift): turned(both, -shift, 0)
@@ -504,7 +506,7 @@
 
 
 def sum_kernel(owners, chunk, column, line, grid_inside, after, grid):
-    values = edge_line(turned(column[...], 3 - RIGHT, 1), turned(column[...], 3 - LEFT, 1))
+    values = edge_line(column[...])
     owner, slot = split_index(line[0:1, :].astype(jnp.int32), chunk)
     acc = hot_product(*hot_rows(values, owner, slot, owners, chunk))
     grid[...] = grid_inside[...] + (acc[:owners] + acc[owners:])

time: 29 us -> 28.9 us (level)
  no operation moved by 1% of the time
where the time goes in v6:
time: 28.9 us; the launch traced here: 28.7 us
  blocking collectives  14.7 us (51%)
  starting transfers between devices  7.32 us (25%)
  Pallas kernels  5.46 us (19%)
  between operations  0.7 us (2%)
  waiting for transfers between devices  0.54 us (2%)
    all_to_all x1, blocking collectives, per_device(): lax.all_to_all(grid.reshape(owners, 1, chunk), BOTH, split_axis=0, concat...  14.7 us
    ppermute x1, starting transfers between devices, per_device(): got_inner = lax.ppermute(inner, 'gy', swap_pairs(gy_count, 0))  5.48 us
    pallas_call x7, Pallas kernels, call(): pl.pallas_call(kernel, out_shape=[to(shape, dtype) for shape, dtype in ou...  5.46 us
    ppermute x1, starting transfers between devices, per_device(): got_outer = lax.ppermute(outer, 'gy', swap_pairs(gy_count, 1))  0.66 us
    ppermute x1, starting transfers between devices, per_device(): got_outer = lax.ppermute(outer, 'gx', swap_pairs(gx_count, 1))  0.65 us
  transfers between devices with their start and end apart: 4, of which 1 were waited for; matrix products, arithmetic and copies ran while one was open for 0% of the time, Pallas kernels for 9%

profile of v6, /device:TPU:0, one launch (start us, length us, event | category | flops | bytes accessed | tf_op | source)
XLA Modules:
  0.0 28.7 jit_solution(3602334739009616953)
XLA Ops:
  0.6 1.0 %shard_map.68 = (f32[12,8,128]{2,1,0:T(8,128)S(1)}, f32[12,8,128]{2,1,0:T(8,128)S(1)}) custom-call(f32[19,2,16,128]{3,2,1,0:T(8,128)} %adj_hbm.3, bf16[19,2,16,128]{3,2,1,0:T(8,128)(2,1)} %fwd_hbm.3, s32[2,16,128]{2,1,0:T(8,128)} %level_hbm.3, s32[2,16,128]{2,1,0:T(8,128)} %mask_hbm.3), custom_call_target="tpu_custom_call" | custom-call | bytes 499712 | tf_op jit(solution)/shard_map/pallas_call | solution.py:531
  1.6 0.5 %collective-permute-start.1 = (f32[12,8,128]{2,1,0:T(8,128)S(1)}, f32[12,8,128]{2,1,0:T(8,128)S(1)}, u32[]{:S(2)}, u32[]{:S(2)}) collective-permute-start(f32[12,8,128]{2,1,0:T(8,128)S(1)} %get-tuple-element.25), channel_id=1, source_target_pairs={{0,4},{4,0},{8,12},{12,8},{16,20},{20,16},{24,28},{28,24},{1,5},{5... | collective-permute-start | bytes 147464 | tf_op jit(solution)/shard_map/ppermute | solution.py:572
  2.2 0.7 %collective-permute-start = (f32[12,8,128]{2,1,0:T(8,128)S(1)}, f32[12,8,128]{2,1,0:T(8,128)S(1)}, u32[]{:S(2)}, u32[]{:S(2)}) collective-permute-start(f32[12,8,128]{2,1,0:T(8,128)S(1)} %get-tuple-element.24.after), channel_id=1, source_target_pairs={{4,8},{8,4},{12,16},{16,12},{20,24},{24,20},{5,9},{9,5},{13,17},{1... | collective-permute-start | bytes 147464 | tf_op jit(solution)/shard_map/ppermute | solution.py:571
  2.8 1.5 %shard_map.69 = (f32[19,2,16,128]{3,2,1,0:T(8,128)S(1)}, bf16[19,2,16,128]{3,2,1,0:T(8,128)(2,1)S(1)}, s32[2,16,128]{2,1,0:T(8,128)S(1)}, s32[16,128]{1,0:T(8,12...) custom-call(f32[19,2,16,128]{3,2,1,0:T(8,128)} %adj_hbm.3, ...), custom_call_target="tpu_custom_call" | custom-call | flops 1000000 | bytes 557056 | tf_op jit(solution)/shard_map/pallas_call | solution.py:531
  4.3 0.0 collective-permute-done.1.got_inner
  4.3 0.0 collective-permute-done.got_outer
  4.3 0.2 shard_map.70
  4.5 0.7 %collective-permute-start.2 = (f32[24,128]{1,0:T(8,128)S(1)}, f32[24,128]{1,0:T(8,128)S(1)}, u32[]{:S(2)}, u32[]{:S(2)}) collective-permute-start(f32[24,128]{1,0:T(8,128)S(1)} %get-tuple-element.28), channel_id=1, source_target_pairs={{1,2},{2,1},{5,6},{6,5},{9,10},{10,9},{13,14},{14,13},{17,18},{18,... | collective-permute-start | bytes 36872 | tf_op jit(solution)/shard_map/ppermute | solution.py:597
  5.2 5.5 %collective-permute-start.3 = (f32[24,128]{1,0:T(8,128)S(1)}, f32[24,128]{1,0:T(8,128)S(1)}, u32[]{:S(2)}, u32[]{:S(2)}) collective-permute-start(f32[24,128]{1,0:T(8,128)S(1)} %get-tuple-element.29), channel_id=1, source_target_pairs={{0,1},{1,0},{2,3},{3,2},{4,5},{5,4},{6,7},{7,6},{8,9},{9,8},{10,11... | collective-permute-start | bytes 36872 | tf_op jit(solution)/shard_map/ppermute | solution.py:598
  10.7 1.1 %shard_map.71 = (f32[32,128]{1,0:T(8,128)S(1)}, f32[19,2,16,128]{3,2,1,0:T(8,128)S(1)}, f32[19,24,128]{2,1,0:T(8,128)S(1)}, f32[5,24,128]{2,1,0:T(8,128)S(1)}) custom-call(f32[19,2,16,128]{3,2,1,0:T(8,128)S(1)} %get-tuple-element.30.refs_0_, f32[19,2,8,128]{3,2,1,0:T(8,128)S(1)} %get-tuple-element.31.refs_1_, ...), custom_call_target="tpu_custom_call" | custom-call | flops 1000000 | bytes 770048 | tf_op jit(solution)/shard_map/pallas_call | solution.py:531
  11.8 0.0 collective-permute-done.2.got_outer
  11.8 0.5 %collective-permute-done.3.got_inner = f32[24,128]{1,0:T(8,128)S(1)} collective-permute-done((f32[24,128]{1,0:T(8,128)S(1)}, f32[24,128]{1,0:T(8,128)S(1)}, u32[]{:S(2)}, u32[]{:S(2)}) %collective-permute-start.3) | collective-permute-done | bytes 12320 | tf_op jit(solution)/shard_map/ppermute | solution.py:598
  12.3 0.7 %shard_map.72 = (f32[16,128]{1,0:T(8,128)S(1)}, f32[19,2,16,128]{3,2,1,0:T(8,128)S(1)}) custom-call(f32[24,128]{1,0:T(8,128)S(1)} %collective-permute-done.2.got_outer, f32[24,128]{1,0:T(8,128)S(1)} %collective-permute-done.3.got_inner, f32[19,24,128]{2,1,0:T(8,128)S(1)} %get-tuple-element.37.strip, f32[5,24,128]{2,1,0:T(8,128)S(1)} %get-tuple-element.38.field_strip, ...), custom_call_target="tpu_custom_call" | custom-call | bytes 794624 | tf_op jit(solution)/shard_map/pallas_call | solution.py:531
  13.1 0.2 shard_map.73
  13.3 14.7 %all_to_all.5 = f32[32,1,128]{2,1,0:T(1,128)S(1)} all-to-all(f32[32,1,128]{2,1,0:T(1,128)S(1)} %bitcast.5), channel_id=1, replica_groups=mesh['gx'=8,'gy'=4] {'gx','gy'}, dimensions={0} | all-to-all | bytes 32768 | tf_op jit(solution)/shard_map/all_to_all | solution.py:620
  28.0 0.7 %shard_map.74 = (f32[19,2,16,128]{3,2,1,0:T(8,128)}, f32[4,32]{1,0:T(4,128)}) custom-call(f32[32,128]{1,0:T(8,128)S(1)} %bitcast.4, f32[19,2,16,128]{3,2,1,0:T(8,128)S(1)} %get-tuple-element.45.refs_3_.out), custom_call_target="tpu_custom_call" | custom-call | bytes 327680 | tf_op jit(solution)/shard_map/pallas_call | solution.py:531
Async XLA Ops:
  1.6 2.7 %collective-permute-start.1 = (f32[12,8,128]{2,1,0:T(8,128)S(1)}, f32[12,8,128]{2,1,0:T(8,128)S(1)}, u32[]{:S(2)}, u32[]{:S(2)}) collective-permute-start(f32[12,8,128]{2,1,0:T(8,128)S(1)} %get-tuple-element.25), channel_id=1, source_target_pairs={{0,4},{4,0},{8,12},{12,8},{16,20},{20,16},{24,28},{28,24},{1,5},{5... | collective-permute-start | bytes 147464 | tf_op jit(solution)/shard_map/ppermute | solution.py:572
  2.2 2.2 %collective-permute-start = (f32[12,8,128]{2,1,0:T(8,128)S(1)}, f32[12,8,128]{2,1,0:T(8,128)S(1)}, u32[]{:S(2)}, u32[]{:S(2)}) collective-permute-start(f32[12,8,128]{2,1,0:T(8,128)S(1)} %get-tuple-element.24.after), channel_id=1, source_target_pairs={{4,8},{8,4},{12,16},{16,12},{20,24},{24,20},{5,9},{9,5},{13,17},{1... | collective-permute-start | bytes 147464 | tf_op jit(solution)/shard_map/ppermute | solution.py:571
  4.5 7.3 %collective-permute-start.2 = (f32[24,128]{1,0:T(8,128)S(1)}, f32[24,128]{1,0:T(8,128)S(1)}, u32[]{:S(2)}, u32[]{:S(2)}) collective-permute-start(f32[24,128]{1,0:T(8,128)S(1)} %get-tuple-element.28), channel_id=1, source_target_pairs={{1,2},{2,1},{5,6},{6,5},{9,10},{10,9},{13,14},{14,13},{17,18},{18,... | collective-permute-start | bytes 36872 | tf_op jit(solution)/shard_map/ppermute | solution.py:597
  5.2 7.2 %collective-permute-start.3 = (f32[24,128]{1,0:T(8,128)S(1)}, f32[24,128]{1,0:T(8,128)S(1)}, u32[]{:S(2)}, u32[]{:S(2)}) collective-permute-start(f32[24,128]{1,0:T(8,128)S(1)} %get-tuple-element.29), channel_id=1, source_target_pairs={{0,1},{1,0},{2,3},{3,2},{4,5},{5,4},{6,7},{7,6},{8,9},{9,8},{10,11... | collective-permute-start | bytes 36872 | tf_op jit(solution)/shard_map/ppermute | solution.py:598

commit v7 on v6

--- a/solution.py
+++ b/solution.py
@@ -154,27 +154,29 @@
     )
 
 
+def parts_of(count, pieces):
+    return [slice(count * n // pieces, count * (n + 1) // pieces) for n in range(pieces)]
+
+
 def edge_kernel(
     adj_hbm, fwd_hbm, level_hbm, mask_hbm, outer, inner, adj, fwd_top, fwd_end, level, mask,
     fields, sems,
 ):
     rows = adj_hbm.shape[2]
+    pairs = [(mask_hbm, mask), (level_hbm, level)]
+    for part in parts_of(19, 1):
+        pairs.append((fwd_hbm.at[part, :, pl.ds(0, 2), :], fwd_top.at[part]))
+        pairs.append((fwd_hbm.at[part, :, pl.ds(rows - 2, 2), :], fwd_end.at[part]))
+    early = len(pairs)
+    for part in parts_of(19, 2):
+        pairs.append((adj_hbm.at[part, :, pl.ds(0, 3), :], adj.at[part, :, pl.ds(0, 3), :]))
+        pairs.append((adj_hbm.at[part, :, pl.ds(rows - 3, 3), :], adj.at[part, :, pl.ds(5, 3), :]))
     copies = [
-        pltpu.make_async_copy(src, dst, sems.at[n])
-        for n, (src, dst) in enumerate(
-            (
-                (fwd_hbm.at[:, :, pl.ds(0, 2), :], fwd_top),
-                (fwd_hbm.at[:, :, pl.ds(rows - 2, 2), :], fwd_end),
-                (mask_hbm, mask),
-                (level_hbm, level),
-                (adj_hbm.at[:, :, pl.ds(0, 3), :], adj.at[:, :, pl.ds(0, 3), :]),
-                (adj_hbm.at[:, :, pl.ds(rows - 3, 3), :], adj.at[:, :, pl.ds(5, 3), :]),
-            )
-        )
+        pltpu.make_async_copy(src, dst, sems.at[n]) for n, (src, dst) in enumerate(pairs)
     ]
-    for copy in copies:
+    for n, copy in enumerate(copies):
         copy.start()
-    for copy in copies[:4]:
+    for copy in copies[:early]:
         copy.wait()
     for z in range(2):
         for fwd, at, to in ((fwd_top, 0, 0), (fwd_end, rows - 2, 6)):
@@ -185,7 +187,7 @@
             )
             for k in range(FIELDS):
                 fields[k, z, to : to + 2, :] = values[k]
-    for copy in copies[4:]:
+    for copy in copies[early:]:
         copy.wait()
     even_x = is_even("gx")
     row = iota((8, 128), 0)
@@ -564,7 +566,7 @@
             pltpu.VMEM((19, depth, 2, tile_y), forward_pop.dtype),
             *[pltpu.VMEM(a.shape, a.dtype) for a in static],
             pltpu.VMEM((FIELDS, depth, 8, tile_y), f32),
-            pltpu.SemaphoreType.DMA((6,)),
+            pltpu.SemaphoreType.DMA((8,)),
         ],
         from_hbm=4,
     )

time: 28.9 us -> 28.9 us (level)
  no operation moved by 1% of the time
where the time goes in v7:
time: 28.9 us; the launch traced here: 28.7 us
  blocking collectives  14.7 us (51%)
  starting transfers between devices  7.32 us (25%)
  Pallas kernels  5.42 us (19%)
  between operations  0.7 us (2%)
  waiting for transfers between devices  0.54 us (2%)
    all_to_all x1, blocking collectives, per_device(): lax.all_to_all(grid.reshape(owners, 1, chunk), BOTH, split_axis=0, concat...  14.7 us
    ppermute x1, starting transfers between devices, per_device(): got_inner = lax.ppermute(inner, 'gy', swap_pairs(gy_count, 0))  5.48 us
    pallas_call x7, Pallas kernels, call(): pl.pallas_call(kernel, out_shape=[to(shape, dtype) for shape, dtype in ou...  5.42 us
    ppermute x1, starting transfers between devices, per_device(): got_outer = lax.ppermute(outer, 'gy', swap_pairs(gy_count, 1))  0.66 us
    ppermute x1, starting transfers between devices, per_device(): got_outer = lax.ppermute(outer, 'gx', swap_pairs(gx_count, 1))  0.65 us
  transfers between devices with their start and end apart: 4, of which 1 were waited for; matrix products, arithmetic and copies ran while one was open for 0% of the time, Pallas kernels for 9%

profile of v7, /device:TPU:0, one launch (start us, length us, event | category | flops | bytes accessed | tf_op | source)
XLA Modules:
  0.0 28.7 jit_solution(12063111129143397066)
XLA Ops:
  0.6 1.0 %shard_map.68 = (f32[12,8,128]{2,1,0:T(8,128)S(1)}, f32[12,8,128]{2,1,0:T(8,128)S(1)}) custom-call(f32[19,2,16,128]{3,2,1,0:T(8,128)} %adj_hbm.3, bf16[19,2,16,128]{3,2,1,0:T(8,128)(2,1)} %fwd_hbm.3, s32[2,16,128]{2,1,0:T(8,128)} %level_hbm.3, s32[2,16,128]{2,1,0:T(8,128)} %mask_hbm.3), custom_call_target="tpu_custom_call" | custom-call | bytes 499712 | tf_op jit(solution)/shard_map/pallas_call | solution.py:533
  1.6 0.5 %collective-permute-start.1 = (f32[12,8,128]{2,1,0:T(8,128)S(1)}, f32[12,8,128]{2,1,0:T(8,128)S(1)}, u32[]{:S(2)}, u32[]{:S(2)}) collective-permute-start(f32[12,8,128]{2,1,0:T(8,128)S(1)} %get-tuple-element.25), channel_id=1, source_target_pairs={{0,4},{4,0},{8,12},{12,8},{16,20},{20,16},{24,28},{28,24},{1,5},{5... | collective-permute-start | bytes 147464 | tf_op jit(solution)/shard_map/ppermute | solution.py:574
  2.1 0.7 %collective-permute-start = (f32[12,8,128]{2,1,0:T(8,128)S(1)}, f32[12,8,128]{2,1,0:T(8,128)S(1)}, u32[]{:S(2)}, u32[]{:S(2)}) collective-permute-start(f32[12,8,128]{2,1,0:T(8,128)S(1)} %get-tuple-element.24.after), channel_id=1, source_target_pairs={{4,8},{8,4},{12,16},{16,12},{20,24},{24,20},{5,9},{9,5},{13,17},{1... | collective-permute-start | bytes 147464 | tf_op jit(solution)/shard_map/ppermute | solution.py:573
  2.8 1.5 %shard_map.69 = (f32[19,2,16,128]{3,2,1,0:T(8,128)S(1)}, bf16[19,2,16,128]{3,2,1,0:T(8,128)(2,1)S(1)}, s32[2,16,128]{2,1,0:T(8,128)S(1)}, s32[16,128]{1,0:T(8,12...) custom-call(f32[19,2,16,128]{3,2,1,0:T(8,128)} %adj_hbm.3, ...), custom_call_target="tpu_custom_call" | custom-call | flops 1000000 | bytes 557056 | tf_op jit(solution)/shard_map/pallas_call | solution.py:533
  4.3 0.0 collective-permute-done.1.got_inner
  4.3 0.0 collective-permute-done.got_outer
  4.3 0.2 shard_map.70
  4.5 0.7 %collective-permute-start.2 = (f32[24,128]{1,0:T(8,128)S(1)}, f32[24,128]{1,0:T(8,128)S(1)}, u32[]{:S(2)}, u32[]{:S(2)}) collective-permute-start(f32[24,128]{1,0:T(8,128)S(1)} %get-tuple-element.28), channel_id=1, source_target_pairs={{1,2},{2,1},{5,6},{6,5},{9,10},{10,9},{13,14},{14,13},{17,18},{18,... | collective-permute-start | bytes 36872 | tf_op jit(solution)/shard_map/ppermute | solution.py:599
  5.1 5.5 %collective-permute-start.3 = (f32[24,128]{1,0:T(8,128)S(1)}, f32[24,128]{1,0:T(8,128)S(1)}, u32[]{:S(2)}, u32[]{:S(2)}) collective-permute-start(f32[24,128]{1,0:T(8,128)S(1)} %get-tuple-element.29), channel_id=1, source_target_pairs={{0,1},{1,0},{2,3},{3,2},{4,5},{5,4},{6,7},{7,6},{8,9},{9,8},{10,11... | collective-permute-start | bytes 36872 | tf_op jit(solution)/shard_map/ppermute | solution.py:600
  10.6 1.1 %shard_map.71 = (f32[32,128]{1,0:T(8,128)S(1)}, f32[19,2,16,128]{3,2,1,0:T(8,128)S(1)}, f32[19,24,128]{2,1,0:T(8,128)S(1)}, f32[5,24,128]{2,1,0:T(8,128)S(1)}) custom-call(f32[19,2,16,128]{3,2,1,0:T(8,128)S(1)} %get-tuple-element.30.refs_0_, f32[19,2,8,128]{3,2,1,0:T(8,128)S(1)} %get-tuple-element.31.refs_1_, ...), custom_call_target="tpu_custom_call" | custom-call | flops 1000000 | bytes 770048 | tf_op jit(solution)/shard_map/pallas_call | solution.py:533
  11.8 0.0 collective-permute-done.2.got_outer
  11.8 0.5 %collective-permute-done.3.got_inner = f32[24,128]{1,0:T(8,128)S(1)} collective-permute-done((f32[24,128]{1,0:T(8,128)S(1)}, f32[24,128]{1,0:T(8,128)S(1)}, u32[]{:S(2)}, u32[]{:S(2)}) %collective-permute-start.3) | collective-permute-done | bytes 12320 | tf_op jit(solution)/shard_map/ppermute | solution.py:600
  12.3 0.7 %shard_map.72 = (f32[16,128]{1,0:T(8,128)S(1)}, f32[19,2,16,128]{3,2,1,0:T(8,128)S(1)}) custom-call(f32[24,128]{1,0:T(8,128)S(1)} %collective-permute-done.2.got_outer, f32[24,128]{1,0:T(8,128)S(1)} %collective-permute-done.3.got_inner, f32[19,24,128]{2,1,0:T(8,128)S(1)} %get-tuple-element.37.strip, f32[5,24,128]{2,1,0:T(8,128)S(1)} %get-tuple-element.38.field_strip, ...), custom_call_target="tpu_custom_call" | custom-call | bytes 794624 | tf_op jit(solution)/shard_map/pallas_call | solution.py:533
  13.1 0.2 shard_map.73
  13.2 14.7 %all_to_all.5 = f32[32,1,128]{2,1,0:T(1,128)S(1)} all-to-all(f32[32,1,128]{2,1,0:T(1,128)S(1)} %bitcast.5), channel_id=1, replica_groups=mesh['gx'=8,'gy'=4] {'gx','gy'}, dimensions={0} | all-to-all | bytes 32768 | tf_op jit(solution)/shard_map/all_to_all | solution.py:622
  27.9 0.7 %shard_map.74 = (f32[19,2,16,128]{3,2,1,0:T(8,128)}, f32[4,32]{1,0:T(4,128)}) custom-call(f32[32,128]{1,0:T(8,128)S(1)} %bitcast.4, f32[19,2,16,128]{3,2,1,0:T(8,128)S(1)} %get-tuple-element.45.refs_3_.out), custom_call_target="tpu_custom_call" | custom-call | bytes 327680 | tf_op jit(solution)/shard_map/pallas_call | solution.py:533
Async XLA Ops:
  1.6 2.7 %collective-permute-start.1 = (f32[12,8,128]{2,1,0:T(8,128)S(1)}, f32[12,8,128]{2,1,0:T(8,128)S(1)}, u32[]{:S(2)}, u32[]{:S(2)}) collective-permute-start(f32[12,8,128]{2,1,0:T(8,128)S(1)} %get-tuple-element.25), channel_id=1, source_target_pairs={{0,4},{4,0},{8,12},{12,8},{16,20},{20,16},{24,28},{28,24},{1,5},{5... | collective-permute-start | bytes 147464 | tf_op jit(solution)/shard_map/ppermute | solution.py:574
  2.1 2.2 %collective-permute-start = (f32[12,8,128]{2,1,0:T(8,128)S(1)}, f32[12,8,128]{2,1,0:T(8,128)S(1)}, u32[]{:S(2)}, u32[]{:S(2)}) collective-permute-start(f32[12,8,128]{2,1,0:T(8,128)S(1)} %get-tuple-element.24.after), channel_id=1, source_target_pairs={{4,8},{8,4},{12,16},{16,12},{20,24},{24,20},{5,9},{9,5},{13,17},{1... | collective-permute-start | bytes 147464 | tf_op jit(solution)/shard_map/ppermute | solution.py:573
  4.5 7.3 %collective-permute-start.2 = (f32[24,128]{1,0:T(8,128)S(1)}, f32[24,128]{1,0:T(8,128)S(1)}, u32[]{:S(2)}, u32[]{:S(2)}) collective-permute-start(f32[24,128]{1,0:T(8,128)S(1)} %get-tuple-element.28), channel_id=1, source_target_pairs={{1,2},{2,1},{5,6},{6,5},{9,10},{10,9},{13,14},{14,13},{17,18},{18,... | collective-permute-start | bytes 36872 | tf_op jit(solution)/shard_map/ppermute | solution.py:599
  5.1 7.2 %collective-permute-start.3 = (f32[24,128]{1,0:T(8,128)S(1)}, f32[24,128]{1,0:T(8,128)S(1)}, u32[]{:S(2)}, u32[]{:S(2)}) collective-permute-start(f32[24,128]{1,0:T(8,128)S(1)} %get-tuple-element.29), channel_id=1, source_target_pairs={{0,1},{1,0},{2,3},{3,2},{4,5},{5,4},{6,7},{7,6},{8,9},{9,8},{10,11... | collective-permute-start | bytes 36872 | tf_op jit(solution)/shard_map/ppermute | solution.py:600

commit v8 on v7

--- a/solution.py
+++ b/solution.py
@@ -175,7 +175,7 @@
         pltpu.make_async_copy(src, dst, sems.at[n]) for n, (src, dst) in enumerate(pairs)
     ]
     for n, copy in enumerate(copies):
-        copy.start()
+        copy.start(priority=n % 2)
     for copy in copies[:early]:
         copy.wait()
     for z in range(2):

time: 28.9 us -> 28.9 us (level)
  no operation moved by 1% of the time
where the time goes in v8:
time: 28.9 us; the launch traced here: 28.7 us
  blocking collectives  14.7 us (51%)
  starting transfers between devices  7.32 us (25%)
  Pallas kernels  5.42 us (19%)
  between operations  0.7 us (2%)
  waiting for transfers between devices  0.54 us (2%)
    all_to_all x1, blocking collectives, per_device(): lax.all_to_all(grid.reshape(owners, 1, chunk), BOTH, split_axis=0, concat...  14.7 us
    ppermute x1, starting transfers between devices, per_device(): got_inner = lax.ppermute(inner, 'gy', swap_pairs(gy_count, 0))  5.48 us
    pallas_call x7, Pallas kernels, call(): pl.pallas_call(kernel, out_shape=[to(shape, dtype) for shape, dtype in ou...  5.42 us
    ppermute x1, starting transfers between devices, per_device(): got_outer = lax.ppermute(outer, 'gy', swap_pairs(gy_count, 1))  0.66 us
    ppermute x1, starting transfers between devices, per_device(): got_outer = lax.ppermute(outer, 'gx', swap_pairs(gx_count, 1))  0.65 us
  transfers between devices with their start and end apart: 4, of which 1 were waited for; matrix products, arithmetic and copies ran while one was open for 0% of the time, Pallas kernels for 9%

profile of v8, /device:TPU:0, one launch (start us, length us, event | category | flops | bytes accessed | tf_op | source)
XLA Modules:
  0.0 28.7 jit_solution(8748958505500556413)
XLA Ops:
  0.6 1.0 %shard_map.68 = (f32[12,8,128]{2,1,0:T(8,128)S(1)}, f32[12,8,128]{2,1,0:T(8,128)S(1)}) custom-call(f32[19,2,16,128]{3,2,1,0:T(8,128)} %adj_hbm.3, bf16[19,2,16,128]{3,2,1,0:T(8,128)(2,1)} %fwd_hbm.3, s32[2,16,128]{2,1,0:T(8,128)} %level_hbm.3, s32[2,16,128]{2,1,0:T(8,128)} %mask_hbm.3), custom_call_target="tpu_custom_call" | custom-call | bytes 499712 | tf_op jit(solution)/shard_map/pallas_call | solution.py:533
  1.6 0.5 %collective-permute-start.1 = (f32[12,8,128]{2,1,0:T(8,128)S(1)}, f32[12,8,128]{2,1,0:T(8,128)S(1)}, u32[]{:S(2)}, u32[]{:S(2)}) collective-permute-start(f32[12,8,128]{2,1,0:T(8,128)S(1)} %get-tuple-element.25), channel_id=1, source_target_pairs={{0,4},{4,0},{8,12},{12,8},{16,20},{20,16},{24,28},{28,24},{1,5},{5... | collective-permute-start | bytes 147464 | tf_op jit(solution)/shard_map/ppermute | solution.py:574
  2.1 0.7 %collective-permute-start = (f32[12,8,128]{2,1,0:T(8,128)S(1)}, f32[12,8,128]{2,1,0:T(8,128)S(1)}, u32[]{:S(2)}, u32[]{:S(2)}) collective-permute-start(f32[12,8,128]{2,1,0:T(8,128)S(1)} %get-tuple-element.24.after), channel_id=1, source_target_pairs={{4,8},{8,4},{12,16},{16,12},{20,24},{24,20},{5,9},{9,5},{13,17},{1... | collective-permute-start | bytes 147464 | tf_op jit(solution)/shard_map/ppermute | solution.py:573
  2.8 1.5 %shard_map.69 = (f32[19,2,16,128]{3,2,1,0:T(8,128)S(1)}, bf16[19,2,16,128]{3,2,1,0:T(8,128)(2,1)S(1)}, s32[2,16,128]{2,1,0:T(8,128)S(1)}, s32[16,128]{1,0:T(8,12...) custom-call(f32[19,2,16,128]{3,2,1,0:T(8,128)} %adj_hbm.3, ...), custom_call_target="tpu_custom_call" | custom-call | flops 1000000 | bytes 557056 | tf_op jit(solution)/shard_map/pallas_call | solution.py:533
  4.3 0.0 collective-permute-done.1.got_inner
  4.3 0.0 collective-permute-done.got_outer
  4.3 0.2 shard_map.70
  4.5 0.7 %collective-permute-start.2 = (f32[24,128]{1,0:T(8,128)S(1)}, f32[24,128]{1,0:T(8,128)S(1)}, u32[]{:S(2)}, u32[]{:S(2)}) collective-permute-start(f32[24,128]{1,0:T(8,128)S(1)} %get-tuple-element.28), channel_id=1, source_target_pairs={{1,2},{2,1},{5,6},{6,5},{9,10},{10,9},{13,14},{14,13},{17,18},{18,... | collective-permute-start | bytes 36872 | tf_op jit(solution)/shard_map/ppermute | solution.py:599
  5.1 5.5 %collective-permute-start.3 = (f32[24,128]{1,0:T(8,128)S(1)}, f32[24,128]{1,0:T(8,128)S(1)}, u32[]{:S(2)}, u32[]{:S(2)}) collective-permute-start(f32[24,128]{1,0:T(8,128)S(1)} %get-tuple-element.29), channel_id=1, source_target_pairs={{0,1},{1,0},{2,3},{3,2},{4,5},{5,4},{6,7},{7,6},{8,9},{9,8},{10,11... | collective-permute-start | bytes 36872 | tf_op jit(solution)/shard_map/ppermute | solution.py:600
  10.6 1.1 %shard_map.71 = (f32[32,128]{1,0:T(8,128)S(1)}, f32[19,2,16,128]{3,2,1,0:T(8,128)S(1)}, f32[19,24,128]{2,1,0:T(8,128)S(1)}, f32[5,24,128]{2,1,0:T(8,128)S(1)}) custom-call(f32[19,2,16,128]{3,2,1,0:T(8,128)S(1)} %get-tuple-element.30.refs_0_, f32[19,2,8,128]{3,2,1,0:T(8,128)S(1)} %get-tuple-element.31.refs_1_, ...), custom_call_target="tpu_custom_call" | custom-call | flops 1000000 | bytes 770048 | tf_op jit(solution)/shard_map/pallas_call | solution.py:533
  11.8 0.0 collective-permute-done.2.got_outer
  11.8 0.5 %collective-permute-done.3.got_inner = f32[24,128]{1,0:T(8,128)S(1)} collective-permute-done((f32[24,128]{1,0:T(8,128)S(1)}, f32[24,128]{1,0:T(8,128)S(1)}, u32[]{:S(2)}, u32[]{:S(2)}) %collective-permute-start.3) | collective-permute-done | bytes 12320 | tf_op jit(solution)/shard_map/ppermute | solution.py:600
  12.3 0.7 %shard_map.72 = (f32[16,128]{1,0:T(8,128)S(1)}, f32[19,2,16,128]{3,2,1,0:T(8,128)S(1)}) custom-call(f32[24,128]{1,0:T(8,128)S(1)} %collective-permute-done.2.got_outer, f32[24,128]{1,0:T(8,128)S(1)} %collective-permute-done.3.got_inner, f32[19,24,128]{2,1,0:T(8,128)S(1)} %get-tuple-element.37.strip, f32[5,24,128]{2,1,0:T(8,128)S(1)} %get-tuple-element.38.field_strip, ...), custom_call_target="tpu_custom_call" | custom-call | bytes 794624 | tf_op jit(solution)/shard_map/pallas_call | solution.py:533
  13.1 0.2 shard_map.73
  13.2 14.7 %all_to_all.5 = f32[32,1,128]{2,1,0:T(1,128)S(1)} all-to-all(f32[32,1,128]{2,1,0:T(1,128)S(1)} %bitcast.5), channel_id=1, replica_groups=mesh['gx'=8,'gy'=4] {'gx','gy'}, dimensions={0} | all-to-all | bytes 32768 | tf_op jit(solution)/shard_map/all_to_all | solution.py:622
  27.9 0.7 %shard_map.74 = (f32[19,2,16,128]{3,2,1,0:T(8,128)}, f32[4,32]{1,0:T(4,128)}) custom-call(f32[32,128]{1,0:T(8,128)S(1)} %bitcast.4, f32[19,2,16,128]{3,2,1,0:T(8,128)S(1)} %get-tuple-element.45.refs_3_.out), custom_call_target="tpu_custom_call" | custom-call | bytes 327680 | tf_op jit(solution)/shard_map/pallas_call | solution.py:533
Async XLA Ops:
  1.6 2.7 %collective-permute-start.1 = (f32[12,8,128]{2,1,0:T(8,128)S(1)}, f32[12,8,128]{2,1,0:T(8,128)S(1)}, u32[]{:S(2)}, u32[]{:S(2)}) collective-permute-start(f32[12,8,128]{2,1,0:T(8,128)S(1)} %get-tuple-element.25), channel_id=1, source_target_pairs={{0,4},{4,0},{8,12},{12,8},{16,20},{20,16},{24,28},{28,24},{1,5},{5... | collective-permute-start | bytes 147464 | tf_op jit(solution)/shard_map/ppermute | solution.py:574
  2.1 2.2 %collective-permute-start = (f32[12,8,128]{2,1,0:T(8,128)S(1)}, f32[12,8,128]{2,1,0:T(8,128)S(1)}, u32[]{:S(2)}, u32[]{:S(2)}) collective-permute-start(f32[12,8,128]{2,1,0:T(8,128)S(1)} %get-tuple-element.24.after), channel_id=1, source_target_pairs={{4,8},{8,4},{12,16},{16,12},{20,24},{24,20},{5,9},{9,5},{13,17},{1... | collective-permute-start | bytes 147464 | tf_op jit(solution)/shard_map/ppermute | solution.py:573
  4.5 7.3 %collective-permute-start.2 = (f32[24,128]{1,0:T(8,128)S(1)}, f32[24,128]{1,0:T(8,128)S(1)}, u32[]{:S(2)}, u32[]{:S(2)}) collective-permute-start(f32[24,128]{1,0:T(8,128)S(1)} %get-tuple-element.28), channel_id=1, source_target_pairs={{1,2},{2,1},{5,6},{6,5},{9,10},{10,9},{13,14},{14,13},{17,18},{18,... | collective-permute-start | bytes 36872 | tf_op jit(solution)/shard_map/ppermute | solution.py:599
  5.1 7.2 %collective-permute-start.3 = (f32[24,128]{1,0:T(8,128)S(1)}, f32[24,128]{1,0:T(8,128)S(1)}, u32[]{:S(2)}, u32[]{:S(2)}) collective-permute-start(f32[24,128]{1,0:T(8,128)S(1)} %get-tuple-element.29), channel_id=1, source_target_pairs={{0,1},{1,0},{2,3},{3,2},{4,5},{5,4},{6,7},{7,6},{8,9},{9,8},{10,11... | collective-permute-start | bytes 36872 | tf_op jit(solution)/shard_map/ppermute | solution.py:600

commit v9 on v6

--- a/solution.py
+++ b/solution.py
@@ -253,7 +253,8 @@
 
 def own_kernel(
     adj_hbm, fwd_hbm, level_hbm, mask_hbm, index_hbm, after,
-    adj, fwd, mask, index, fields, low_own, high_own, fwd_strip, mask_strip, line, level, sems,
+    adj, fwd, mask, index, fields, low_own, high_own, fwd_strip, mask_strip, hot, slots,
+    level, sems,
 ):
     copies = [
         pltpu.make_async_copy(src, dst, sems.at[n])
@@ -280,7 +281,9 @@
     where = index[...].astype(jnp.float32)
     lane = iota(where.shape, 1)
     where = jnp.where(lane < Z_LANES // 2, turned(where, RIGHT, 1), turned(where, LEFT, 1))
-    line[...] = jnp.broadcast_to(edge_line(where), line.shape)
+    owner, slot = split_index(edge_line(where).astype(jnp.int32), slots.shape[0])
+    hot[...] = jnp.where(iota(hot.shape, 0) == owner, 1.0, 0.0)
+    slots[...] = jnp.where(iota(slots.shape, 0) == slot, 1.0, 0.0).astype(jnp.bfloat16)
     copies[4].wait()
     low, high = pack_sides(lambda n, z: adj[n, z] if n < 19 else fields[n - 19, z])
     low_own[...] = low
@@ -505,10 +508,14 @@
             )
 
 
-def sum_kernel(owners, chunk, column, line, grid_inside, after, grid):
+def sum_kernel(owners, column, hot, slots, grid_inside, after, grid):
     values = edge_line(column[...])
-    owner, slot = split_index(line[0:1, :].astype(jnp.int32), chunk)
-    acc = hot_product(*hot_rows(values, owner, slot, owners, chunk))
+    top = values.astype(jnp.bfloat16).astype(jnp.float32)
+    lhs = jnp.concatenate(
+        [(hot[...] * top).astype(jnp.bfloat16), (hot[...] * (values - top)).astype(jnp.bfloat16)],
+        axis=0,
+    )
+    acc = hot_product(lhs, slots[...])
     grid[...] = grid_inside[...] + (acc[:owners] + acc[owners:])
 
 
@@ -571,12 +578,13 @@
     got_outer = lax.ppermute(outer, "gx", swap_pairs(gx_count, 1))
     got_inner = lax.ppermute(inner, "gx", swap_pairs(gx_count, 0))
     flat = ((tile_x, 128), f32)
-    adj, fwd, mask, index, fields, low_own, high_own, fwd_strip, mask_strip, line = call(
+    adj, fwd, mask, index, fields, low_own, high_own, fwd_strip, mask_strip, hot, slots = call(
         own_kernel,
         [
             own, (forward_pop.shape, forward_pop.dtype), (fluid_mask.shape, fluid_mask.dtype),
             (design_index.shape, design_index.dtype), ((FIELDS, depth, tile_x, tile_y), f32),
-            flat, flat, ((19, tile_x, 128), f32), flat, ((8, 128), f32),
+            flat, flat, ((19, tile_x, 128), f32), flat, ((owners, 128), f32),
+            ((chunk, 128), jnp.bfloat16),
         ],
         [adjoint_end, forward_pop, *static, design_index, outer],
         [
@@ -613,9 +621,9 @@
         ],
     )
     (grid,) = call(
-        lambda *refs: sum_kernel(owners, chunk, *refs),
+        lambda *refs: sum_kernel(owners, *refs),
         [((owners, chunk), f32)],
-        [column, line, grid, out],
+        [column, hot, slots, grid, out],
     )
     received = lax.all_to_all(
         grid.reshape(owners, 1, chunk), BOTH, split_axis=0, concat_axis=0, tiled=True

time: 28.9 us -> 28.9 us (level)
  no operation moved by 1% of the time
where the time goes in v9:
time: 28.9 us; the launch traced here: 28.7 us
  blocking collectives  14.7 us (51%)
  starting transfers between devices  7.32 us (25%)
  Pallas kernels  5.47 us (19%)
  between operations  0.7 us (2%)
  waiting for transfers between devices  0.55 us (2%)
    all_to_all x1, blocking collectives, per_device(): lax.all_to_all(grid.reshape(owners, 1, chunk), BOTH, split_axis=0, concat...  14.7 us
    ppermute x1, starting transfers between devices, per_device(): got_inner = lax.ppermute(inner, 'gy', swap_pairs(gy_count, 0))  5.48 us
    pallas_call x7, Pallas kernels, call(): pl.pallas_call(kernel, out_shape=[to(shape, dtype) for shape, dtype in ou...  5.47 us
    ppermute x1, starting transfers between devices, per_device(): got_outer = lax.ppermute(outer, 'gy', swap_pairs(gy_count, 1))  0.66 us
    ppermute x1, starting transfers between devices, per_device(): got_outer = lax.ppermute(outer, 'gx', swap_pairs(gx_count, 1))  0.65 us
  transfers between devices with their start and end apart: 4, of which 1 were waited for; matrix products, arithmetic and copies ran while one was open for 0% of the time, Pallas kernels for 9%

profile of v9, /device:TPU:0, one launch (start us, length us, event | category | flops | bytes accessed | tf_op | source)
XLA Modules:
  0.0 28.7 jit_solution(6402152723322146447)
XLA Ops:
  0.6 1.0 %shard_map.68 = (f32[12,8,128]{2,1,0:T(8,128)S(1)}, f32[12,8,128]{2,1,0:T(8,128)S(1)}) custom-call(f32[19,2,16,128]{3,2,1,0:T(8,128)} %adj_hbm.3, bf16[19,2,16,128]{3,2,1,0:T(8,128)(2,1)} %fwd_hbm.3, s32[2,16,128]{2,1,0:T(8,128)} %level_hbm.3, s32[2,16,128]{2,1,0:T(8,128)} %mask_hbm.3), custom_call_target="tpu_custom_call" | custom-call | bytes 499712 | tf_op jit(solution)/shard_map/pallas_call | solution.py:538
  1.6 0.5 %collective-permute-start.1 = (f32[12,8,128]{2,1,0:T(8,128)S(1)}, f32[12,8,128]{2,1,0:T(8,128)S(1)}, u32[]{:S(2)}, u32[]{:S(2)}) collective-permute-start(f32[12,8,128]{2,1,0:T(8,128)S(1)} %get-tuple-element.26), channel_id=1, source_target_pairs={{0,4},{4,0},{8,12},{12,8},{16,20},{20,16},{24,28},{28,24},{1,5},{5... | collective-permute-start | bytes 147464 | tf_op jit(solution)/shard_map/ppermute | solution.py:579
  2.2 0.7 %collective-permute-start = (f32[12,8,128]{2,1,0:T(8,128)S(1)}, f32[12,8,128]{2,1,0:T(8,128)S(1)}, u32[]{:S(2)}, u32[]{:S(2)}) collective-permute-start(f32[12,8,128]{2,1,0:T(8,128)S(1)} %get-tuple-element.25.after), channel_id=1, source_target_pairs={{4,8},{8,4},{12,16},{16,12},{20,24},{24,20},{5,9},{9,5},{13,17},{1... | collective-permute-start | bytes 147464 | tf_op jit(solution)/shard_map/ppermute | solution.py:578
  2.8 1.5 %shard_map.69 = (f32[19,2,16,128]{3,2,1,0:T(8,128)S(1)}, bf16[19,2,16,128]{3,2,1,0:T(8,128)(2,1)S(1)}, s32[2,16,128]{2,1,0:T(8,128)S(1)}, s32[16,128]{1,0:T(8,12...) custom-call(f32[19,2,16,128]{3,2,1,0:T(8,128)} %adj_hbm.3, ...), custom_call_target="tpu_custom_call" | custom-call | flops 1000000 | bytes 557056 | tf_op jit(solution)/shard_map/pallas_call | solution.py:538
  4.3 0.0 collective-permute-done.1.got_inner
  4.3 0.0 collective-permute-done.got_outer
  4.3 0.2 shard_map.70
  4.5 0.7 %collective-permute-start.2 = (f32[24,128]{1,0:T(8,128)S(1)}, f32[24,128]{1,0:T(8,128)S(1)}, u32[]{:S(2)}, u32[]{:S(2)}) collective-permute-start(f32[24,128]{1,0:T(8,128)S(1)} %get-tuple-element.29), channel_id=1, source_target_pairs={{1,2},{2,1},{5,6},{6,5},{9,10},{10,9},{13,14},{14,13},{17,18},{18,... | collective-permute-start | bytes 36872 | tf_op jit(solution)/shard_map/ppermute | solution.py:605
  5.2 5.5 %collective-permute-start.3 = (f32[24,128]{1,0:T(8,128)S(1)}, f32[24,128]{1,0:T(8,128)S(1)}, u32[]{:S(2)}, u32[]{:S(2)}) collective-permute-start(f32[24,128]{1,0:T(8,128)S(1)} %get-tuple-element.30), channel_id=1, source_target_pairs={{0,1},{1,0},{2,3},{3,2},{4,5},{5,4},{6,7},{7,6},{8,9},{9,8},{10,11... | collective-permute-start | bytes 36872 | tf_op jit(solution)/shard_map/ppermute | solution.py:606
  10.7 1.1 %shard_map.71 = (f32[32,128]{1,0:T(8,128)S(1)}, f32[19,2,16,128]{3,2,1,0:T(8,128)S(1)}, f32[19,24,128]{2,1,0:T(8,128)S(1)}, f32[5,24,128]{2,1,0:T(8,128)S(1)}) custom-call(f32[19,2,16,128]{3,2,1,0:T(8,128)S(1)} %get-tuple-element.31.refs_0_, f32[19,2,8,128]{3,2,1,0:T(8,128)S(1)} %get-tuple-element.32.refs_1_, ...), custom_call_target="tpu_custom_call" | custom-call | flops 1000000 | bytes 770048 | tf_op jit(solution)/shard_map/pallas_call | solution.py:538
  11.8 0.0 collective-permute-done.2.got_outer
  11.8 0.5 %collective-permute-done.3.got_inner = f32[24,128]{1,0:T(8,128)S(1)} collective-permute-done((f32[24,128]{1,0:T(8,128)S(1)}, f32[24,128]{1,0:T(8,128)S(1)}, u32[]{:S(2)}, u32[]{:S(2)}) %collective-permute-start.3) | collective-permute-done | bytes 12320 | tf_op jit(solution)/shard_map/ppermute | solution.py:606
  12.3 0.7 %shard_map.72 = (f32[16,128]{1,0:T(8,128)S(1)}, f32[19,2,16,128]{3,2,1,0:T(8,128)S(1)}) custom-call(f32[24,128]{1,0:T(8,128)S(1)} %collective-permute-done.2.got_outer, f32[24,128]{1,0:T(8,128)S(1)} %collective-permute-done.3.got_inner, f32[19,24,128]{2,1,0:T(8,128)S(1)} %get-tuple-element.38.strip, f32[5,24,128]{2,1,0:T(8,128)S(1)} %get-tuple-element.39.field_strip, ...), custom_call_target="tpu_custom_call" | custom-call | bytes 794624 | tf_op jit(solution)/shard_map/pallas_call | solution.py:538
  13.1 0.2 shard_map.73
  13.3 14.7 %all_to_all.5 = f32[32,1,128]{2,1,0:T(1,128)S(1)} all-to-all(f32[32,1,128]{2,1,0:T(1,128)S(1)} %bitcast.4), channel_id=1, replica_groups=mesh['gx'=8,'gy'=4] {'gx','gy'}, dimensions={0} | all-to-all | bytes 32768 | tf_op jit(solution)/shard_map/all_to_all | solution.py:628
  28.0 0.7 %shard_map.74 = (f32[19,2,16,128]{3,2,1,0:T(8,128)}, f32[4,32]{1,0:T(4,128)}) custom-call(f32[32,128]{1,0:T(8,128)S(1)} %bitcast.5, f32[19,2,16,128]{3,2,1,0:T(8,128)S(1)} %get-tuple-element.47.refs_4_.out), custom_call_target="tpu_custom_call" | custom-call | bytes 327680 | tf_op jit(solution)/shard_map/pallas_call | solution.py:538
Async XLA Ops:
  1.6 2.7 %collective-permute-start.1 = (f32[12,8,128]{2,1,0:T(8,128)S(1)}, f32[12,8,128]{2,1,0:T(8,128)S(1)}, u32[]{:S(2)}, u32[]{:S(2)}) collective-permute-start(f32[12,8,128]{2,1,0:T(8,128)S(1)} %get-tuple-element.26), channel_id=1, source_target_pairs={{0,4},{4,0},{8,12},{12,8},{16,20},{20,16},{24,28},{28,24},{1,5},{5... | collective-permute-start | bytes 147464 | tf_op jit(solution)/shard_map/ppermute | solution.py:579
  2.2 2.2 %collective-permute-start = (f32[12,8,128]{2,1,0:T(8,128)S(1)}, f32[12,8,128]{2,1,0:T(8,128)S(1)}, u32[]{:S(2)}, u32[]{:S(2)}) collective-permute-start(f32[12,8,128]{2,1,0:T(8,128)S(1)} %get-tuple-element.25.after), channel_id=1, source_target_pairs={{4,8},{8,4},{12,16},{16,12},{20,24},{24,20},{5,9},{9,5},{13,17},{1... | collective-permute-start | bytes 147464 | tf_op jit(solution)/shard_map/ppermute | solution.py:578
  4.5 7.3 %collective-permute-start.2 = (f32[24,128]{1,0:T(8,128)S(1)}, f32[24,128]{1,0:T(8,128)S(1)}, u32[]{:S(2)}, u32[]{:S(2)}) collective-permute-start(f32[24,128]{1,0:T(8,128)S(1)} %get-tuple-element.29), channel_id=1, source_target_pairs={{1,2},{2,1},{5,6},{6,5},{9,10},{10,9},{13,14},{14,13},{17,18},{18,... | collective-permute-start | bytes 36872 | tf_op jit(solution)/shard_map/ppermute | solution.py:605
  5.2 7.2 %collective-permute-start.3 = (f32[24,128]{1,0:T(8,128)S(1)}, f32[24,128]{1,0:T(8,128)S(1)}, u32[]{:S(2)}, u32[]{:S(2)}) collective-permute-start(f32[24,128]{1,0:T(8,128)S(1)} %get-tuple-element.30), channel_id=1, source_target_pairs={{0,1},{1,0},{2,3},{3,2},{4,5},{5,4},{6,7},{7,6},{8,9},{9,8},{10,11... | collective-permute-start | bytes 36872 | tf_op jit(solution)/shard_map/ppermute | solution.py:606

commit v10 on v6

--- a/solution.py
+++ b/solution.py
@@ -578,7 +578,7 @@
             (design_index.shape, design_index.dtype), ((FIELDS, depth, tile_x, tile_y), f32),
             flat, flat, ((19, tile_x, 128), f32), flat, ((8, 128), f32),
         ],
-        [adjoint_end, forward_pop, *static, design_index, outer],
+        [adjoint_end, forward_pop, *static, design_index, inner],
         [
             pltpu.VMEM(porosity_level.shape, porosity_level.dtype),
             pltpu.SemaphoreType.DMA((5,)),

time: 28.9 us -> 29.1 us (level)
  starting transfers between devices: 7.32 us -> 10.2 us
  blocking collectives: 14.7 us -> 12.1 us
    ppermute x1, starting transfers between devices: 0.52 us -> 4.36 us  [per_device(): got_inner = lax.ppermute(inner, 'gx', swap_pairs(gx_count, 0))]
    all_to_all x1, blocking collectives: 14.7 us -> 12.1 us  [per_device(): lax.all_to_all(grid.reshape(owners, 1, chunk), BOTH, split_axis=0, concat...]
    ppermute x1, starting transfers between devices: 5.48 us -> 4.46 us  [per_device(): got_inner = lax.ppermute(inner, 'gy', swap_pairs(gy_count, 0))]
where the time goes in v10:
time: 29.1 us; the launch traced here: 28.9 us
  blocking collectives  12.1 us (42%)
  starting transfers between devices  10.2 us (35%)
  Pallas kernels  5.45 us (19%)
  between operations  0.7 us (2%)
  waiting for transfers between devices  0.54 us (2%)
    all_to_all x1, blocking collectives, per_device(): lax.all_to_all(grid.reshape(owners, 1, chunk), BOTH, split_axis=0, concat...  12.1 us
    pallas_call x7, Pallas kernels, call(): pl.pallas_call(kernel, out_shape=[to(shape, dtype) for shape, dtype in ou...  5.45 us
    ppermute x1, starting transfers between devices, per_device(): got_inner = lax.ppermute(inner, 'gy', swap_pairs(gy_count, 0))  4.46 us
    ppermute x1, starting transfers between devices, per_device(): got_inner = lax.ppermute(inner, 'gx', swap_pairs(gx_count, 0))  4.36 us
    ppermute x1, starting transfers between devices, per_device(): got_outer = lax.ppermute(outer, 'gx', swap_pairs(gx_count, 1))  0.66 us
    ppermute x1, starting transfers between devices, per_device(): got_outer = lax.ppermute(outer, 'gy', swap_pairs(gy_count, 1))  0.66 us
  transfers between devices with their start and end apart: 4, of which 1 were waited for; matrix products, arithmetic and copies ran while one was open for 0% of the time, Pallas kernels for 9%

profile of v10, /device:TPU:0, one launch (start us, length us, event | category | flops | bytes accessed | tf_op | source)
XLA Modules:
  0.0 28.9 jit_solution(14975019282787128937)
XLA Ops:
  0.6 1.0 %shard_map.68 = (f32[12,8,128]{2,1,0:T(8,128)S(1)}, f32[12,8,128]{2,1,0:T(8,128)S(1)}) custom-call(f32[19,2,16,128]{3,2,1,0:T(8,128)} %adj_hbm.3, bf16[19,2,16,128]{3,2,1,0:T(8,128)(2,1)} %fwd_hbm.3, s32[2,16,128]{2,1,0:T(8,128)} %level_hbm.3, s32[2,16,128]{2,1,0:T(8,128)} %mask_hbm.3), custom_call_target="tpu_custom_call" | custom-call | bytes 499712 | tf_op jit(solution)/shard_map/pallas_call | solution.py:531
  1.6 0.7 %collective-permute-start = (f32[12,8,128]{2,1,0:T(8,128)S(1)}, f32[12,8,128]{2,1,0:T(8,128)S(1)}, u32[]{:S(2)}, u32[]{:S(2)}) collective-permute-start(f32[12,8,128]{2,1,0:T(8,128)S(1)} %get-tuple-element.24), channel_id=1, source_target_pairs={{4,8},{8,4},{12,16},{16,12},{20,24},{24,20},{5,9},{9,5},{13,17},{1... | collective-permute-start | bytes 147464 | tf_op jit(solution)/shard_map/ppermute | solution.py:571
  2.3 4.4 %collective-permute-start.1 = (f32[12,8,128]{2,1,0:T(8,128)S(1)}, f32[12,8,128]{2,1,0:T(8,128)S(1)}, u32[]{:S(2)}, u32[]{:S(2)}) collective-permute-start(f32[12,8,128]{2,1,0:T(8,128)S(1)} %get-tuple-element.25.after), channel_id=1, source_target_pairs={{0,4},{4,0},{8,12},{12,8},{16,20},{20,16},{24,28},{28,24},{1,5},{5... | collective-permute-start | bytes 147464 | tf_op jit(solution)/shard_map/ppermute | solution.py:572
  6.7 1.5 %shard_map.69 = (f32[19,2,16,128]{3,2,1,0:T(8,128)S(1)}, bf16[19,2,16,128]{3,2,1,0:T(8,128)(2,1)S(1)}, s32[2,16,128]{2,1,0:T(8,128)S(1)}, s32[16,128]{1,0:T(8,12...) custom-call(f32[19,2,16,128]{3,2,1,0:T(8,128)} %adj_hbm.3, ...), custom_call_target="tpu_custom_call" | custom-call | flops 1000000 | bytes 557056 | tf_op jit(solution)/shard_map/pallas_call | solution.py:531
  8.2 0.0 collective-permute-done.got_outer
  8.2 0.0 collective-permute-done.1.got_inner
  8.2 0.2 shard_map.70
  8.4 0.7 %collective-permute-start.2 = (f32[24,128]{1,0:T(8,128)S(1)}, f32[24,128]{1,0:T(8,128)S(1)}, u32[]{:S(2)}, u32[]{:S(2)}) collective-permute-start(f32[24,128]{1,0:T(8,128)S(1)} %get-tuple-element.28), channel_id=1, source_target_pairs={{1,2},{2,1},{5,6},{6,5},{9,10},{10,9},{13,14},{14,13},{17,18},{18,... | collective-permute-start | bytes 36872 | tf_op jit(solution)/shard_map/ppermute | solution.py:597
  9.0 4.5 %collective-permute-start.3 = (f32[24,128]{1,0:T(8,128)S(1)}, f32[24,128]{1,0:T(8,128)S(1)}, u32[]{:S(2)}, u32[]{:S(2)}) collective-permute-start(f32[24,128]{1,0:T(8,128)S(1)} %get-tuple-element.29), channel_id=1, source_target_pairs={{0,1},{1,0},{2,3},{3,2},{4,5},{5,4},{6,7},{7,6},{8,9},{9,8},{10,11... | collective-permute-start | bytes 36872 | tf_op jit(solution)/shard_map/ppermute | solution.py:598
  13.5 1.1 %shard_map.71 = (f32[32,128]{1,0:T(8,128)S(1)}, f32[19,2,16,128]{3,2,1,0:T(8,128)S(1)}, f32[19,24,128]{2,1,0:T(8,128)S(1)}, f32[5,24,128]{2,1,0:T(8,128)S(1)}) custom-call(f32[19,2,16,128]{3,2,1,0:T(8,128)S(1)} %get-tuple-element.30.refs_0_, f32[19,2,8,128]{3,2,1,0:T(8,128)S(1)} %get-tuple-element.31.refs_1_, ...), custom_call_target="tpu_custom_call" | custom-call | flops 1000000 | bytes 770048 | tf_op jit(solution)/shard_map/pallas_call | solution.py:531
  14.6 0.0 collective-permute-done.2.got_outer
  14.6 0.5 %collective-permute-done.3.got_inner = f32[24,128]{1,0:T(8,128)S(1)} collective-permute-done((f32[24,128]{1,0:T(8,128)S(1)}, f32[24,128]{1,0:T(8,128)S(1)}, u32[]{:S(2)}, u32[]{:S(2)}) %collective-permute-start.3) | collective-permute-done | bytes 12320 | tf_op jit(solution)/shard_map/ppermute | solution.py:598
  15.2 0.7 %shard_map.72 = (f32[16,128]{1,0:T(8,128)S(1)}, f32[19,2,16,128]{3,2,1,0:T(8,128)S(1)}) custom-call(f32[24,128]{1,0:T(8,128)S(1)} %collective-permute-done.2.got_outer, f32[24,128]{1,0:T(8,128)S(1)} %collective-permute-done.3.got_inner, f32[19,24,128]{2,1,0:T(8,128)S(1)} %get-tuple-element.37.strip, f32[5,24,128]{2,1,0:T(8,128)S(1)} %get-tuple-element.38.field_strip, ...), custom_call_target="tpu_custom_call" | custom-call | bytes 794624 | tf_op jit(solution)/shard_map/pallas_call | solution.py:531
  15.9 0.2 shard_map.73
  16.1 12.1 %all_to_all.5 = f32[32,1,128]{2,1,0:T(1,128)S(1)} all-to-all(f32[32,1,128]{2,1,0:T(1,128)S(1)} %bitcast.5), channel_id=1, replica_groups=mesh['gx'=8,'gy'=4] {'gx','gy'}, dimensions={0} | all-to-all | bytes 32768 | tf_op jit(solution)/shard_map/all_to_all | solution.py:620
  28.2 0.7 %shard_map.74 = (f32[19,2,16,128]{3,2,1,0:T(8,128)}, f32[4,32]{1,0:T(4,128)}) custom-call(f32[32,128]{1,0:T(8,128)S(1)} %bitcast.4, f32[19,2,16,128]{3,2,1,0:T(8,128)S(1)} %get-tuple-element.45.refs_3_.out), custom_call_target="tpu_custom_call" | custom-call | bytes 327680 | tf_op jit(solution)/shard_map/pallas_call | solution.py:531
Async XLA Ops:
  1.6 6.5 %collective-permute-start = (f32[12,8,128]{2,1,0:T(8,128)S(1)}, f32[12,8,128]{2,1,0:T(8,128)S(1)}, u32[]{:S(2)}, u32[]{:S(2)}) collective-permute-start(f32[12,8,128]{2,1,0:T(8,128)S(1)} %get-tuple-element.24), channel_id=1, source_target_pairs={{4,8},{8,4},{12,16},{16,12},{20,24},{24,20},{5,9},{9,5},{13,17},{1... | collective-permute-start | bytes 147464 | tf_op jit(solution)/shard_map/ppermute | solution.py:571
  2.3 5.9 %collective-permute-start.1 = (f32[12,8,128]{2,1,0:T(8,128)S(1)}, f32[12,8,128]{2,1,0:T(8,128)S(1)}, u32[]{:S(2)}, u32[]{:S(2)}) collective-permute-start(f32[12,8,128]{2,1,0:T(8,128)S(1)} %get-tuple-element.25.after), channel_id=1, source_target_pairs={{0,4},{4,0},{8,12},{12,8},{16,20},{20,16},{24,28},{28,24},{1,5},{5... | collective-permute-start | bytes 147464 | tf_op jit(solution)/shard_map/ppermute | solution.py:572
  8.4 6.3 %collective-permute-start.2 = (f32[24,128]{1,0:T(8,128)S(1)}, f32[24,128]{1,0:T(8,128)S(1)}, u32[]{:S(2)}, u32[]{:S(2)}) collective-permute-start(f32[24,128]{1,0:T(8,128)S(1)} %get-tuple-element.28), channel_id=1, source_target_pairs={{1,2},{2,1},{5,6},{6,5},{9,10},{10,9},{13,14},{14,13},{17,18},{18,... | collective-permute-start | bytes 36872 | tf_op jit(solution)/shard_map/ppermute | solution.py:597
  9.0 6.1 %collective-permute-start.3 = (f32[24,128]{1,0:T(8,128)S(1)}, f32[24,128]{1,0:T(8,128)S(1)}, u32[]{:S(2)}, u32[]{:S(2)}) collective-permute-start(f32[24,128]{1,0:T(8,128)S(1)} %get-tuple-element.29), channel_id=1, source_target_pairs={{0,1},{1,0},{2,3},{3,2},{4,5},{5,4},{6,7},{7,6},{8,9},{9,8},{10,11... | collective-permute-start | bytes 36872 | tf_op jit(solution)/shard_map/ppermute | solution.py:598
